TPU v7x, 128 devices: a whole 4x4x4 slice. The times are simulated.
128 devices in a mesh: dp: 8 (over y, core), expert: 16 (over z, x).
Axes of the slice: x: 4, y: 4, z: 4, core: 2. Of those that a mesh axis runs over, the one named last changes fastest.
Arguments:
- tokens: bfloat16 [24576, 4096], P(('dp', 'expert')), may hold values from -6 to 6
- cotangent: bfloat16 [24576, 4096], P(('dp', 'expert')), may hold values from -6 to 6
- expert_ids: int32 [24576, 6], P(('dp', 'expert')), may hold values from 0 to 63, as said below
- route_weights: float32 [24576, 6], P(('dp', 'expert')), may hold values from 0.05 to 1
- expert_weights: bfloat16 [16, 704, 3, 4096], P('expert'), may hold values from -0.09375 to 0.09375
Outputs:
- input_grad: bfloat16 [24576, 4096], P(('dp', 'expert'))
- route_grad: bfloat16 [24576, 6], P(('dp', 'expert'))
- weight_grad: float32 [16, 704, 3, 4096], P('expert', 'dp')
Inputs may be any that keep to these rules, and one draw needn't show every extreme that they name: `expert_ids`: each row names 6 different experts. Only experts below 16 are in this window; in the rows of one device (aligned blocks of 192 rows) each of them is named at most 36 times.
All inputs are finite; a program needn't handle non-finite values.
Results may differ from a plain program's by a relative error of at most 0.015.
Values may be sent and summed in bfloat16 or wider, within the bound.
No kernel may reach another device: no remote copies, remote signals or barrier semaphores. Data moves between devices by JAX's collectives and lax.ppermute only.
A program may use at most 128 MiB of HBM per device.

v0:
```python
import functools

import jax
import jax.numpy as jnp
from jax import lax
from jax.experimental import pallas as pl
from jax.experimental.pallas import tpu as pltpu
from jax.sharding import PartitionSpec as P

CAP = 36
SIDE = 4
BLOCK = SIDE * CAP
ROWS = SIDE * BLOCK
EXTRA = 128
HOPS = (0, 1, 3, 2)
PLACE = (0, 1, 3, 2)
BIG = 56 << 20


def hop(dz, dx):
    return [
        (z * SIDE + x, (z + dz) % SIDE * SIDE + (x + dx) % SIDE)
        for z in range(SIDE)
        for x in range(SIDE)
    ]


def move(value, axis, step):
    if step % SIDE == 0:
        return value
    return lax.ppermute(value, "expert", hop(step, 0) if axis == "z" else hop(0, step))


def spread(blocks, axis, sign):
    return [move(blocks[p], axis, sign * HOPS[p]) for p in range(SIDE)]


def product(left, right, dims=((1,), (0,))):
    return lax.dot_general(left, right, (dims, ((), ())), preferred_element_type=jnp.float32)


def swap_matrix():
    row = jnp.arange(ROWS, dtype=jnp.int32)[:, None]
    col = jnp.arange(ROWS, dtype=jnp.int32)[None, :]
    block, slot = row // CAP, row % CAP
    return (col == ((block % SIDE) * SIDE + block // SIDE) * CAP + slot).astype(jnp.bfloat16)


def params(*axes):
    return pltpu.CompilerParams(dimension_semantics=axes, vmem_limit_bytes=BIG)


def cost(flops, moved):
    return pl.CostEstimate(flops=int(flops), bytes_accessed=int(moved), transcendentals=0)


def swap_kernel(matrix_ref, *refs):
    rows = jnp.concatenate([ref[...] for ref in refs[:SIDE]], axis=0)
    out = product(matrix_ref[...], rows).astype(jnp.bfloat16)
    for p in range(SIDE):
        refs[SIDE + p][...] = out[p * BLOCK : (p + 1) * BLOCK]


def swap_blocks(matrix, blocks):
    width = blocks[0].shape[1]
    tile = 1024 if width % 1024 == 0 else 1408 if width % 1408 == 0 else width
    spec = pl.BlockSpec((BLOCK, tile), lambda i: (0, i))
    return pl.pallas_call(
        swap_kernel,
        grid=(width // tile,),
        in_specs=[pl.BlockSpec((ROWS, ROWS), lambda i: (0, 0))] + [spec] * SIDE,
        out_specs=[spec] * SIDE,
        out_shape=[jax.ShapeDtypeStruct((BLOCK, width), jnp.bfloat16)] * SIDE,
        compiler_params=params("arbitrary"),
        cost_estimate=cost(2 * ROWS * ROWS * width, 4 * ROWS * width),
        name="swap_blocks",
    )(matrix, *blocks)


def forward_kernel(steps, matrix_ref, weight_ref, *refs):
    toks, cots, scales = refs[0:4], refs[4:8], refs[8:12]
    gate_out, up_out, hidden_out, gate_turned, up_turned, route_out = refs[12:18]
    gate_acc, up_acc, back_acc = refs[18:21]
    step = pl.program_id(0)

    @pl.when(step == 0)
    def _():
        gate_acc[...] = jnp.zeros_like(gate_acc)
        up_acc[...] = jnp.zeros_like(up_acc)
        back_acc[...] = jnp.zeros_like(back_acc)

    tok = jnp.concatenate([ref[...] for ref in toks], axis=0)
    cot = jnp.concatenate([ref[...] for ref in cots], axis=0)
    last = ((1,), (1,))
    gate_acc[...] += product(tok, weight_ref[0], last)
    up_acc[...] += product(tok, weight_ref[1], last)
    back_acc[...] += product(cot, weight_ref[2], last)

    @pl.when(step == steps - 1)
    def _():
        matrix = matrix_ref[...]
        gate_pre, up_pre, back = gate_acc[...], up_acc[...], back_acc[...]
        scale = jnp.concatenate([ref[:, :1] for ref in scales], axis=0).astype(jnp.float32)
        logistic = 1.0 / (1.0 + jnp.exp(-gate_pre))
        gated = gate_pre * logistic
        hidden = (gated * up_pre).astype(jnp.bfloat16)
        hidden_turned = product(matrix, hidden)
        hidden_out[...] = hidden_turned.astype(jnp.bfloat16)
        route = jnp.sum(hidden_turned * back, axis=1, keepdims=True).astype(jnp.bfloat16)
        route = jnp.broadcast_to(route, (ROWS, EXTRA))
        route_out[...] = product(matrix, route).astype(jnp.bfloat16)
        grad = scale * back
        high = grad.astype(jnp.bfloat16)
        low = (grad - high.astype(jnp.float32)).astype(jnp.bfloat16)
        grad = product(matrix, high) + product(matrix, low)
        gate_delta = (grad * up_pre * logistic * (1.0 + gate_pre * (1.0 - logistic))).astype(
            jnp.bfloat16
        )
        up_delta = (grad * gated).astype(jnp.bfloat16)
        gate_out[...] = gate_delta
        up_out[...] = up_delta
        gate_turned[...] = product(matrix, gate_delta).astype(jnp.bfloat16)
        up_turned[...] = product(matrix, up_delta).astype(jnp.bfloat16)


def forward(matrix, weights, toks, cots):
    units, width = weights.shape[1:]
    tile = 512
    steps = width // tile
    rows = pl.BlockSpec((BLOCK, tile), lambda i: (0, i))
    extra = pl.BlockSpec((BLOCK, EXTRA), lambda i: (0, width // EXTRA))
    whole = pl.BlockSpec((ROWS, units), lambda i: (0, 0))
    small = jax.ShapeDtypeStruct((ROWS, units), jnp.bfloat16)
    return pl.pallas_call(
        functools.partial(forward_kernel, steps),
        grid=(steps,),
        in_specs=[
            pl.BlockSpec((ROWS, ROWS), lambda i: (0, 0)),
            pl.BlockSpec((3, units, tile), lambda i: (0, 0, i)),
        ]
        + [rows] * 8
        + [extra] * 4,
        out_specs=[whole] * 5 + [pl.BlockSpec((ROWS, EXTRA), lambda i: (0, 0))],
        out_shape=[small] * 5 + [jax.ShapeDtypeStruct((ROWS, EXTRA), jnp.bfloat16)],
        scratch_shapes=[pltpu.VMEM((ROWS, units), jnp.float32)] * 3,
        compiler_params=params("arbitrary"),
        cost_estimate=cost(6 * ROWS * units * width, 6 * units * width + 4 * ROWS * width),
        name="forward",
    )(matrix, weights, *toks, *cots, *cots)


def terms_kernel(gate_ref, up_ref, hidden_ref, *refs):
    toks, cots, scales, out_ref = refs[0:4], refs[4:8], refs[8:12], refs[12]
    tok = jnp.concatenate([ref[...] for ref in toks], axis=0)
    scaled = jnp.concatenate(
        [
            (ref[...].astype(jnp.float32) * scale[:, :1].astype(jnp.float32)).astype(jnp.bfloat16)
            for ref, scale in zip(cots, scales)
        ],
        axis=0,
    )
    share = out_ref.shape[2]
    for kind, (left, right) in enumerate(
        ((gate_ref, tok), (up_ref, tok), (hidden_ref, scaled))
    ):
        term = product(left[...], right, ((0,), (0,))).astype(jnp.bfloat16)
        for owner in range(out_ref.shape[0]):
            out_ref[owner, kind] = term[owner * share : (owner + 1) * share]


def terms(gate_delta, up_delta, hidden, toks, cots, owners):
    units = gate_delta.shape[1]
    width = toks[0].shape[1]
    tile = 512
    rows = pl.BlockSpec((BLOCK, tile), lambda i: (0, i))
    extra = pl.BlockSpec((BLOCK, EXTRA), lambda i: (0, width // EXTRA))
    whole = pl.BlockSpec((ROWS, units), lambda i: (0, 0))
    share = units // owners
    return pl.pallas_call(
        terms_kernel,
        grid=(width // tile,),
        in_specs=[whole] * 3 + [rows] * 8 + [extra] * 4,
        out_specs=pl.BlockSpec((owners, 3, share, tile), lambda i: (0, 0, 0, i)),
        out_shape=jax.ShapeDtypeStruct((owners, 3, share, width), jnp.bfloat16),
        compiler_params=params("arbitrary"),
        cost_estimate=cost(6 * ROWS * units * width, 6 * units * width + 4 * ROWS * width),
        name="terms",
    )(gate_delta, up_delta, hidden, *toks, *cots, *cots)


def inputs_kernel(tiles, gate_ref, up_ref, weight_ref, *refs):
    def columns():
        return (product(gate_ref[...], weight_ref[0]) + product(up_ref[...], weight_ref[1])).astype(
            jnp.bfloat16
        )

    def put(value, width):
        for p in range(SIDE):
            refs[-SIDE + p][:, :width] = value[p * BLOCK : (p + 1) * BLOCK]

    put(columns(), weight_ref.shape[2])


def inputs(gate_delta, up_delta, weights, first, count):
    units = weights.shape[1]
    tile = 512
    whole = pl.BlockSpec((ROWS, units), lambda i: (0, 0))
    return pl.pallas_call(
        functools.partial(inputs_kernel, count // tile),
        grid=(count // tile,),
        in_specs=[
            whole,
            whole,
            pl.BlockSpec((2, units, tile), lambda i: (0, 0, first // tile + i)),
        ],
        out_specs=[pl.BlockSpec((BLOCK, tile), lambda i: (0, i))] * SIDE,
        out_shape=[jax.ShapeDtypeStruct((BLOCK, count), jnp.bfloat16)] * SIDE,
        compiler_params=params("arbitrary"),
        cost_estimate=cost(4 * ROWS * units * count, 4 * units * count + 2 * ROWS * count),
        name="inputs",
    )(gate_delta, up_delta, weights)


def shards(tokens, cotangent, expert_ids, route_weights, expert_weights):
    me = lax.axis_index("expert")
    z, x = me // SIDE, me % SIDE
    tok_rows, width = tokens.shape
    half = width // 2
    experts = SIDE * SIDE
    owners = lax.axis_size("dp")

    ids = expert_ids.T
    column = lax.broadcasted_iota(jnp.int32, (experts, 1, 1), 0)
    named = ids[None] == column
    routed = jnp.any(named, axis=1)
    earlier = (
        lax.broadcasted_iota(jnp.int32, (tok_rows, tok_rows), 0)
        < lax.broadcasted_iota(jnp.int32, (tok_rows, tok_rows), 1)
    ).astype(jnp.bfloat16)
    slots = jnp.dot(routed.astype(jnp.bfloat16), earlier, preferred_element_type=jnp.float32)
    slots = slots.astype(jnp.int32)
    expert = lax.broadcasted_iota(jnp.int32, (experts, 1), 0)
    far_z, far_x = (expert // SIDE - z) % SIDE, (expert % SIDE - x) % SIDE
    near_z = jnp.where(far_z >= 2, 5 - far_z, far_z)
    near_x = jnp.where(far_x >= 2, 5 - far_x, far_x)
    live = jnp.any(named, axis=0)

    def codes(blocks):
        code = jnp.sum(jnp.where(named, (slots + blocks * CAP)[:, None, :], 0), axis=0)
        return jnp.where(live, code, -1)

    def one_hot(code, first, count):
        row = lax.broadcasted_iota(jnp.int32, (count, tok_rows), 0) + first
        hot = row == code[0][None, :]
        for k in range(1, code.shape[0]):
            hot = hot | (row == code[k][None, :])
        return hot.astype(jnp.bfloat16)

    z_first = codes(near_z * SIDE + near_x)
    x_first = codes(near_x * SIDE + near_z)

    def row_scales(code, first):
        row = lax.broadcasted_iota(jnp.int32, (BLOCK, 1, 1), 0) + first
        scale = jnp.where(row == code[None], route_weights.T[None], 0.0)
        return jnp.sum(scale, axis=(1, 2))[:, None].astype(jnp.bfloat16)

    def pick(left, right):
        return jnp.dot(left, right, preferred_element_type=jnp.float32).astype(jnp.bfloat16)

    tok_blocks, cot_blocks = [], []
    for p in range(SIDE):
        tok_blocks.append(pick(one_hot(z_first, p * BLOCK, BLOCK), tokens))
        picked = pick(one_hot(x_first, p * BLOCK, BLOCK), cotangent)
        scale = jnp.broadcast_to(row_scales(x_first, p * BLOCK), (BLOCK, EXTRA))
        cot_blocks.append(jnp.concatenate([picked, scale], axis=1))

    matrix = swap_matrix()
    toks = spread(swap_blocks(matrix, spread(tok_blocks, "z", 1)), "x", 1)
    cots = spread(swap_blocks(matrix, spread(cot_blocks, "x", 1)), "z", 1)

    weights = expert_weights[0].transpose(1, 0, 2)
    gate_delta, up_delta, hidden, gate_turned, up_turned, route = forward(
        matrix, weights, toks, cots
    )
    partial_sums = terms(gate_delta, up_delta, hidden, toks, cots, owners)
    summed = lax.psum_scatter(partial_sums, "dp", scatter_dimension=0, tiled=True)
    weight_grad = summed.astype(jnp.float32).transpose(0, 2, 1, 3)

    left = inputs(gate_delta, up_delta, weights, 0, half)
    right = inputs(gate_turned, up_turned, weights, half, half)
    left = [
        jnp.concatenate([left[p], route[p * BLOCK : (p + 1) * BLOCK]], axis=1)
        for p in range(SIDE)
    ]
    left = spread(swap_blocks(matrix, spread(left, "x", -1)), "z", -1)
    right = spread(swap_blocks(matrix, spread(right, "z", -1)), "x", -1)

    def combine(blocks, code):
        return jnp.einsum(
            "ct,cd->td",
            one_hot(code, 0, ROWS),
            jnp.concatenate(blocks, axis=0),
            preferred_element_type=jnp.float32,
        ).astype(jnp.bfloat16)

    input_grad = jnp.concatenate(
        [combine([b[:, :half] for b in left], z_first), combine(right, x_first)], axis=1
    )
    route_mine = jnp.concatenate([b[:, half] for b in left], axis=0).astype(jnp.float32)
    row = lax.broadcasted_iota(jnp.int32, (ROWS, 1, 1), 0)
    route_grad = jnp.sum(jnp.where(row == z_first[None], route_mine[:, None, None], 0.0), axis=0)
    return input_grad, route_grad.astype(jnp.bfloat16).T, weight_grad


def solution(mesh):
    rows = P(("dp", "expert"), None)
    return jax.shard_map(
        shards,
        mesh=mesh,
        in_specs=(rows, rows, rows, rows, P("expert", None, None, None)),
        out_specs=(rows, rows, P("expert", "dp", None, None)),
        check_vma=False,
    )
```

profile of v0, /device:TPU:1, one launch (start us, length us, event | category | flops | bytes accessed | tf_op | source)
XLA Modules:
  0.0 295.4 jit_solution(10825887785887144024)
XLA Ops:
  7.3 0.8 fusion.117
  8.2 0.8 select_reduce_fusion.5
  9.1 0.6 convolution_convert_fusion.4
  9.6 4.5 %collective-permute-start.2 = (bf16[144,4096]{1,0:T(8,128)(2,1)S(1)}, bf16[144,4096]{1,0:T(8,128)(2,1)S(1)}, u32[]{:S(2)}, u32[]{:S(2)}) collective-permute-start(bf16[144,4096]{1,0:T(8,128)(2,1)S(1)} %convolution_convert_fusion.4), channel_id=1, source_target_pairs={{0,8},{1,9},{2,10},{3,11},{4,12},{5,13},{6,14},{7,15},{8,0},{9,1},... | collective-permute-start | bytes 3538952 | tf_op jit(solution)/shard_map/ppermute | solution.py:31
  15.2 0.6 convolution_convert_fusion.6
  15.8 1.1 collective-permute-start
  16.9 0.6 select_reduce_fusion.1
  17.5 0.6 convolution_convert_fusion
  18.2 2.8 collective-permute-start.8
  21.0 0.6 convolution_convert_fusion.1
  21.8 0.9 collective-permute-start.7
  22.7 1.5 convolution_convert_fusion.7.refs_0_
  24.3 0.6 convolution_convert_fusion.2
  25.0 14.9 %collective-permute-done.2.refs_3_ = bf16[144,4096]{1,0:T(8,128)(2,1)S(1)} collective-permute-done((bf16[144,4096]{1,0:T(8,128)(2,1)S(1)}, bf16[144,4096]{1,0:T(8,128)(2,1)S(1)}, u32[]{:S(2)}, u32[]{:S(2)}) %collective-permute-start.2) | collective-permute-done | bytes 1179680 | tf_op jit(solution)/shard_map/ppermute | solution.py:31
  39.9 1.2 collective-permute-start.6
  41.1 1.1 fusion.14.matrix_ref
  42.2 23.5 %collective-permute-done.1.refs_2_ = bf16[144,4096]{1,0:T(8,128)(2,1)S(1)} collective-permute-done((bf16[144,4096]{1,0:T(8,128)(2,1)S(1)}, bf16[144,4096]{1,0:T(8,128)(2,1)S(1)}, u32[]{:S(2)}, u32[]{:S(2)}) %collective-permute-start.1) | collective-permute-done | bytes 1179680 | tf_op jit(solution)/shard_map/ppermute | solution.py:31
  65.7 1.0 copy-done.13
  66.7 7.6 %swap_blocks.4 = (bf16[144,4096]{1,0:T(8,128)(2,1)}, bf16[144,4096]{1,0:T(8,128)(2,1)}, bf16[144,4096]{1,0:T(8,128)(2,1)}, bf16[144,4096]{1,0:T(8,128)(2,1)}) custom-call(bf16[576,576]{1,0:T(8,128)(2,1)} %fusion.14.matrix_ref, bf16[144,4096]{1,0:T(8,128)(2,1)} %convolution_convert_fusion.7.refs_0_, bf16[144,4096]{1,0:T(8,128)(2,1)} %collective-permute-done.refs_1_, ...), custom_call_target="tpu_custom_call" | custom-call | flops 2717908992 | bytes 9437184 | tf_op jit(solution)/shard_map/swap_blocks/pallas_call | solution.py:68
  74.3 1.2 collective-permute-start.3
  76.1 1.1 pad_maximum_fusion.1.refs_0_
  77.2 1.0 copy-done.8
  78.2 7.9 %swap_blocks.5 = (bf16[144,4224]{1,0:T(8,128)(2,1)}, bf16[144,4224]{1,0:T(8,128)(2,1)}, bf16[144,4224]{1,0:T(8,128)(2,1)}, bf16[144,4224]{1,0:T(8,128)(2,1)}) custom-call(bf16[576,576]{1,0:T(8,128)(2,1)} %fusion.14.matrix_ref, bf16[144,4224]{1,0:T(8,128)(2,1)} %pad_maximum_fusion.1.refs_0_, bf16[144,4224]{1,0:T(8,128)(2,1)} %collective-permute-done.6.refs_1_, ...), custom_call_target="tpu_custom_call" | custom-call | flops 2802843648 | bytes 9732096 | tf_op jit(solution)/shard_map/swap_blocks/pallas_call | solution.py:68
  86.1 1.3 collective-permute-start.9
  87.4 2.1 collective-permute-start.10
  89.4 1.1 collective-permute-start.11
  90.6 1.6 collective-permute-start.4
  92.1 9.7 %collective-permute-done.3.refs_1_ = bf16[144,4096]{1,0:T(8,128)(2,1)} collective-permute-done((bf16[144,4096]{1,0:T(8,128)(2,1)}, bf16[144,4096]{1,0:T(8,128)(2,1)}, u32[]{:S(2)}, u32[]{:S(2)}) %collective-permute-start.3) | collective-permute-done | bytes 1179680 | tf_op jit(solution)/shard_map/ppermute | solution.py:31
  101.8 1.5 collective-permute-start.5
  103.3 13.6 %collective-permute-done.4.refs_2_ = bf16[144,4096]{1,0:T(8,128)(2,1)S(1)} collective-permute-done((bf16[144,4096]{1,0:T(8,128)(2,1)}, bf16[144,4096]{1,0:T(8,128)(2,1)S(1)}, u32[]{:S(2)}, u32[]{:S(2)}) %collective-permute-start.4) | collective-permute-done | bytes 1179680 | tf_op jit(solution)/shard_map/ppermute | solution.py:31
  116.9 11.7 %collective-permute-done.5.refs_3_ = bf16[144,4096]{1,0:T(8,128)(2,1)S(1)} collective-permute-done((bf16[144,4096]{1,0:T(8,128)(2,1)}, bf16[144,4096]{1,0:T(8,128)(2,1)S(1)}, u32[]{:S(2)}, u32[]{:S(2)}) %collective-permute-start.5) | collective-permute-done | bytes 1179680 | tf_op jit(solution)/shard_map/ppermute | solution.py:31
  128.6 14.2 %collective-permute-done.11.refs_7_.refs_11_ = bf16[144,4224]{1,0:T(8,128)(2,1)S(1)} collective-permute-done((bf16[144,4224]{1,0:T(8,128)(2,1)}, bf16[144,4224]{1,0:T(8,128)(2,1)S(1)}, u32[]{:S(2)}, u32[]{:S(2)}) %collective-permute-start.11) | collective-permute-done | bytes 1216544 | tf_op jit(solution)/shard_map/ppermute | solution.py:31
  142.9 1.0 copy-done.11
  143.9 23.7 %forward.1 = (bf16[576,704]{1,0:T(8,128)(2,1)}, bf16[576,704]{1,0:T(8,128)(2,1)}, bf16[576,704]{1,0:T(8,128)(2,1)}, bf16[576,704]{1,0:T(8,128)(2,1)}, bf16[576,7...) custom-call(bf16[576,576]{1,0:T(8,128)(2,1)} %fusion.14.matrix_ref, bf16[3,704,4096]{2,1,0:T(8,128)(2,1)} %bitcast.31, ...), custom_call_target="tpu_custom_call" | custom-call | flops 9965666304 | bytes 26738688 | tf_op jit(solution)/shard_map/forward/pallas_call | solution.py:134
  167.6 19.8 %terms.1 = bf16[8,3,88,4096]{3,2,1,0:T(8,128)(2,1)} custom-call(bf16[576,704]{1,0:T(8,128)(2,1)} %get-tuple-element.41.gate_ref, bf16[576,704]{1,0:T(8,128)(2,1)} %get-tuple-element.42.up_ref, bf16[576,704]{1,0:T(8,128)(2,1)} %get-tuple-element.62.hidden_ref, bf16[144,4096]{1,0:T(8,128)(2,1)} %get-tuple-element.33.refs_0_, ...), custom_call_target="tpu_custom_call" | custom-call | flops 9965666304 | bytes 26738688 | tf_op jit(solution)/shard_map/terms/pallas_call | solution.py:179
  187.5 7.5 %inputs.3 = (bf16[144,2048]{1,0:T(8,128)(2,1)}, bf16[144,2048]{1,0:T(8,128)(2,1)}, bf16[144,2048]{1,0:T(8,128)(2,1)}, bf16[144,2048]{1,0:T(8,128)(2,1)}) custom-call(bf16[576,704]{1,0:T(8,128)(2,1)} %get-tuple-element.52.gate_ref, bf16[576,704]{1,0:T(8,128)(2,1)} %get-tuple-element.53.up_ref, bf16[3,704,4096]{2,1,0:T(8,128)(2,1)} %bitcast.32), custom_call_target="tpu_custom_call" | custom-call | flops 3321888768 | bytes 8126464 | tf_op jit(solution)/shard_map/inputs/pallas_call | solution.py:208
  195.5 0.9 collective-permute-start.19
  196.4 0.9 collective-permute-start.20
  197.3 7.5 %inputs.2 = (bf16[144,2048]{1,0:T(8,128)(2,1)}, bf16[144,2048]{1,0:T(8,128)(2,1)}, bf16[144,2048]{1,0:T(8,128)(2,1)}, bf16[144,2048]{1,0:T(8,128)(2,1)}) custom-call(bf16[576,704]{1,0:T(8,128)(2,1)} %get-tuple-element.41.gate_ref, bf16[576,704]{1,0:T(8,128)(2,1)} %get-tuple-element.42.up_ref, bf16[3,704,4096]{2,1,0:T(8,128)(2,1)} %bitcast.33), custom_call_target="tpu_custom_call" | custom-call | flops 3321888768 | bytes 8126464 | tf_op jit(solution)/shard_map/inputs/pallas_call | solution.py:208
  204.7 1.2 pad_maximum_fusion.8
  205.9 2.8 collective-permute-start.14
  208.8 1.8 collective-permute-start.13
  210.7 1.7 collective-permute-start.12
  212.3 7.2 %collective-permute-done.20.refs_3_ = bf16[144,2048]{1,0:T(8,128)(2,1)S(1)} collective-permute-done((bf16[144,2048]{1,0:T(8,128)(2,1)}, bf16[144,2048]{1,0:T(8,128)(2,1)S(1)}, u32[]{:S(2)}, u32[]{:S(2)}) %collective-permute-start.20) | collective-permute-done | bytes 589856 | tf_op jit(solution)/shard_map/ppermute | solution.py:31
  219.6 0.8 copy-done.21
  220.4 4.9 %swap_blocks.7 = (bf16[144,2048]{1,0:T(8,128)(2,1)}, bf16[144,2048]{1,0:T(8,128)(2,1)}, bf16[144,2048]{1,0:T(8,128)(2,1)}, bf16[144,2048]{1,0:T(8,128)(2,1)}) custom-call(bf16[576,576]{1,0:T(8,128)(2,1)} %fusion.14.matrix_ref, bf16[144,2048]{1,0:T(8,128)(2,1)} %get-tuple-element.54.refs_0_, bf16[144,2048]{1,0:T(8,128)(2,1)} %copy-done.19, ...), custom_call_target="tpu_custom_call" | custom-call | flops 1358954496 | bytes 4718592 | tf_op jit(solution)/shard_map/swap_blocks/pallas_call | solution.py:68
  225.3 3.6 %collective-permute-start.21 = (bf16[144,2048]{1,0:T(8,128)(2,1)}, bf16[144,2048]{1,0:T(8,128)(2,1)S(1)}, u32[]{:S(2)}, u32[]{:S(2)}) collective-permute-start(bf16[144,2048]{1,0:T(8,128)(2,1)} %get-tuple-element.59), channel_id=1, source_target_pairs={{0,3},{1,0},{2,1},{3,2},{4,7},{5,4},{6,5},{7,6},{8,11},{9,8},{10,9... | collective-permute-start | bytes 1769480 | tf_op jit(solution)/shard_map/ppermute | solution.py:31
  229.4 2.0 collective-permute-start.23
  231.4 0.9 pad_maximum_fusion.5.refs_0_
  232.3 4.8 %collective-permute-done.13.refs_2_ = bf16[144,2176]{1,0:T(8,128)(2,1)S(1)} collective-permute-done((bf16[144,2176]{1,0:T(8,128)(2,1)S(1)}, bf16[144,2176]{1,0:T(8,128)(2,1)S(1)}, u32[]{:S(2)}, u32[]{:S(2)}) %collective-permute-start.13) | collective-permute-done | bytes 626720 | tf_op jit(solution)/shard_map/ppermute | solution.py:31
  238.0 0.8 copy-done.18
  238.8 5.7 %swap_blocks.6 = (bf16[144,2176]{1,0:T(8,128)(2,1)}, bf16[144,2176]{1,0:T(8,128)(2,1)}, bf16[144,2176]{1,0:T(8,128)(2,1)}, bf16[144,2176]{1,0:T(8,128)(2,1)}) custom-call(bf16[576,576]{1,0:T(8,128)(2,1)} %fusion.14.matrix_ref, bf16[144,2176]{1,0:T(8,128)(2,1)} %pad_maximum_fusion.5.refs_0_, bf16[144,2176]{1,0:T(8,128)(2,1)} %copy-done.18, ...), custom_call_target="tpu_custom_call" | custom-call | flops 1443889152 | bytes 5013504 | tf_op jit(solution)/shard_map/swap_blocks/pallas_call | solution.py:68
  244.5 2.3 collective-permute-start.15
  246.8 7.2 %collective-permute-done.21 = bf16[144,2048]{1,0:T(8,128)(2,1)S(1)} collective-permute-done((bf16[144,2048]{1,0:T(8,128)(2,1)}, bf16[144,2048]{1,0:T(8,128)(2,1)S(1)}, u32[]{:S(2)}, u32[]{:S(2)}) %collective-permute-start.21) | collective-permute-done | bytes 589856 | tf_op jit(solution)/shard_map/ppermute | solution.py:31
  254.0 1.1 slice.64
  255.1 0.9 slice_reduce_fusion.3
  256.0 1.9 collective-permute-done.23
  257.9 1.0 convolution_convert_fusion.8
  259.5 12.5 %collective-permute-done.17 = bf16[144,2176]{1,0:T(8,128)(2,1)S(1)} collective-permute-done((bf16[144,2176]{1,0:T(8,128)(2,1)}, bf16[144,2176]{1,0:T(8,128)(2,1)S(1)}, u32[]{:S(2)}, u32[]{:S(2)}) %collective-permute-start.17) | collective-permute-done | bytes 626720 | tf_op jit(solution)/shard_map/ppermute | solution.py:31
  272.5 1.2 select_reduce_fusion
  273.6 1.0 convolution_convert_fusion.9
  274.7 1.3 pad_maximum_fusion
  276.0 8.3 %reduce-scatter.2.cloned.1.call-done = bf16[1,3,88,4096]{3,2,1,0:T(8,128)(2,1)} async-done(((bf16[8,3,88,4096]{3,2,1,0:T(8,128)(2,1)}), bf16[1,3,88,4096]{3,2,1,0:T(8,128)(2,1)}) %reduce-scatter.2.cloned.1.call-update) | async-done | bytes 2162704 | tf_op jit(solution)/shard_map/reduce_scatter | solution.py:286
  284.3 4.3 %convert_bitcast_fusion = f32[1,88,3,4096]{3,1,2,0:T(8,128)} fusion(bf16[1,3,88,4096]{3,2,1,0:T(8,128)(2,1)} %reduce-scatter.2.cloned.1.call-done), kind=kLoop, calls=%fused_computation.8 | loop fusion | flops 1081344 | bytes 6488064 | tf_op jit(solution)/shard_map/transpose | solution.py:287
  (88 shorter events, 5.5 us)
Async XLA Ops:
  7.2 1.9 copy-start
  7.2 277.1 %reduce-scatter.2.cloned.1.call-start = ((), (), s32[]{:S(2)}) async-start(), calls=%async_computation.1 | async-start | bytes 19464192 | tf_op jit(solution)/shard_map/reduce_scatter | solution.py:286
  9.6 30.2 %collective-permute-start.2 = (bf16[144,4096]{1,0:T(8,128)(2,1)S(1)}, bf16[144,4096]{1,0:T(8,128)(2,1)S(1)}, u32[]{:S(2)}, u32[]{:S(2)}) collective-permute-start(bf16[144,4096]{1,0:T(8,128)(2,1)S(1)} %convolution_convert_fusion.4), channel_id=1, source_target_pairs={{0,8},{1,9},{2,10},{3,11},{4,12},{5,13},{6,14},{7,15},{8,0},{9,1},... | collective-permute-start | bytes 3538952 | tf_op jit(solution)/shard_map/ppermute | solution.py:31
  14.7 2.2 copy-start.7
  14.7 2.8 copy-start.2
  14.7 51.0 %collective-permute-start.1 = (bf16[144,4096]{1,0:T(8,128)(2,1)S(1)}, bf16[144,4096]{1,0:T(8,128)(2,1)S(1)}, u32[]{:S(2)}, u32[]{:S(2)}) collective-permute-start(bf16[144,4096]{1,0:T(8,128)(2,1)S(1)} %convolution_convert_fusion.5), channel_id=1, source_target_pairs={{0,12},{1,13},{2,14},{3,15},{4,0},{5,1},{6,2},{7,3},{8,4},{9,5},{1... | collective-permute-start | bytes 3538952 | tf_op jit(solution)/shard_map/ppermute | solution.py:31
  15.8 50.9 %collective-permute-start = (bf16[144,4096]{1,0:T(8,128)(2,1)S(1)}, bf16[144,4096]{1,0:T(8,128)(2,1)}, u32[]{:S(2)}, u32[]{:S(2)}) collective-permute-start(bf16[144,4096]{1,0:T(8,128)(2,1)S(1)} %convolution_convert_fusion.6), channel_id=1, source_target_pairs={{0,4},{1,5},{2,6},{3,7},{4,8},{5,9},{6,10},{7,11},{8,12},{9,13},{1... | collective-permute-start | bytes 3538952 | tf_op jit(solution)/shard_map/ppermute | solution.py:31
  18.2 59.0 %collective-permute-start.8 = (bf16[144,4224]{1,0:T(8,128)(2,1)S(1)}, bf16[144,4224]{1,0:T(8,128)(2,1)S(1)}, u32[]{:S(2)}, u32[]{:S(2)}) collective-permute-start(bf16[144,4224]{1,0:T(8,128)(2,1)S(1)} %pad_maximum_fusion.4), channel_id=1, source_target_pairs={{0,2},{1,3},{2,0},{3,1},{4,6},{5,7},{6,4},{7,5},{8,10},{9,11},{10,... | collective-permute-start | bytes 3649544 | tf_op jit(solution)/shard_map/ppermute | solution.py:31
  21.8 55.4 %collective-permute-start.7 = (bf16[144,4224]{1,0:T(8,128)(2,1)S(1)}, bf16[144,4224]{1,0:T(8,128)(2,1)}, u32[]{:S(2)}, u32[]{:S(2)}) collective-permute-start(bf16[144,4224]{1,0:T(8,128)(2,1)S(1)} %pad_maximum_fusion.3), channel_id=1, source_target_pairs={{0,3},{1,0},{2,1},{3,2},{4,7},{5,4},{6,5},{7,6},{8,11},{9,8},{10,9... | collective-permute-start | bytes 3649544 | tf_op jit(solution)/shard_map/ppermute | solution.py:31
  39.9 25.8 %copy-start.12 = (bf16[144,4096]{1,0:T(8,128)(2,1)}, bf16[144,4096]{1,0:T(8,128)(2,1)S(1)}, u32[]{:S(2)}) copy-start(bf16[144,4096]{1,0:T(8,128)(2,1)S(1)} %collective-permute-done.2.refs_3_) | copy-start | bytes 3538948
  39.9 37.3 %collective-permute-start.6 = (bf16[144,4224]{1,0:T(8,128)(2,1)S(1)}, bf16[144,4224]{1,0:T(8,128)(2,1)}, u32[]{:S(2)}, u32[]{:S(2)}) collective-permute-start(bf16[144,4224]{1,0:T(8,128)(2,1)S(1)} %pad_maximum_fusion.2), channel_id=1, source_target_pairs={{0,1},{1,2},{2,3},{3,0},{4,5},{5,6},{6,7},{7,4},{8,9},{9,10},{10,1... | collective-permute-start | bytes 3649544 | tf_op jit(solution)/shard_map/ppermute | solution.py:31
  65.7 1.0 copy-start.13
  74.3 27.5 %collective-permute-start.3 = (bf16[144,4096]{1,0:T(8,128)(2,1)}, bf16[144,4096]{1,0:T(8,128)(2,1)}, u32[]{:S(2)}, u32[]{:S(2)}) collective-permute-start(bf16[144,4096]{1,0:T(8,128)(2,1)} %get-tuple-element.34), channel_id=1, source_target_pairs={{0,1},{1,2},{2,3},{3,0},{4,5},{5,6},{6,7},{7,4},{8,9},{9,10},{10,1... | collective-permute-start | bytes 3538952 | tf_op jit(solution)/shard_map/ppermute | solution.py:31
  77.2 1.0 copy-start.8
  86.1 42.5 %collective-permute-start.9 = (bf16[144,4224]{1,0:T(8,128)(2,1)}, bf16[144,4224]{1,0:T(8,128)(2,1)S(1)}, u32[]{:S(2)}, u32[]{:S(2)}) collective-permute-start(bf16[144,4224]{1,0:T(8,128)(2,1)} %get-tuple-element.38), channel_id=1, source_target_pairs={{0,4},{1,5},{2,6},{3,7},{4,8},{5,9},{6,10},{7,11},{8,12},{9,13},{1... | collective-permute-start | bytes 3649544 | tf_op jit(solution)/shard_map/ppermute | solution.py:31
  87.4 41.3 %collective-permute-start.10 = (bf16[144,4224]{1,0:T(8,128)(2,1)}, bf16[144,4224]{1,0:T(8,128)(2,1)S(1)}, u32[]{:S(2)}, u32[]{:S(2)}) collective-permute-start(bf16[144,4224]{1,0:T(8,128)(2,1)} %get-tuple-element.39), channel_id=1, source_target_pairs={{0,12},{1,13},{2,14},{3,15},{4,0},{5,1},{6,2},{7,3},{8,4},{9,5},{1... | collective-permute-start | bytes 3649544 | tf_op jit(solution)/shard_map/ppermute | solution.py:31
  89.4 53.4 %collective-permute-start.11 = (bf16[144,4224]{1,0:T(8,128)(2,1)}, bf16[144,4224]{1,0:T(8,128)(2,1)S(1)}, u32[]{:S(2)}, u32[]{:S(2)}) collective-permute-start(bf16[144,4224]{1,0:T(8,128)(2,1)} %get-tuple-element.40), channel_id=1, source_target_pairs={{0,8},{1,9},{2,10},{3,11},{4,12},{5,13},{6,14},{7,15},{8,0},{9,1},... | collective-permute-start | bytes 3649544 | tf_op jit(solution)/shard_map/ppermute | solution.py:31
  90.6 26.3 %collective-permute-start.4 = (bf16[144,4096]{1,0:T(8,128)(2,1)}, bf16[144,4096]{1,0:T(8,128)(2,1)S(1)}, u32[]{:S(2)}, u32[]{:S(2)}) collective-permute-start(bf16[144,4096]{1,0:T(8,128)(2,1)} %get-tuple-element.35), channel_id=1, source_target_pairs={{0,3},{1,0},{2,1},{3,2},{4,7},{5,4},{6,5},{7,6},{8,11},{9,8},{10,9... | collective-permute-start | bytes 3538952 | tf_op jit(solution)/shard_map/ppermute | solution.py:31
  101.8 26.8 %collective-permute-start.5 = (bf16[144,4096]{1,0:T(8,128)(2,1)}, bf16[144,4096]{1,0:T(8,128)(2,1)S(1)}, u32[]{:S(2)}, u32[]{:S(2)}) collective-permute-start(bf16[144,4096]{1,0:T(8,128)(2,1)} %get-tuple-element.36), channel_id=1, source_target_pairs={{0,2},{1,3},{2,0},{3,1},{4,6},{5,7},{6,4},{7,5},{8,10},{9,11},{10,... | collective-permute-start | bytes 3538952 | tf_op jit(solution)/shard_map/ppermute | solution.py:31
  116.9 26.0 %copy-start.14 = (bf16[144,4096]{1,0:T(8,128)(2,1)}, bf16[144,4096]{1,0:T(8,128)(2,1)S(1)}, u32[]{:S(2)}) copy-start(bf16[144,4096]{1,0:T(8,128)(2,1)S(1)} %collective-permute-done.4.refs_2_) | copy-start | bytes 3538948
  128.6 14.3 %copy-start.15 = (bf16[144,4096]{1,0:T(8,128)(2,1)}, bf16[144,4096]{1,0:T(8,128)(2,1)S(1)}, u32[]{:S(2)}) copy-start(bf16[144,4096]{1,0:T(8,128)(2,1)S(1)} %collective-permute-done.5.refs_3_) | copy-start | bytes 3538948
  128.6 14.3 %copy-start.9 = (bf16[144,4224]{1,0:T(8,128)(2,1)}, bf16[144,4224]{1,0:T(8,128)(2,1)S(1)}, u32[]{:S(2)}) copy-start(bf16[144,4224]{1,0:T(8,128)(2,1)S(1)} %collective-permute-done.9.refs_5_.refs_9_) | copy-start | bytes 3649540
  128.6 14.3 %copy-start.10 = (bf16[144,4224]{1,0:T(8,128)(2,1)}, bf16[144,4224]{1,0:T(8,128)(2,1)S(1)}, u32[]{:S(2)}) copy-start(bf16[144,4224]{1,0:T(8,128)(2,1)S(1)} %collective-permute-done.10.refs_6_.refs_10_) | copy-start | bytes 3649540
  142.9 1.0 copy-start.11
  187.5 9.8 %copy-start.6 = (bf16[576,128]{1,0:T(8,128)(2,1)S(1)}, bf16[576,128]{1,0:T(8,128)(2,1)}, u32[]{:S(2)}) copy-start(bf16[576,128]{1,0:T(8,128)(2,1)} %get-tuple-element.44) | copy-start | bytes 442372
  194.9 15.7 %collective-permute-start.18 = (bf16[144,2048]{1,0:T(8,128)(2,1)}, bf16[144,2048]{1,0:T(8,128)(2,1)S(1)}, u32[]{:S(2)}, u32[]{:S(2)}) collective-permute-start(bf16[144,2048]{1,0:T(8,128)(2,1)} %get-tuple-element.55), channel_id=1, source_target_pairs={{0,12},{1,13},{2,14},{3,15},{4,0},{5,1},{6,2},{7,3},{8,4},{9,5},{1... | collective-permute-start | bytes 1769480 | tf_op jit(solution)/shard_map/ppermute | solution.py:31
  195.5 16.9 %collective-permute-start.19 = (bf16[144,2048]{1,0:T(8,128)(2,1)}, bf16[144,2048]{1,0:T(8,128)(2,1)S(1)}, u32[]{:S(2)}, u32[]{:S(2)}) collective-permute-start(bf16[144,2048]{1,0:T(8,128)(2,1)} %get-tuple-element.56), channel_id=1, source_target_pairs={{0,4},{1,5},{2,6},{3,7},{4,8},{5,9},{6,10},{7,11},{8,12},{9,13},{1... | collective-permute-start | bytes 1769480 | tf_op jit(solution)/shard_map/ppermute | solution.py:31
  196.4 23.2 %collective-permute-start.20 = (bf16[144,2048]{1,0:T(8,128)(2,1)}, bf16[144,2048]{1,0:T(8,128)(2,1)S(1)}, u32[]{:S(2)}, u32[]{:S(2)}) collective-permute-start(bf16[144,2048]{1,0:T(8,128)(2,1)} %get-tuple-element.57), channel_id=1, source_target_pairs={{0,8},{1,9},{2,10},{3,11},{4,12},{5,13},{6,14},{7,15},{8,0},{9,1},... | collective-permute-start | bytes 1769480 | tf_op jit(solution)/shard_map/ppermute | solution.py:31
  204.7 4.0 %copy-start.5 = (bf16[144,2048]{1,0:T(8,128)(2,1)S(1)}, bf16[144,2048]{1,0:T(8,128)(2,1)}, u32[]{:S(2)}) copy-start(bf16[144,2048]{1,0:T(8,128)(2,1)} %get-tuple-element.46) | copy-start | bytes 1769476
  204.7 5.9 %copy-start.4 = (bf16[144,2048]{1,0:T(8,128)(2,1)S(1)}, bf16[144,2048]{1,0:T(8,128)(2,1)}, u32[]{:S(2)}) copy-start(bf16[144,2048]{1,0:T(8,128)(2,1)} %get-tuple-element.45) | copy-start | bytes 1769476
  205.9 23.4 %collective-permute-start.14 = (bf16[144,2176]{1,0:T(8,128)(2,1)S(1)}, bf16[144,2176]{1,0:T(8,128)(2,1)S(1)}, u32[]{:S(2)}, u32[]{:S(2)}) collective-permute-start(bf16[144,2176]{1,0:T(8,128)(2,1)S(1)} %pad_maximum_fusion.8), channel_id=1, source_target_pairs={{0,2},{1,3},{2,0},{3,1},{4,6},{5,7},{6,4},{7,5},{8,10},{9,11},{10,... | collective-permute-start | bytes 1880072 | tf_op jit(solution)/shard_map/ppermute | solution.py:31
  208.8 28.3 %collective-permute-start.13 = (bf16[144,2176]{1,0:T(8,128)(2,1)S(1)}, bf16[144,2176]{1,0:T(8,128)(2,1)S(1)}, u32[]{:S(2)}, u32[]{:S(2)}) collective-permute-start(bf16[144,2176]{1,0:T(8,128)(2,1)S(1)} %pad_maximum_fusion.7), channel_id=1, source_target_pairs={{0,1},{1,2},{2,3},{3,0},{4,5},{5,6},{6,7},{7,4},{8,9},{9,10},{10,1... | collective-permute-start | bytes 1880072 | tf_op jit(solution)/shard_map/ppermute | solution.py:31
  210.7 8.9 %copy-start.19 = (bf16[144,2048]{1,0:T(8,128)(2,1)}, bf16[144,2048]{1,0:T(8,128)(2,1)S(1)}, u32[]{:S(2)}) copy-start(bf16[144,2048]{1,0:T(8,128)(2,1)S(1)} %collective-permute-done.18.refs_1_) | copy-start | bytes 1769476
  210.7 26.8 %collective-permute-start.12 = (bf16[144,2176]{1,0:T(8,128)(2,1)S(1)}, bf16[144,2176]{1,0:T(8,128)(2,1)S(1)}, u32[]{:S(2)}, u32[]{:S(2)}) collective-permute-start(bf16[144,2176]{1,0:T(8,128)(2,1)S(1)} %pad_maximum_fusion.6), channel_id=1, source_target_pairs={{0,3},{1,0},{2,1},{3,2},{4,7},{5,4},{6,5},{7,6},{8,11},{9,8},{10,9... | collective-permute-start | bytes 1880072 | tf_op jit(solution)/shard_map/ppermute | solution.py:31
  212.3 7.2 %copy-start.20 = (bf16[144,2048]{1,0:T(8,128)(2,1)}, bf16[144,2048]{1,0:T(8,128)(2,1)S(1)}, u32[]{:S(2)}) copy-start(bf16[144,2048]{1,0:T(8,128)(2,1)S(1)} %collective-permute-done.19.refs_2_) | copy-start | bytes 1769476
  219.6 0.8 copy-start.21
  220.4 11.0 %copy-start.3 = (bf16[144,2048]{1,0:T(8,128)(2,1)S(1)}, bf16[144,2048]{1,0:T(8,128)(2,1)}, u32[]{:S(2)}) copy-start(bf16[144,2048]{1,0:T(8,128)(2,1)} %get-tuple-element.43) | copy-start | bytes 1769476
  225.3 28.7 %collective-permute-start.21 = (bf16[144,2048]{1,0:T(8,128)(2,1)}, bf16[144,2048]{1,0:T(8,128)(2,1)S(1)}, u32[]{:S(2)}, u32[]{:S(2)}) collective-permute-start(bf16[144,2048]{1,0:T(8,128)(2,1)} %get-tuple-element.59), channel_id=1, source_target_pairs={{0,3},{1,0},{2,1},{3,2},{4,7},{5,4},{6,5},{7,6},{8,11},{9,8},{10,9... | collective-permute-start | bytes 1769480 | tf_op jit(solution)/shard_map/ppermute | solution.py:31
  228.9 27.1 %collective-permute-start.22 = (bf16[144,2048]{1,0:T(8,128)(2,1)}, bf16[144,2048]{1,0:T(8,128)(2,1)S(1)}, u32[]{:S(2)}, u32[]{:S(2)}) collective-permute-start(bf16[144,2048]{1,0:T(8,128)(2,1)} %get-tuple-element.60), channel_id=1, source_target_pairs={{0,1},{1,2},{2,3},{3,0},{4,5},{5,6},{6,7},{7,4},{8,9},{9,10},{10,1... | collective-permute-start | bytes 1769480 | tf_op jit(solution)/shard_map/ppermute | solution.py:31
  229.4 8.1 %copy-start.16 = (bf16[144,2176]{1,0:T(8,128)(2,1)}, bf16[144,2176]{1,0:T(8,128)(2,1)S(1)}, u32[]{:S(2)}) copy-start(bf16[144,2176]{1,0:T(8,128)(2,1)S(1)} %collective-permute-done.14.refs_3_) | copy-start | bytes 1880068
  229.4 28.5 %collective-permute-start.23 = (bf16[144,2048]{1,0:T(8,128)(2,1)}, bf16[144,2048]{1,0:T(8,128)(2,1)S(1)}, u32[]{:S(2)}, u32[]{:S(2)}) collective-permute-start(bf16[144,2048]{1,0:T(8,128)(2,1)} %get-tuple-element.61), channel_id=1, source_target_pairs={{0,2},{1,3},{2,0},{3,1},{4,6},{5,7},{6,4},{7,5},{8,10},{9,11},{10,... | collective-permute-start | bytes 1769480 | tf_op jit(solution)/shard_map/ppermute | solution.py:31
  232.3 25.6 %copy-start.22 = (bf16[144,2048]{1,0:T(8,128)(2,1)S(1)}, bf16[144,2048]{1,0:T(8,128)(2,1)}, u32[]{:S(2)}) copy-start(bf16[144,2048]{1,0:T(8,128)(2,1)} %get-tuple-element.58) | copy-start | bytes 1769476
  237.1 0.8 copy-start.17
  237.9 0.8 copy-start.18
  244.5 14.4 %collective-permute-start.15 = (bf16[144,2176]{1,0:T(8,128)(2,1)}, bf16[144,2176]{1,0:T(8,128)(2,1)S(1)}, u32[]{:S(2)}, u32[]{:S(2)}) collective-permute-start(bf16[144,2176]{1,0:T(8,128)(2,1)} %get-tuple-element.49), channel_id=1, source_target_pairs={{0,12},{1,13},{2,14},{3,15},{4,0},{5,1},{6,2},{7,3},{8,4},{9,5},{1... | collective-permute-start | bytes 1880072 | tf_op jit(solution)/shard_map/ppermute | solution.py:31
  246.8 12.7 %collective-permute-start.16 = (bf16[144,2176]{1,0:T(8,128)(2,1)}, bf16[144,2176]{1,0:T(8,128)(2,1)S(1)}, u32[]{:S(2)}, u32[]{:S(2)}) collective-permute-start(bf16[144,2176]{1,0:T(8,128)(2,1)} %get-tuple-element.50), channel_id=1, source_target_pairs={{0,4},{1,5},{2,6},{3,7},{4,8},{5,9},{6,10},{7,11},{8,12},{9,13},{1... | collective-permute-start | bytes 1880072 | tf_op jit(solution)/shard_map/ppermute | solution.py:31
  254.0 18.0 %collective-permute-start.17 = (bf16[144,2176]{1,0:T(8,128)(2,1)}, bf16[144,2176]{1,0:T(8,128)(2,1)S(1)}, u32[]{:S(2)}, u32[]{:S(2)}) collective-permute-start(bf16[144,2176]{1,0:T(8,128)(2,1)} %get-tuple-element.51), channel_id=1, source_target_pairs={{0,8},{1,9},{2,10},{3,11},{4,12},{5,13},{6,14},{7,15},{8,0},{9,1},... | collective-permute-start | bytes 1880072 | tf_op jit(solution)/shard_map/ppermute | solution.py:31
  284.3 4.3 %copy-start.1 = (bf16[192,4096]{1,0:T(8,128)(2,1)S(1)}, bf16[192,4096]{1,0:T(8,128)(2,1)}, u32[]{:S(2)}) copy-start(bf16[192,4096]{1,0:T(8,128)(2,1)} %param.5) | copy-start | bytes 4718596
Sparse Core Ops, SparseCore 0:
  187.6 96.6 reduce-scatter.1
where the time goes:
time: 296 us; the launch traced here: 295 us
  waiting for transfers between devices  130 us (44%)
  Pallas kernels  84.5 us (29%)
  starting transfers between devices  36.8 us (12%)
  between operations  14.4 us (5%)
  other arithmetic  13.8 us (5%)
  local copies, waits for them, and re-layouts  8.06 us (3%)
  matrix products  7.52 us (3%)
    ppermute x24, waiting for transfers between devices, move(): lax.ppermute(value, 'expert', hop(step, 0) if axis == 'z' else hop(0, step))  122 us
    ppermute x24, starting transfers between devices, move(): lax.ppermute(value, 'expert', hop(step, 0) if axis == 'z' else hop(0, step))  36.8 us
    pallas_call x4, Pallas kernels, swap_blocks(): pl.pallas_call(swap_kernel, grid=(width // tile,), in_specs=[pl.BlockSpec...  26 us
    pallas_call x1, Pallas kernels, forward(): pl.pallas_call(functools.partial(forward_kernel, steps), grid=(steps,), i...  23.7 us
    pallas_call x1, Pallas kernels, terms(): pl.pallas_call(terms_kernel, grid=(width // tile,), in_specs=[whole] * 3...  19.8 us
    pallas_call x2, Pallas kernels, inputs(): pl.pallas_call(functools.partial(inputs_kernel, count // tile), grid=(cou...  14.9 us
    reduce_scatter x1, waiting for transfers between devices, shards(): lax.psum_scatter(partial_sums, 'dp', scatter_dimension=0, tiled=True)  8.29 us
  transfers between devices with their start and end apart: 25, of which 14 were waited for; matrix products, arithmetic and copies ran while one was open for 6% of the time, Pallas kernels for 14%

commit v1 on v0

v1 whole, which is shorter than its diff:
```python
import functools

import jax
import jax.numpy as jnp
from jax import lax
from jax.experimental import pallas as pl
from jax.experimental.pallas import tpu as pltpu
from jax.sharding import PartitionSpec as P

CAP = 36
SIDE = 4
BLOCK = SIDE * CAP
ROWS = SIDE * BLOCK
EXTRA = 128
HOPS = (0, 1, 3, 2)
MAIN = 32
TAIL = CAP - MAIN
EARLY = 384
BIG = 56 << 20


def hop(dz, dx):
    return [
        (z * SIDE + x, (z + dz) % SIDE * SIDE + (x + dx) % SIDE)
        for z in range(SIDE)
        for x in range(SIDE)
    ]


def move(value, axis, step):
    if step % SIDE == 0:
        return value
    return lax.ppermute(value, "expert", hop(step, 0) if axis == "z" else hop(0, step))


def spread(blocks, axis, sign):
    return [move(blocks[p], axis, sign * HOPS[p]) for p in range(SIDE)]


def product(left, right, dims=((1,), (0,))):
    return lax.dot_general(left, right, (dims, ((), ())), preferred_element_type=jnp.float32)


def place(block, lane, slot):
    inner = jnp.where(slot < MAIN, lane * MAIN + slot, SIDE * MAIN + lane * TAIL + slot - MAIN)
    return block * BLOCK + inner


def swap_matrix(tails):
    size = SIDE * SIDE * TAIL if tails else ROWS
    row = jnp.arange(size, dtype=jnp.int32)
    if tails:
        source = row // TAIL % SIDE * SIDE * TAIL + row // TAIL // SIDE * TAIL + row % TAIL
    else:
        block, inner = row // BLOCK, row % BLOCK
        tail = inner - SIDE * MAIN
        lane = jnp.where(tail < 0, inner // MAIN, tail // TAIL)
        slot = jnp.where(tail < 0, inner % MAIN, MAIN + tail % TAIL)
        source = place(lane, block, slot)
    return (source[:, None] == row[None, :]).astype(jnp.bfloat16)


def params():
    return pltpu.CompilerParams(dimension_semantics=("arbitrary",), vmem_limit_bytes=BIG)


def cost(flops, moved):
    return pl.CostEstimate(flops=int(flops), bytes_accessed=int(moved), transcendentals=0)


def swap_kernel(matrix_ref, *refs):
    ins, outs = refs[:SIDE], refs[SIDE:]
    for p in range(SIDE):
        for q in range(SIDE):
            outs[q][p * MAIN : (p + 1) * MAIN] = ins[p][q * MAIN : (q + 1) * MAIN]
    tails = jnp.concatenate([ref[SIDE * MAIN :] for ref in ins], axis=0)
    tails = product(matrix_ref[...], tails).astype(jnp.bfloat16)
    for q in range(SIDE):
        outs[q][SIDE * MAIN :] = tails[q * SIDE * TAIL : (q + 1) * SIDE * TAIL]


def swap_blocks(matrix, blocks):
    width = blocks[0].shape[1]
    tile = 1024 if width % 1024 == 0 else 1408 if width % 1408 == 0 else width
    spec = pl.BlockSpec((BLOCK, tile), lambda i: (0, i))
    return pl.pallas_call(
        swap_kernel,
        grid=(width // tile,),
        in_specs=[pl.BlockSpec(matrix.shape, lambda i: (0, 0))] + [spec] * SIDE,
        out_specs=[spec] * SIDE,
        out_shape=[jax.ShapeDtypeStruct((BLOCK, width), jnp.bfloat16)] * SIDE,
        compiler_params=params(),
        cost_estimate=cost(2 * 64 * 64 * width, 4 * ROWS * width),
        name="swap_blocks",
    )(matrix, *blocks)


LAST = ((1,), (1,))


def early_kernel(weight_ref, *refs):
    toks, cots, outs = refs[0:3], refs[3:6], refs[6:9]

    @pl.when(pl.program_id(0) == 0)
    def _():
        for out in outs:
            out[...] = jnp.zeros_like(out)

    tok, cot = (
        jnp.concatenate([r[0][...], r[1][...], r[2][: EARLY - 2 * BLOCK]], axis=0)
        for r in (toks, cots)
    )
    for kind, right in enumerate((tok, tok, cot)):
        outs[kind][...] += product(weight_ref[kind], right, LAST)


def forward_early(weights, toks, cots):
    units, width = weights.shape[1:]
    tile = 1024
    rows = pl.BlockSpec((BLOCK, tile), lambda i: (0, i))
    whole = pl.BlockSpec((units, EARLY), lambda i: (0, 0))
    return pl.pallas_call(
        early_kernel,
        grid=(width // tile,),
        in_specs=[pl.BlockSpec((3, units, tile), lambda i: (0, 0, i))] + [rows] * 6,
        out_specs=[whole] * 3,
        out_shape=[jax.ShapeDtypeStruct((units, EARLY), jnp.float32)] * 3,
        compiler_params=params(),
        cost_estimate=cost(6 * EARLY * units * width, 6 * units * width + 4 * EARLY * width),
        name="forward_early",
    )(weights, *toks, *cots)


def late_kernel(steps, matrix_ref, weight_ref, *refs):
    toks, cots, scales = refs[0:2], refs[2:4], refs[4:8]
    early = refs[8:11]
    gate_out, up_out, hidden_out, route_out = refs[11:15]
    accs = refs[15:18]
    step = pl.program_id(0)

    @pl.when(step == 0)
    def _():
        for acc in accs:
            acc[...] = jnp.zeros_like(acc)

    tok, cot = (
        jnp.concatenate([r[0][EARLY - 2 * BLOCK :], r[1][...]], axis=0) for r in (toks, cots)
    )
    for kind, right in enumerate((tok, tok, cot)):
        accs[kind][...] += product(weight_ref[kind], right, LAST)

    @pl.when(step == steps - 1)
    def _():
        matrix = matrix_ref[...]
        gate_pre, up_pre, back = (
            jnp.concatenate([first[...], acc[...]], axis=1) for first, acc in zip(early, accs)
        )
        lane = lax.broadcasted_iota(jnp.int32, (8, EXTRA), 1)
        first_lane = jnp.where(lane == 0, 1.0, 0.0).astype(jnp.bfloat16)
        scale = jnp.concatenate([ref[...] for ref in scales], axis=0)
        scale = product(first_lane, scale, LAST)[:1]
        grad = scale * back
        high = grad.astype(jnp.bfloat16)
        low = (grad - high.astype(jnp.float32)).astype(jnp.bfloat16)
        grad = product(high, matrix) + product(low, matrix)
        logistic = 1.0 / (1.0 + jnp.exp(-gate_pre))
        gated = gate_pre * logistic
        hidden = product((gated * up_pre).astype(jnp.bfloat16), matrix)
        hidden_out[...] = hidden.astype(jnp.bfloat16)
        gate_out[...] = (grad * up_pre * logistic * (1.0 + gate_pre * (1.0 - logistic))).astype(
            jnp.bfloat16
        )
        up_out[...] = (grad * gated).astype(jnp.bfloat16)
        route = jnp.sum(hidden * back, axis=0, keepdims=True).astype(jnp.bfloat16)
        route_out[...] = product(matrix, jnp.broadcast_to(route, (EXTRA, ROWS)), LAST).astype(
            jnp.bfloat16
        )


def forward_late(matrix, weights, toks, cots, early):
    units, width = weights.shape[1:]
    tile = 1024
    steps = width // tile
    rows = pl.BlockSpec((BLOCK, tile), lambda i: (0, i))
    extra = pl.BlockSpec((BLOCK, EXTRA), lambda i: (0, width // EXTRA))
    whole = pl.BlockSpec((units, ROWS), lambda i: (0, 0))
    small = jax.ShapeDtypeStruct((units, ROWS), jnp.bfloat16)
    late = ROWS - EARLY
    return pl.pallas_call(
        functools.partial(late_kernel, steps),
        grid=(steps,),
        in_specs=[
            pl.BlockSpec((ROWS, ROWS), lambda i: (0, 0)),
            pl.BlockSpec((3, units, tile), lambda i: (0, 0, i)),
        ]
        + [rows] * 4
        + [extra] * 4
        + [pl.BlockSpec((units, EARLY), lambda i: (0, 0))] * 3,
        out_specs=[whole] * 3 + [pl.BlockSpec((ROWS, EXTRA), lambda i: (0, 0))],
        out_shape=[small] * 3 + [jax.ShapeDtypeStruct((ROWS, EXTRA), jnp.bfloat16)],
        scratch_shapes=[pltpu.VMEM((units, late), jnp.float32)] * 3,
        compiler_params=params(),
        cost_estimate=cost(6 * late * units * width, 6 * units * width + 12 * EARLY * units),
        name="forward_late",
    )(matrix, weights, *toks[2:], *cots[2:], *cots, *early)


def terms_kernel(gate_ref, up_ref, hidden_ref, *refs):
    toks, cots, scales, out_ref = refs[0:4], refs[4:8], refs[8:12], refs[12]
    tok = jnp.concatenate([ref[...] for ref in toks], axis=0)
    scaled = jnp.concatenate(
        [
            (ref[...].astype(jnp.float32) * scale[:, :1].astype(jnp.float32)).astype(jnp.bfloat16)
            for ref, scale in zip(cots, scales)
        ],
        axis=0,
    )
    share = out_ref.shape[2]
    for kind, (left, right) in enumerate(((gate_ref, tok), (up_ref, tok), (hidden_ref, scaled))):
        term = product(left[...], right)
        for owner in range(out_ref.shape[0]):
            out_ref[owner, kind] = term[owner * share : (owner + 1) * share].astype(jnp.bfloat16)


def terms(gate_delta, up_delta, hidden, toks, cots, owners):
    units = gate_delta.shape[0]
    width = toks[0].shape[1]
    tile = 512
    rows = pl.BlockSpec((BLOCK, tile), lambda i: (0, i))
    extra = pl.BlockSpec((BLOCK, EXTRA), lambda i: (0, width // EXTRA))
    whole = pl.BlockSpec((units, ROWS), lambda i: (0, 0))
    share = units // owners
    return pl.pallas_call(
        terms_kernel,
        grid=(width // tile,),
        in_specs=[whole] * 3 + [rows] * 8 + [extra] * 4,
        out_specs=pl.BlockSpec((owners, 3, share, tile), lambda i: (0, 0, 0, i)),
        out_shape=jax.ShapeDtypeStruct((owners, 3, share, width), jnp.bfloat16),
        compiler_params=params(),
        cost_estimate=cost(6 * ROWS * units * width, 6 * units * width + 4 * ROWS * width),
        name="terms",
    )(gate_delta, up_delta, hidden, *toks, *cots, *cots)


def inputs_kernel(tile, turn_ref, gate_ref, up_ref, weight_ref, route_ref, *refs):
    outs, (gate_rows, up_rows) = refs[:SIDE], refs[SIDE:]
    step = pl.program_id(0)

    @pl.when(step == 0)
    def _():
        gate_rows[...] = product(turn_ref[...], gate_ref[...], LAST).astype(jnp.bfloat16)
        up_rows[...] = product(turn_ref[...], up_ref[...], LAST).astype(jnp.bfloat16)
        for p in range(SIDE):
            width = outs[p].shape[1]
            if width % tile:
                outs[p][:, width - EXTRA :] = route_ref[p * BLOCK : (p + 1) * BLOCK]

    value = product(gate_rows[...], weight_ref[0]) + product(up_rows[...], weight_ref[1])
    value = value.astype(jnp.bfloat16)
    columns = pl.ds(pl.multiple_of(step * tile, tile), tile)
    for p in range(SIDE):
        outs[p][:, columns] = value[p * BLOCK : (p + 1) * BLOCK]


def inputs(turn, gate_delta, up_delta, weights, route, first, count, extra):
    units = weights.shape[1]
    tile = 512
    whole = pl.BlockSpec((units, ROWS), lambda i: (0, 0))
    block = (BLOCK, count + extra)
    return pl.pallas_call(
        functools.partial(inputs_kernel, tile),
        grid=(count // tile,),
        in_specs=[
            pl.BlockSpec((ROWS, ROWS), lambda i: (0, 0)),
            whole,
            whole,
            pl.BlockSpec((2, units, tile), lambda i: (0, 0, first // tile + i)),
            pl.BlockSpec((ROWS, EXTRA), lambda i: (0, 0)),
        ],
        out_specs=[pl.BlockSpec(block, lambda i: (0, 0))] * SIDE,
        out_shape=[jax.ShapeDtypeStruct(block, jnp.bfloat16)] * SIDE,
        scratch_shapes=[pltpu.VMEM((ROWS, units), jnp.bfloat16)] * 2,
        compiler_params=params(),
        cost_estimate=cost(4 * ROWS * units * count, 4 * units * count + 2 * ROWS * count),
        name="inputs",
    )(turn, gate_delta, up_delta, weights, route)


def shards(tokens, cotangent, expert_ids, route_weights, expert_weights):
    me = lax.axis_index("expert")
    z, x = me // SIDE, me % SIDE
    tok_rows, width = tokens.shape
    half = width // 2
    experts = SIDE * SIDE
    owners = lax.axis_size("dp")

    ids = expert_ids.T
    column = lax.broadcasted_iota(jnp.int32, (experts, 1, 1), 0)
    named = ids[None] == column
    routed = jnp.any(named, axis=1)
    earlier = (
        lax.broadcasted_iota(jnp.int32, (tok_rows, tok_rows), 0)
        < lax.broadcasted_iota(jnp.int32, (tok_rows, tok_rows), 1)
    ).astype(jnp.bfloat16)
    slots = jnp.dot(routed.astype(jnp.bfloat16), earlier, preferred_element_type=jnp.float32)
    slots = slots.astype(jnp.int32)
    expert = lax.broadcasted_iota(jnp.int32, (experts, 1), 0)
    far_z, far_x = (expert // SIDE - z) % SIDE, (expert % SIDE - x) % SIDE
    near_z = jnp.where(far_z >= 2, 5 - far_z, far_z)
    near_x = jnp.where(far_x >= 2, 5 - far_x, far_x)
    live = jnp.any(named, axis=0)

    def codes(block, lane):
        row = place(block, lane, slots)
        return jnp.where(live, jnp.sum(jnp.where(named, row[:, None, :], 0), axis=0), -1)

    def one_hot(code, first, count):
        row = lax.broadcasted_iota(jnp.int32, (count, tok_rows), 0) + first
        hot = row == code[0][None, :]
        for k in range(1, code.shape[0]):
            hot = hot | (row == code[k][None, :])
        return hot.astype(jnp.bfloat16)

    z_first = codes(near_z, near_x)
    x_first = codes(near_x, near_z)

    def row_scales(code, first):
        row = lax.broadcasted_iota(jnp.int32, (BLOCK, 1, 1), 0) + first
        scale = jnp.where(row == code[None], route_weights.T[None], 0.0)
        return jnp.sum(scale, axis=(1, 2))[:, None].astype(jnp.bfloat16)

    def pick(left, right):
        return jnp.dot(left, right, preferred_element_type=jnp.float32).astype(jnp.bfloat16)

    tok_blocks, cot_blocks = [], []
    for p in range(SIDE):
        tok_blocks.append(pick(one_hot(z_first, p * BLOCK, BLOCK), tokens))
        picked = pick(one_hot(x_first, p * BLOCK, BLOCK), cotangent)
        scale = jnp.broadcast_to(row_scales(x_first, p * BLOCK), (BLOCK, EXTRA))
        cot_blocks.append(jnp.concatenate([picked, scale], axis=1))

    turn = swap_matrix(False)
    small_turn = swap_matrix(True)
    same = (jnp.arange(ROWS)[:, None] == jnp.arange(ROWS)[None, :]).astype(jnp.bfloat16)

    def near_then_far(blocks, axis):
        near = [blocks[0]] + [move(blocks[p], axis, HOPS[p]) for p in (1, 2)]
        far = lax.optimization_barrier((blocks[3], near[1], near[2]))
        return [near[0], far[1], far[2], move(far[0], axis, HOPS[3])]

    toks = near_then_far(swap_blocks(small_turn, spread(tok_blocks, "z", 1)), "x")
    cots = near_then_far(swap_blocks(small_turn, spread(cot_blocks, "x", 1)), "z")

    weights = expert_weights[0].transpose(1, 0, 2)
    early = forward_early(weights, toks[:3], cots[:3])
    gate_delta, up_delta, hidden, route = forward_late(turn, weights, toks, cots, early)
    partial_sums = terms(gate_delta, up_delta, hidden, toks, cots, owners)
    summed = lax.psum_scatter(partial_sums, "dp", scatter_dimension=0, tiled=True)
    weight_grad = summed.astype(jnp.float32).transpose(0, 2, 1, 3)

    right = inputs(turn, gate_delta, up_delta, weights, route, half, half, 0)
    left = inputs(same, gate_delta, up_delta, weights, route, 0, half, EXTRA)
    left = spread(swap_blocks(small_turn, spread(left, "x", -1)), "z", -1)
    right = spread(swap_blocks(small_turn, spread(right, "z", -1)), "x", -1)

    def combine(blocks, code):
        return jnp.einsum(
            "ct,cd->td",
            one_hot(code, 0, ROWS),
            jnp.concatenate(blocks, axis=0),
            preferred_element_type=jnp.float32,
        ).astype(jnp.bfloat16)

    input_grad = jnp.concatenate(
        [combine([b[:, :half] for b in left], z_first), combine(right, x_first)], axis=1
    )
    route_mine = jnp.concatenate([b[:, half] for b in left], axis=0).astype(jnp.float32)
    row = lax.broadcasted_iota(jnp.int32, (ROWS, 1, 1), 0)
    route_grad = jnp.sum(jnp.where(row == z_first[None], route_mine[:, None, None], 0.0), axis=0)
    return input_grad, route_grad.astype(jnp.bfloat16).T, weight_grad


def solution(mesh):
    rows = P(("dp", "expert"), None)
    return jax.shard_map(
        shards,
        mesh=mesh,
        in_specs=(rows, rows, rows, rows, P("expert", None, None, None)),
        out_specs=(rows, rows, P("expert", "dp", None, None)),
        check_vma=False,
    )
```

time: 296 us -> 303 us (1.024)
  starting transfers between devices: 36.8 us -> 50.1 us
  waiting for transfers between devices: 130 us -> 120 us
    ppermute x24, waiting for transfers between devices: 122 us -> 89.8 us  [move(): lax.ppermute(value, 'expert', hop(step, 0) if axis == 'z' else hop(0, step))]
    reduce_scatter x1, waiting for transfers between devices: 8.29 us -> 30.2 us  [shards(): lax.psum_scatter(partial_sums, 'dp', scatter_dimension=0, tiled=True)]
    ppermute x24, starting transfers between devices: 36.8 us -> 50 us  [move(): lax.ppermute(value, 'expert', hop(step, 0) if axis == 'z' else hop(0, step))]
    pallas_call x3 -> x4, Pallas kernels: 38.6 us -> 49.8 us  [the longest x2 19.7 us: inputs(): pl.pallas_call(functools.partial(inputs_kernel, tile), grid=(count // til...]
    pallas_call x4, Pallas kernels: 26 us -> 17.3 us  [swap_blocks(): pl.pallas_call(swap_kernel, grid=(width // tile,), in_specs=[pl.BlockSpec...]
  transfers between devices with their start and end apart: 25 -> 25, of which waited for: 14 -> 14; matrix products, arithmetic and copies ran while one was open for 6% -> 6% of each run, Pallas kernels for 14% -> 17%
where the time goes in v1:
time: 303 us; the launch traced here: 302 us
  waiting for transfers between devices  120 us (40%)
  Pallas kernels  86.5 us (29%)
  starting transfers between devices  50.1 us (17%)
  between operations  14.4 us (5%)
  other arithmetic  13.8 us (5%)
  matrix products  9.65 us (3%)
  local copies, waits for them, and re-layouts  7.75 us (3%)
    ppermute x24, waiting for transfers between devices, move(): lax.ppermute(value, 'expert', hop(step, 0) if axis == 'z' else hop(0, step))  89.8 us
    ppermute x24, starting transfers between devices, move(): lax.ppermute(value, 'expert', hop(step, 0) if axis == 'z' else hop(0, step))  50 us
    reduce_scatter x1, waiting for transfers between devices, shards(): lax.psum_scatter(partial_sums, 'dp', scatter_dimension=0, tiled=True)  30.2 us
    pallas_call x2, Pallas kernels, inputs(): pl.pallas_call(functools.partial(inputs_kernel, tile), grid=(count // til...  19.7 us
    pallas_call x1, Pallas kernels, terms(): pl.pallas_call(terms_kernel, grid=(width // tile,), in_specs=[whole] * 3...  19.4 us
    pallas_call x4, Pallas kernels, swap_blocks(): pl.pallas_call(swap_kernel, grid=(width // tile,), in_specs=[pl.BlockSpec...  17.3 us
    pallas_call x1, Pallas kernels, forward_late(): pl.pallas_call(functools.partial(late_kernel, steps), grid=(steps,), in_s...  15.9 us
    pallas_call x1, Pallas kernels, forward_early(): pl.pallas_call(early_kernel, grid=(width // tile,), in_specs=[pl.BlockSpe...  14.3 us
  transfers between devices with their start and end apart: 25, of which 14 were waited for; matrix products, arithmetic and copies ran while one was open for 6% of the time, Pallas kernels for 17%

profile of v1, /device:TPU:1, one launch (start us, length us, event | category | flops | bytes accessed | tf_op | source)
XLA Modules:
  0.0 302.2 jit_solution(9752096619383693907)
XLA Ops:
  7.3 0.8 fusion.118
  8.3 0.7 select_reduce_fusion.5
  9.1 1.3 select_reduce_fusion.1
  10.4 0.6 convolution_convert_fusion.1
  11.1 3.4 %collective-permute-start.7 = (bf16[144,4224]{1,0:T(8,128)(2,1)S(1)}, bf16[144,4224]{1,0:T(8,128)(2,1)S(1)}, u32[]{:S(2)}, u32[]{:S(2)}) collective-permute-start(bf16[144,4224]{1,0:T(8,128)(2,1)S(1)} %pad_maximum_fusion.3), channel_id=1, source_target_pairs={{0,3},{1,0},{2,1},{3,2},{4,7},{5,4},{6,5},{7,6},{8,11},{9,8},{10,9... | collective-permute-start | bytes 3649544 | tf_op jit(solution)/shard_map/ppermute | solution.py:33
  14.5 0.6 convolution_convert_fusion
  15.2 0.6 collective-permute-start.8
  15.8 0.6 convolution_convert_fusion.2
  16.6 0.7 collective-permute-start.6
  17.3 0.5 copy-done.2
  17.8 0.6 convolution_convert_fusion.4
  18.4 3.7 %collective-permute-start.2 = (bf16[144,4096]{1,0:T(8,128)(2,1)S(1)}, bf16[144,4096]{1,0:T(8,128)(2,1)}, u32[]{:S(2)}, u32[]{:S(2)}) collective-permute-start(bf16[144,4096]{1,0:T(8,128)(2,1)S(1)} %convolution_convert_fusion.4), channel_id=1, source_target_pairs={{0,8},{1,9},{2,10},{3,11},{4,12},{5,13},{6,14},{7,15},{8,0},{9,1},... | collective-permute-start | bytes 3538952 | tf_op jit(solution)/shard_map/ppermute | solution.py:33
  22.0 1.6 convolution_convert_fusion.5
  23.7 0.4 collective-permute-start.1
  24.1 0.7 fusion.174.matrix_ref
  24.8 1.6 convolution_convert_fusion.6
  26.4 14.7 %collective-permute-done.7.refs_2_ = bf16[144,4224]{1,0:T(8,128)(2,1)S(1)} collective-permute-done((bf16[144,4224]{1,0:T(8,128)(2,1)S(1)}, bf16[144,4224]{1,0:T(8,128)(2,1)S(1)}, u32[]{:S(2)}, u32[]{:S(2)}) %collective-permute-start.7) | collective-permute-done | bytes 1216544 | tf_op jit(solution)/shard_map/ppermute | solution.py:33
  41.1 1.2 collective-permute-start
  42.4 0.5 convolution_convert_fusion.3
  43.0 1.1 pad_maximum_fusion.1.refs_0_
  44.3 27.3 %collective-permute-done.6.refs_1_ = bf16[144,4224]{1,0:T(8,128)(2,1)S(1)} collective-permute-done((bf16[144,4224]{1,0:T(8,128)(2,1)S(1)}, bf16[144,4224]{1,0:T(8,128)(2,1)S(1)}, u32[]{:S(2)}, u32[]{:S(2)}) %collective-permute-start.6) | collective-permute-done | bytes 1216544 | tf_op jit(solution)/shard_map/ppermute | solution.py:33
  71.6 1.0 copy-done.8
  72.6 5.6 %swap_blocks.5 = (bf16[144,4224]{1,0:T(8,128)(2,1)}, bf16[144,4224]{1,0:T(8,128)(2,1)}, bf16[144,4224]{1,0:T(8,128)(2,1)}, bf16[144,4224]{1,0:T(8,128)(2,1)}) custom-call(bf16[64,64]{1,0:T(8,128)(2,1)} %fusion.174.matrix_ref, bf16[144,4224]{1,0:T(8,128)(2,1)} %pad_maximum_fusion.1.refs_0_, bf16[144,4224]{1,0:T(8,128)(2,1)} %copy-done.8, ...), custom_call_target="tpu_custom_call" | custom-call | flops 34603008 | bytes 9732096 | tf_op jit(solution)/shard_map/swap_blocks/pallas_call | solution.py:86
  78.2 3.9 %collective-permute-start.10 = (bf16[144,4224]{1,0:T(8,128)(2,1)}, bf16[144,4224]{1,0:T(8,128)(2,1)S(1)}, u32[]{:S(2)}, u32[]{:S(2)}) collective-permute-start(bf16[144,4224]{1,0:T(8,128)(2,1)} %get-tuple-element.47), channel_id=1, source_target_pairs={{0,12},{1,13},{2,14},{3,15},{4,0},{5,1},{6,2},{7,3},{8,4},{9,5},{1... | collective-permute-start | bytes 3649544 | tf_op jit(solution)/shard_map/ppermute | solution.py:33
  82.1 1.5 convolution_convert_fusion.7.refs_0_
  83.6 5.3 %swap_blocks.4 = (bf16[144,4096]{1,0:T(8,128)(2,1)}, bf16[144,4096]{1,0:T(8,128)(2,1)}, bf16[144,4096]{1,0:T(8,128)(2,1)}, bf16[144,4096]{1,0:T(8,128)(2,1)}) custom-call(bf16[64,64]{1,0:T(8,128)(2,1)} %fusion.174.matrix_ref, bf16[144,4096]{1,0:T(8,128)(2,1)} %convolution_convert_fusion.7.refs_0_, bf16[144,4096]{1,0:T(8,128)(2,1)} %collective-permute-done.refs_1_, ...), custom_call_target="tpu_custom_call" | custom-call | flops 33554432 | bytes 9437184 | tf_op jit(solution)/shard_map/swap_blocks/pallas_call | solution.py:86
  88.9 14.8 %collective-permute-start.4 = (bf16[144,4096]{1,0:T(8,128)(2,1)}, bf16[144,4096]{1,0:T(8,128)(2,1)S(1)}, u32[]{:S(2)}, u32[]{:S(2)}) collective-permute-start(bf16[144,4096]{1,0:T(8,128)(2,1)} %get-tuple-element.42), channel_id=1, source_target_pairs={{0,3},{1,0},{2,1},{3,2},{4,7},{5,4},{6,5},{7,6},{8,11},{9,8},{10,9... | collective-permute-start | bytes 3538952 | tf_op jit(solution)/shard_map/ppermute | solution.py:33
  103.8 4.4 %collective-permute-done.10.refs_5_.refs_2_.refs_6_.refs_10_ = bf16[144,4224]{1,0:T(8,128)(2,1)S(1)} collective-permute-done((bf16[144,4224]{1,0:T(8,128)(2,1)}, bf16[144,4224]{1,0:T(8,128)(2,1)S(1)}, u32[]{:S(2)}, u32[]{:S(2)}) %collective-permute-start.10) | collective-permute-done | bytes 1216544 | tf_op jit(solution)/shard_map/ppermute | solution.py:33
  108.2 3.0 collective-permute-done.9.refs_4_.refs_5_.refs_9_
  111.1 15.3 %collective-permute-done.3.refs_1_ = bf16[144,4096]{1,0:T(8,128)(2,1)S(1)} collective-permute-done((bf16[144,4096]{1,0:T(8,128)(2,1)}, bf16[144,4096]{1,0:T(8,128)(2,1)S(1)}, u32[]{:S(2)}, u32[]{:S(2)}) %collective-permute-start.3) | collective-permute-done | bytes 1179680 | tf_op jit(solution)/shard_map/ppermute | solution.py:33
  126.4 2.1 collective-permute-start.5
  128.5 1.1 fusion.15.matrix_ref.turn_ref
  129.6 14.3 %forward_early.1 = (f32[704,384]{1,0:T(8,128)}, f32[704,384]{1,0:T(8,128)}, f32[704,384]{1,0:T(8,128)}) custom-call(bf16[3,704,4096]{2,1,0:T(8,128)(2,1)} %bitcast.31, bf16[144,4096]{1,0:T(8,128)(2,1)} %get-tuple-element.52.refs_0_, bf16[144,4096]{1,0:T(8,128)(2,1)} %copy-done.17, bf16[144,4096]{1,0:T(8,128)(2,1)} %copy-done.9, ...), custom_call_target="tpu_custom_call" | custom-call | flops 6643777536 | bytes 23592960 | tf_op jit(solution)/shard_map/forward_early/pallas_call | solution.py:122
  143.9 8.5 %collective-permute-done.5.refs_1_.refs_3_ = bf16[144,4096]{1,0:T(8,128)(2,1)S(1)} collective-permute-done((bf16[144,4096]{1,0:T(8,128)(2,1)}, bf16[144,4096]{1,0:T(8,128)(2,1)S(1)}, u32[]{:S(2)}, u32[]{:S(2)}) %collective-permute-start.5) | collective-permute-done | bytes 1179680 | tf_op jit(solution)/shard_map/ppermute | solution.py:33
  152.3 1.0 copy-done.10
  153.7 15.9 %forward_late.1 = (bf16[704,576]{1,0:T(8,128)(2,1)}, bf16[704,576]{1,0:T(8,128)(2,1)}, bf16[704,576]{1,0:T(8,128)(2,1)}, bf16[576,128]{1,0:T(8,128)(2,1)}) custom-call(bf16[576,576]{1,0:T(8,128)(2,1)} %fusion.15.matrix_ref.turn_ref, bf16[3,704,4096]{2,1,0:T(8,128)(2,1)} %bitcast.32, bf16[144,4096]{1,0:T(8,128)(2,1)} %copy-done.9, ...), custom_call_target="tpu_custom_call" | custom-call | flops 3321888768 | bytes 20545536 | tf_op jit(solution)/shard_map/forward_late/pallas_call | solution.py:189
  169.7 19.4 %terms.1 = bf16[8,3,88,4096]{3,2,1,0:T(8,128)(2,1)} custom-call(bf16[704,576]{1,0:T(8,128)(2,1)} %get-tuple-element.57.gate_ref, bf16[704,576]{1,0:T(8,128)(2,1)} %get-tuple-element.58.up_ref, bf16[704,576]{1,0:T(8,128)(2,1)} %get-tuple-element.76.hidden_ref, bf16[144,4096]{1,0:T(8,128)(2,1)} %get-tuple-element.52.refs_0_, bf16[144,4096]{1,0:T(8,128)(2,1)} %copy-done.17, ...), custom_call_target="tpu_custom_call" | custom-call | flops 9965666304 | bytes 26738688 | tf_op jit(solution)/shard_map/terms/pallas_call | solution.py:233
  189.1 0.9 fusion.14.turn_ref
  190.0 9.7 %inputs.3 = (bf16[144,2048]{1,0:T(8,128)(2,1)}, bf16[144,2048]{1,0:T(8,128)(2,1)}, bf16[144,2048]{1,0:T(8,128)(2,1)}, bf16[144,2048]{1,0:T(8,128)(2,1)}) custom-call(bf16[576,576]{1,0:T(8,128)(2,1)} %fusion.15.matrix_ref.turn_ref, bf16[704,576]{1,0:T(8,128)(2,1)} %get-tuple-element.57.gate_ref, bf16[704,576]{1,0:T(8,128)(2,1)} %get-tuple-element.58.up_ref, ...), custom_call_target="tpu_custom_call" | custom-call | flops 3321888768 | bytes 8126464 | tf_op jit(solution)/shard_map/inputs/pallas_call | solution.py:270
  199.7 1.5 collective-permute-start.19
  201.2 9.9 %inputs.2 = (bf16[144,2176]{1,0:T(8,128)(2,1)}, bf16[144,2176]{1,0:T(8,128)(2,1)}, bf16[144,2176]{1,0:T(8,128)(2,1)}, bf16[144,2176]{1,0:T(8,128)(2,1)}) custom-call(bf16[576,576]{1,0:T(8,128)(2,1)} %fusion.14.turn_ref, bf16[704,576]{1,0:T(8,128)(2,1)} %get-tuple-element.57.gate_ref, bf16[704,576]{1,0:T(8,128)(2,1)} %get-tuple-element.58.up_ref, ...), custom_call_target="tpu_custom_call" | custom-call | flops 3321888768 | bytes 8126464 | tf_op jit(solution)/shard_map/inputs/pallas_call | solution.py:270
  211.1 1.3 collective-permute-start.12
  212.6 1.7 collective-permute-start.14
  214.3 4.4 %collective-permute-done.19.refs_2_ = bf16[144,2048]{1,0:T(8,128)(2,1)S(1)} collective-permute-done((bf16[144,2048]{1,0:T(8,128)(2,1)}, bf16[144,2048]{1,0:T(8,128)(2,1)S(1)}, u32[]{:S(2)}, u32[]{:S(2)}) %collective-permute-start.19) | collective-permute-done | bytes 589856 | tf_op jit(solution)/shard_map/ppermute | solution.py:33
  218.7 0.8 copy-done.15
  219.8 2.9 swap_blocks.7
  222.7 1.5 collective-permute-start.22
  224.1 4.9 %collective-permute-start.23 = (bf16[144,2048]{1,0:T(8,128)(2,1)}, bf16[144,2048]{1,0:T(8,128)(2,1)S(1)}, u32[]{:S(2)}, u32[]{:S(2)}) collective-permute-start(bf16[144,2048]{1,0:T(8,128)(2,1)} %get-tuple-element.75), channel_id=1, source_target_pairs={{0,2},{1,3},{2,0},{3,1},{4,6},{5,7},{6,4},{7,5},{8,10},{9,11},{10,... | collective-permute-start | bytes 1769480 | tf_op jit(solution)/shard_map/ppermute | solution.py:33
  229.4 1.0 collective-permute-done.14.refs_3_
  230.4 0.8 copy-done.13
  231.2 3.5 %swap_blocks.6 = (bf16[144,2176]{1,0:T(8,128)(2,1)}, bf16[144,2176]{1,0:T(8,128)(2,1)}, bf16[144,2176]{1,0:T(8,128)(2,1)}, bf16[144,2176]{1,0:T(8,128)(2,1)}) custom-call(bf16[64,64]{1,0:T(8,128)(2,1)} %fusion.174.matrix_ref, bf16[144,2176]{1,0:T(8,128)(2,1)} %get-tuple-element.60.refs_0_, bf16[144,2176]{1,0:T(8,128)(2,1)} %copy-done.11, ...), custom_call_target="tpu_custom_call" | custom-call | flops 17825792 | bytes 5013504 | tf_op jit(solution)/shard_map/swap_blocks/pallas_call | solution.py:86
  234.7 3.8 %collective-permute-start.15 = (bf16[144,2176]{1,0:T(8,128)(2,1)}, bf16[144,2176]{1,0:T(8,128)(2,1)S(1)}, u32[]{:S(2)}, u32[]{:S(2)}) collective-permute-start(bf16[144,2176]{1,0:T(8,128)(2,1)} %get-tuple-element.65), channel_id=1, source_target_pairs={{0,12},{1,13},{2,14},{3,15},{4,0},{5,1},{6,2},{7,3},{8,4},{9,5},{1... | collective-permute-start | bytes 1880072 | tf_op jit(solution)/shard_map/ppermute | solution.py:33
  238.5 4.6 %collective-permute-done.21 = bf16[144,2048]{1,0:T(8,128)(2,1)S(1)} collective-permute-done((bf16[144,2048]{1,0:T(8,128)(2,1)}, bf16[144,2048]{1,0:T(8,128)(2,1)S(1)}, u32[]{:S(2)}, u32[]{:S(2)}) %collective-permute-start.21) | collective-permute-done | bytes 589856 | tf_op jit(solution)/shard_map/ppermute | solution.py:33
  243.1 4.4 %collective-permute-start.17 = (bf16[144,2176]{1,0:T(8,128)(2,1)}, bf16[144,2176]{1,0:T(8,128)(2,1)S(1)}, u32[]{:S(2)}, u32[]{:S(2)}) collective-permute-start(bf16[144,2176]{1,0:T(8,128)(2,1)} %get-tuple-element.67), channel_id=1, source_target_pairs={{0,8},{1,9},{2,10},{3,11},{4,12},{5,13},{6,14},{7,15},{8,0},{9,1},... | collective-permute-start | bytes 1880072 | tf_op jit(solution)/shard_map/ppermute | solution.py:33
  247.5 1.1 slice.52
  248.7 0.9 slice_reduce_fusion.3
  249.6 5.6 %collective-permute-done.22 = bf16[144,2048]{1,0:T(8,128)(2,1)S(1)} collective-permute-done((bf16[144,2048]{1,0:T(8,128)(2,1)}, bf16[144,2048]{1,0:T(8,128)(2,1)S(1)}, u32[]{:S(2)}, u32[]{:S(2)}) %collective-permute-start.22) | collective-permute-done | bytes 589856 | tf_op jit(solution)/shard_map/ppermute | solution.py:33
  255.2 0.5 collective-permute-done.23
  255.7 1.0 convolution_convert_fusion.8
  257.4 1.2 select_reduce_fusion
  258.5 1.0 convolution_convert_fusion.9
  259.6 1.3 pad_maximum_fusion
  260.8 30.2 %reduce-scatter.2.cloned.1.call-done = bf16[1,3,88,4096]{3,2,1,0:T(8,128)(2,1)} async-done(((bf16[8,3,88,4096]{3,2,1,0:T(8,128)(2,1)}), bf16[1,3,88,4096]{3,2,1,0:T(8,128)(2,1)}) %reduce-scatter.2.cloned.1.call-update) | async-done | bytes 2162704 | tf_op jit(solution)/shard_map/reduce_scatter | solution.py:358
  291.1 4.3 %convert_bitcast_fusion = f32[1,88,3,4096]{3,1,2,0:T(8,128)} fusion(bf16[1,3,88,4096]{3,2,1,0:T(8,128)(2,1)} %reduce-scatter.2.cloned.1.call-done), kind=kLoop, calls=%fused_computation.8 | loop fusion | flops 1081344 | bytes 6488064 | tf_op jit(solution)/shard_map/transpose | solution.py:359
  (81 shorter events, 2.9 us)
Async XLA Ops:
  7.2 3.2 %copy-start = (bf16[192,4096]{1,0:T(8,128)(2,1)S(1)}, bf16[192,4096]{1,0:T(8,128)(2,1)}, u32[]{:S(2)}) copy-start(bf16[192,4096]{1,0:T(8,128)(2,1)} %param.6) | copy-start | bytes 4718596
  7.2 283.9 %reduce-scatter.2.cloned.1.call-start = ((), (), s32[]{:S(2)}) async-start(), calls=%async_computation.1 | async-start | bytes 19464192 | tf_op jit(solution)/shard_map/reduce_scatter | solution.py:358
  11.1 30.0 %collective-permute-start.7 = (bf16[144,4224]{1,0:T(8,128)(2,1)S(1)}, bf16[144,4224]{1,0:T(8,128)(2,1)S(1)}, u32[]{:S(2)}, u32[]{:S(2)}) collective-permute-start(bf16[144,4224]{1,0:T(8,128)(2,1)S(1)} %pad_maximum_fusion.3), channel_id=1, source_target_pairs={{0,3},{1,0},{2,1},{3,2},{4,7},{5,4},{6,5},{7,6},{8,11},{9,8},{10,9... | collective-permute-start | bytes 3649544 | tf_op jit(solution)/shard_map/ppermute | solution.py:33
  15.2 29.0 %collective-permute-start.8 = (bf16[144,4224]{1,0:T(8,128)(2,1)S(1)}, bf16[144,4224]{1,0:T(8,128)(2,1)S(1)}, u32[]{:S(2)}, u32[]{:S(2)}) collective-permute-start(bf16[144,4224]{1,0:T(8,128)(2,1)S(1)} %pad_maximum_fusion.4), channel_id=1, source_target_pairs={{0,2},{1,3},{2,0},{3,1},{4,6},{5,7},{6,4},{7,5},{8,10},{9,11},{10,... | collective-permute-start | bytes 3649544 | tf_op jit(solution)/shard_map/ppermute | solution.py:33
  16.4 1.4 copy-start.2
  16.6 55.0 %collective-permute-start.6 = (bf16[144,4224]{1,0:T(8,128)(2,1)S(1)}, bf16[144,4224]{1,0:T(8,128)(2,1)S(1)}, u32[]{:S(2)}, u32[]{:S(2)}) collective-permute-start(bf16[144,4224]{1,0:T(8,128)(2,1)S(1)} %pad_maximum_fusion.2), channel_id=1, source_target_pairs={{0,1},{1,2},{2,3},{3,0},{4,5},{5,6},{6,7},{7,4},{8,9},{9,10},{10,1... | collective-permute-start | bytes 3649544 | tf_op jit(solution)/shard_map/ppermute | solution.py:33
  18.4 65.2 %collective-permute-start.2 = (bf16[144,4096]{1,0:T(8,128)(2,1)S(1)}, bf16[144,4096]{1,0:T(8,128)(2,1)}, u32[]{:S(2)}, u32[]{:S(2)}) collective-permute-start(bf16[144,4096]{1,0:T(8,128)(2,1)S(1)} %convolution_convert_fusion.4), channel_id=1, source_target_pairs={{0,8},{1,9},{2,10},{3,11},{4,12},{5,13},{6,14},{7,15},{8,0},{9,1},... | collective-permute-start | bytes 3538952 | tf_op jit(solution)/shard_map/ppermute | solution.py:33
  23.7 59.9 %collective-permute-start.1 = (bf16[144,4096]{1,0:T(8,128)(2,1)}, bf16[144,4096]{1,0:T(8,128)(2,1)}, u32[]{:S(2)}, u32[]{:S(2)}) collective-permute-start(bf16[144,4096]{1,0:T(8,128)(2,1)} %convolution_convert_fusion.5), channel_id=1, source_target_pairs={{0,12},{1,13},{2,14},{3,15},{4,0},{5,1},{6,2},{7,3},{8,4},{9,5},{1... | collective-permute-start | bytes 3538952 | tf_op jit(solution)/shard_map/ppermute | solution.py:33
  41.1 2.9 copy-start.6
  41.1 42.5 %collective-permute-start = (bf16[144,4096]{1,0:T(8,128)(2,1)}, bf16[144,4096]{1,0:T(8,128)(2,1)}, u32[]{:S(2)}, u32[]{:S(2)}) collective-permute-start(bf16[144,4096]{1,0:T(8,128)(2,1)} %convolution_convert_fusion.6), channel_id=1, source_target_pairs={{0,4},{1,5},{2,6},{3,7},{4,8},{5,9},{6,10},{7,11},{8,12},{9,13},{1... | collective-permute-start | bytes 3538952 | tf_op jit(solution)/shard_map/ppermute | solution.py:33
  44.3 27.3 %copy-start.7 = (bf16[144,4224]{1,0:T(8,128)(2,1)}, bf16[144,4224]{1,0:T(8,128)(2,1)S(1)}, u32[]{:S(2)}) copy-start(bf16[144,4224]{1,0:T(8,128)(2,1)S(1)} %collective-permute-done.8.refs_3_) | copy-start | bytes 3649540
  71.6 1.0 copy-start.8
  78.2 29.9 %collective-permute-start.10 = (bf16[144,4224]{1,0:T(8,128)(2,1)}, bf16[144,4224]{1,0:T(8,128)(2,1)S(1)}, u32[]{:S(2)}, u32[]{:S(2)}) collective-permute-start(bf16[144,4224]{1,0:T(8,128)(2,1)} %get-tuple-element.47), channel_id=1, source_target_pairs={{0,12},{1,13},{2,14},{3,15},{4,0},{5,1},{6,2},{7,3},{8,4},{9,5},{1... | collective-permute-start | bytes 3649544 | tf_op jit(solution)/shard_map/ppermute | solution.py:33
  82.1 29.1 %collective-permute-start.9 = (bf16[144,4224]{1,0:T(8,128)(2,1)}, bf16[144,4224]{1,0:T(8,128)(2,1)S(1)}, u32[]{:S(2)}, u32[]{:S(2)}) collective-permute-start(bf16[144,4224]{1,0:T(8,128)(2,1)} %get-tuple-element.46), channel_id=1, source_target_pairs={{0,4},{1,5},{2,6},{3,7},{4,8},{5,9},{6,10},{7,11},{8,12},{9,13},{1... | collective-permute-start | bytes 3649544 | tf_op jit(solution)/shard_map/ppermute | solution.py:33
  88.9 37.5 %collective-permute-start.3 = (bf16[144,4096]{1,0:T(8,128)(2,1)}, bf16[144,4096]{1,0:T(8,128)(2,1)S(1)}, u32[]{:S(2)}, u32[]{:S(2)}) collective-permute-start(bf16[144,4096]{1,0:T(8,128)(2,1)} %get-tuple-element.41), channel_id=1, source_target_pairs={{0,1},{1,2},{2,3},{3,0},{4,5},{5,6},{6,7},{7,4},{8,9},{9,10},{10,1... | collective-permute-start | bytes 3538952 | tf_op jit(solution)/shard_map/ppermute | solution.py:33
  88.9 37.5 %collective-permute-start.4 = (bf16[144,4096]{1,0:T(8,128)(2,1)}, bf16[144,4096]{1,0:T(8,128)(2,1)S(1)}, u32[]{:S(2)}, u32[]{:S(2)}) collective-permute-start(bf16[144,4096]{1,0:T(8,128)(2,1)} %get-tuple-element.42), channel_id=1, source_target_pairs={{0,3},{1,0},{2,1},{3,2},{4,7},{5,4},{6,5},{7,6},{8,11},{9,8},{10,9... | collective-permute-start | bytes 3538952 | tf_op jit(solution)/shard_map/ppermute | solution.py:33
  108.2 21.4 %copy-start.3 = (bf16[144,4224]{1,0:T(8,128)(2,1)}, bf16[144,4224]{1,0:T(8,128)(2,1)S(1)}, u32[]{:S(2)}) copy-start(bf16[144,4224]{1,0:T(8,128)(2,1)S(1)} %collective-permute-done.10.refs_5_.refs_2_.refs_6_.refs_10_) | copy-start | bytes 3649540
  111.1 18.5 %copy-start.5 = (bf16[144,4224]{1,0:T(8,128)(2,1)}, bf16[144,4224]{1,0:T(8,128)(2,1)S(1)}, u32[]{:S(2)}) copy-start(bf16[144,4224]{1,0:T(8,128)(2,1)S(1)} %collective-permute-done.9.refs_4_.refs_5_.refs_9_) | copy-start | bytes 3649540
  111.1 41.2 %collective-permute-start.11 = (bf16[144,4224]{1,0:T(8,128)(2,1)}, bf16[144,4224]{1,0:T(8,128)(2,1)S(1)}, u32[]{:S(2)}, u32[]{:S(2)}) collective-permute-start(bf16[144,4224]{1,0:T(8,128)(2,1)} %get-tuple-element.49), channel_id=1, source_target_pairs={{0,8},{1,9},{2,10},{3,11},{4,12},{5,13},{6,14},{7,15},{8,0},{9,1},... | collective-permute-start | bytes 3649544 | tf_op jit(solution)/shard_map/ppermute | solution.py:33
  126.4 3.2 %copy-start.17 = (bf16[144,4096]{1,0:T(8,128)(2,1)}, bf16[144,4096]{1,0:T(8,128)(2,1)S(1)}, u32[]{:S(2)}) copy-start(bf16[144,4096]{1,0:T(8,128)(2,1)S(1)} %collective-permute-done.3.refs_1_) | copy-start | bytes 3538948
  126.4 3.2 %copy-start.9 = (bf16[144,4096]{1,0:T(8,128)(2,1)}, bf16[144,4096]{1,0:T(8,128)(2,1)S(1)}, u32[]{:S(2)}) copy-start(bf16[144,4096]{1,0:T(8,128)(2,1)S(1)} %collective-permute-done.4.refs_2_.refs_0_) | copy-start | bytes 3538948
  126.4 25.9 %collective-permute-start.5 = (bf16[144,4096]{1,0:T(8,128)(2,1)}, bf16[144,4096]{1,0:T(8,128)(2,1)S(1)}, u32[]{:S(2)}, u32[]{:S(2)}) collective-permute-start(bf16[144,4096]{1,0:T(8,128)(2,1)} %get-tuple-element.44), channel_id=1, source_target_pairs={{0,2},{1,3},{2,0},{3,1},{4,6},{5,7},{6,4},{7,5},{8,10},{9,11},{10,... | collective-permute-start | bytes 3538952 | tf_op jit(solution)/shard_map/ppermute | solution.py:33
  152.3 1.0 copy-start.10
  152.3 1.4 copy-start.4
  199.7 12.9 %collective-permute-start.18 = (bf16[144,2048]{1,0:T(8,128)(2,1)}, bf16[144,2048]{1,0:T(8,128)(2,1)S(1)}, u32[]{:S(2)}, u32[]{:S(2)}) collective-permute-start(bf16[144,2048]{1,0:T(8,128)(2,1)} %get-tuple-element.69), channel_id=1, source_target_pairs={{0,12},{1,13},{2,14},{3,15},{4,0},{5,1},{6,2},{7,3},{8,4},{9,5},{1... | collective-permute-start | bytes 1769480 | tf_op jit(solution)/shard_map/ppermute | solution.py:33
  199.7 19.0 %collective-permute-start.19 = (bf16[144,2048]{1,0:T(8,128)(2,1)}, bf16[144,2048]{1,0:T(8,128)(2,1)S(1)}, u32[]{:S(2)}, u32[]{:S(2)}) collective-permute-start(bf16[144,2048]{1,0:T(8,128)(2,1)} %get-tuple-element.70), channel_id=1, source_target_pairs={{0,4},{1,5},{2,6},{3,7},{4,8},{5,9},{6,10},{7,11},{8,12},{9,13},{1... | collective-permute-start | bytes 1769480 | tf_op jit(solution)/shard_map/ppermute | solution.py:33
  201.2 17.5 %collective-permute-start.20 = (bf16[144,2048]{1,0:T(8,128)(2,1)}, bf16[144,2048]{1,0:T(8,128)(2,1)S(1)}, u32[]{:S(2)}, u32[]{:S(2)}) collective-permute-start(bf16[144,2048]{1,0:T(8,128)(2,1)} %get-tuple-element.71), channel_id=1, source_target_pairs={{0,8},{1,9},{2,10},{3,11},{4,12},{5,13},{6,14},{7,15},{8,0},{9,1},... | collective-permute-start | bytes 1769480 | tf_op jit(solution)/shard_map/ppermute | solution.py:33
  211.1 13.0 %collective-permute-start.12 = (bf16[144,2176]{1,0:T(8,128)(2,1)}, bf16[144,2176]{1,0:T(8,128)(2,1)S(1)}, u32[]{:S(2)}, u32[]{:S(2)}) collective-permute-start(bf16[144,2176]{1,0:T(8,128)(2,1)} %get-tuple-element.61), channel_id=1, source_target_pairs={{0,3},{1,0},{2,1},{3,2},{4,7},{5,4},{6,5},{7,6},{8,11},{9,8},{10,9... | collective-permute-start | bytes 1880072 | tf_op jit(solution)/shard_map/ppermute | solution.py:33
  212.4 17.0 %collective-permute-start.13 = (bf16[144,2176]{1,0:T(8,128)(2,1)}, bf16[144,2176]{1,0:T(8,128)(2,1)S(1)}, u32[]{:S(2)}, u32[]{:S(2)}) collective-permute-start(bf16[144,2176]{1,0:T(8,128)(2,1)} %get-tuple-element.62), channel_id=1, source_target_pairs={{0,1},{1,2},{2,3},{3,0},{4,5},{5,6},{6,7},{7,4},{8,9},{9,10},{10,1... | collective-permute-start | bytes 1880072 | tf_op jit(solution)/shard_map/ppermute | solution.py:33
  212.6 6.1 %copy-start.14 = (bf16[144,2048]{1,0:T(8,128)(2,1)}, bf16[144,2048]{1,0:T(8,128)(2,1)S(1)}, u32[]{:S(2)}) copy-start(bf16[144,2048]{1,0:T(8,128)(2,1)S(1)} %collective-permute-done.18.refs_1_) | copy-start | bytes 1769476
  212.6 17.7 %collective-permute-start.14 = (bf16[144,2176]{1,0:T(8,128)(2,1)}, bf16[144,2176]{1,0:T(8,128)(2,1)S(1)}, u32[]{:S(2)}, u32[]{:S(2)}) collective-permute-start(bf16[144,2176]{1,0:T(8,128)(2,1)} %get-tuple-element.63), channel_id=1, source_target_pairs={{0,2},{1,3},{2,0},{3,1},{4,6},{5,7},{6,4},{7,5},{8,10},{9,11},{10,... | collective-permute-start | bytes 1880072 | tf_op jit(solution)/shard_map/ppermute | solution.py:33
  218.7 0.8 copy-start.15
  218.7 1.0 copy-start.16
  222.7 20.4 %collective-permute-start.21 = (bf16[144,2048]{1,0:T(8,128)(2,1)}, bf16[144,2048]{1,0:T(8,128)(2,1)S(1)}, u32[]{:S(2)}, u32[]{:S(2)}) collective-permute-start(bf16[144,2048]{1,0:T(8,128)(2,1)} %get-tuple-element.73), channel_id=1, source_target_pairs={{0,3},{1,0},{2,1},{3,2},{4,7},{5,4},{6,5},{7,6},{8,11},{9,8},{10,9... | collective-permute-start | bytes 1769480 | tf_op jit(solution)/shard_map/ppermute | solution.py:33
  222.7 32.5 %collective-permute-start.22 = (bf16[144,2048]{1,0:T(8,128)(2,1)}, bf16[144,2048]{1,0:T(8,128)(2,1)S(1)}, u32[]{:S(2)}, u32[]{:S(2)}) collective-permute-start(bf16[144,2048]{1,0:T(8,128)(2,1)} %get-tuple-element.74), channel_id=1, source_target_pairs={{0,1},{1,2},{2,3},{3,0},{4,5},{5,6},{6,7},{7,4},{8,9},{9,10},{10,1... | collective-permute-start | bytes 1769480 | tf_op jit(solution)/shard_map/ppermute | solution.py:33
  224.1 6.2 %copy-start.11 = (bf16[144,2176]{1,0:T(8,128)(2,1)}, bf16[144,2176]{1,0:T(8,128)(2,1)S(1)}, u32[]{:S(2)}) copy-start(bf16[144,2176]{1,0:T(8,128)(2,1)S(1)} %collective-permute-done.12.refs_1_) | copy-start | bytes 1880068
  224.1 31.5 %collective-permute-start.23 = (bf16[144,2048]{1,0:T(8,128)(2,1)}, bf16[144,2048]{1,0:T(8,128)(2,1)S(1)}, u32[]{:S(2)}, u32[]{:S(2)}) collective-permute-start(bf16[144,2048]{1,0:T(8,128)(2,1)} %get-tuple-element.75), channel_id=1, source_target_pairs={{0,2},{1,3},{2,0},{3,1},{4,6},{5,7},{6,4},{7,5},{8,10},{9,11},{10,... | collective-permute-start | bytes 1769480 | tf_op jit(solution)/shard_map/ppermute | solution.py:33
  229.4 1.0 copy-start.12
  230.3 0.8 copy-start.13
  231.2 24.5 %copy-start.18 = (bf16[144,2048]{1,0:T(8,128)(2,1)S(1)}, bf16[144,2048]{1,0:T(8,128)(2,1)}, u32[]{:S(2)}) copy-start(bf16[144,2048]{1,0:T(8,128)(2,1)} %get-tuple-element.72) | copy-start | bytes 1769476
  234.7 22.0 %collective-permute-start.15 = (bf16[144,2176]{1,0:T(8,128)(2,1)}, bf16[144,2176]{1,0:T(8,128)(2,1)S(1)}, u32[]{:S(2)}, u32[]{:S(2)}) collective-permute-start(bf16[144,2176]{1,0:T(8,128)(2,1)} %get-tuple-element.65), channel_id=1, source_target_pairs={{0,12},{1,13},{2,14},{3,15},{4,0},{5,1},{6,2},{7,3},{8,4},{9,5},{1... | collective-permute-start | bytes 1880072 | tf_op jit(solution)/shard_map/ppermute | solution.py:33
  238.5 18.3 %collective-permute-start.16 = (bf16[144,2176]{1,0:T(8,128)(2,1)}, bf16[144,2176]{1,0:T(8,128)(2,1)S(1)}, u32[]{:S(2)}, u32[]{:S(2)}) collective-permute-start(bf16[144,2176]{1,0:T(8,128)(2,1)} %get-tuple-element.66), channel_id=1, source_target_pairs={{0,4},{1,5},{2,6},{3,7},{4,8},{5,9},{6,10},{7,11},{8,12},{9,13},{1... | collective-permute-start | bytes 1880072 | tf_op jit(solution)/shard_map/ppermute | solution.py:33
  243.1 13.7 %collective-permute-start.17 = (bf16[144,2176]{1,0:T(8,128)(2,1)}, bf16[144,2176]{1,0:T(8,128)(2,1)S(1)}, u32[]{:S(2)}, u32[]{:S(2)}) collective-permute-start(bf16[144,2176]{1,0:T(8,128)(2,1)} %get-tuple-element.67), channel_id=1, source_target_pairs={{0,8},{1,9},{2,10},{3,11},{4,12},{5,13},{6,14},{7,15},{8,0},{9,1},... | collective-permute-start | bytes 1880072 | tf_op jit(solution)/shard_map/ppermute | solution.py:33
  291.1 4.3 %copy-start.1 = (bf16[192,4096]{1,0:T(8,128)(2,1)S(1)}, bf16[192,4096]{1,0:T(8,128)(2,1)}, u32[]{:S(2)}) copy-start(bf16[192,4096]{1,0:T(8,128)(2,1)} %param.6) | copy-start | bytes 4718596
Sparse Core Ops, SparseCore 0:
  189.2 101.8 reduce-scatter.1

commit v2 on v1

--- a/solution.py
+++ b/solution.py
@@ -68,38 +68,69 @@
     return pl.CostEstimate(flops=int(flops), bytes_accessed=int(moved), transcendentals=0)
 
 
-def swap_kernel(matrix_ref, *refs):
-    ins, outs = refs[:SIDE], refs[SIDE:]
-    for p in range(SIDE):
+def swap_near_kernel(*refs):
+    ins, outs = refs[: SIDE - 1], refs[SIDE - 1 :]
+    for p in range(SIDE - 1):
         for q in range(SIDE):
             outs[q][p * MAIN : (p + 1) * MAIN] = ins[p][q * MAIN : (q + 1) * MAIN]
-    tails = jnp.concatenate([ref[SIDE * MAIN :] for ref in ins], axis=0)
+
+
+def swap_far_kernel(matrix_ref, far_ref, *refs):
+    near_tails, outs = refs[: SIDE - 1], refs[-SIDE:]
+    far = far_ref[...]
+    tails = jnp.concatenate([ref[...] for ref in near_tails] + [far[SIDE * MAIN :]], axis=0)
     tails = product(matrix_ref[...], tails).astype(jnp.bfloat16)
     for q in range(SIDE):
-        outs[q][SIDE * MAIN :] = tails[q * SIDE * TAIL : (q + 1) * SIDE * TAIL]
+        outs[q][:MAIN] = far[q * MAIN : (q + 1) * MAIN]
+        outs[q][MAIN:] = tails[q * SIDE * TAIL : (q + 1) * SIDE * TAIL]
 
 
 def swap_blocks(matrix, blocks):
     width = blocks[0].shape[1]
-    tile = 1024 if width % 1024 == 0 else 1408 if width % 1408 == 0 else width
-    spec = pl.BlockSpec((BLOCK, tile), lambda i: (0, i))
+    tile = width // 2 if width % 4096 == 0 else width
+    grid = (width // tile,)
+    shapes = [jax.ShapeDtypeStruct((BLOCK, width), jnp.bfloat16)] * SIDE
+    last = SIDE - 1
+    placed = pl.pallas_call(
+        swap_near_kernel,
+        grid=grid,
+        in_specs=[pl.BlockSpec((SIDE * MAIN, tile), lambda i: (0, i))] * last,
+        out_specs=[pl.BlockSpec((last * MAIN, tile), lambda i: (0, i))] * SIDE,
+        out_shape=shapes,
+        compiler_params=params(),
+        cost_estimate=cost(0, 3 * ROWS * width),
+        name="swap_near",
+    )(*blocks[:last])
+    left = BLOCK - last * MAIN
+    tail = SIDE * TAIL
     return pl.pallas_call(
-        swap_kernel,
-        grid=(width // tile,),
-        in_specs=[pl.BlockSpec(matrix.shape, lambda i: (0, 0))] + [spec] * SIDE,
-        out_specs=[spec] * SIDE,
-        out_shape=[jax.ShapeDtypeStruct((BLOCK, width), jnp.bfloat16)] * SIDE,
-        compiler_params=params(),
-        cost_estimate=cost(2 * 64 * 64 * width, 4 * ROWS * width),
-        name="swap_blocks",
-    )(matrix, *blocks)
+        swap_far_kernel,
+        grid=grid,
+        in_specs=[
+            pl.BlockSpec(matrix.shape, lambda i: (0, 0)),
+            pl.BlockSpec((BLOCK, tile), lambda i: (0, i)),
+        ]
+        + [pl.BlockSpec((tail, tile), lambda i: (BLOCK // tail - 1, i))] * last
+        + [pl.BlockSpec(memory_space=pl.ANY)] * SIDE,
+        out_specs=[pl.BlockSpec((left, tile), lambda i: (BLOCK // left - 1, i))] * SIDE,
+        out_shape=shapes,
+        input_output_aliases={2 + last + q: q for q in range(SIDE)},
+        compiler_params=params(),
+        cost_estimate=cost(2 * 64 * 64 * width, ROWS * width),
+        name="swap_far",
+    )(matrix, blocks[last], *blocks[:last], *placed)
 
 
 LAST = ((1,), (1,))
 
 
+def two(weight_ref):
+    units, columns = weight_ref.shape[1:]
+    return weight_ref[:2].reshape(2 * units, columns)
+
+
 def early_kernel(weight_ref, *refs):
-    toks, cots, outs = refs[0:3], refs[3:6], refs[6:9]
+    toks, cots, outs = refs[0:3], refs[3:6], refs[6:8]
 
     @pl.when(pl.program_id(0) == 0)
     def _():
@@ -110,21 +141,22 @@
         jnp.concatenate([r[0][...], r[1][...], r[2][: EARLY - 2 * BLOCK]], axis=0)
         for r in (toks, cots)
     )
-    for kind, right in enumerate((tok, tok, cot)):
-        outs[kind][...] += product(weight_ref[kind], right, LAST)
+    both_out, back_out = outs
+    both_out[...] += product(two(weight_ref), tok, LAST)
+    back_out[...] += product(weight_ref[2], cot, LAST)
 
 
 def forward_early(weights, toks, cots):
     units, width = weights.shape[1:]
     tile = 1024
     rows = pl.BlockSpec((BLOCK, tile), lambda i: (0, i))
-    whole = pl.BlockSpec((units, EARLY), lambda i: (0, 0))
+    shapes = [(2 * units, EARLY), (units, EARLY)]
     return pl.pallas_call(
         early_kernel,
         grid=(width // tile,),
         in_specs=[pl.BlockSpec((3, units, tile), lambda i: (0, 0, i))] + [rows] * 6,
-        out_specs=[whole] * 3,
-        out_shape=[jax.ShapeDtypeStruct((units, EARLY), jnp.float32)] * 3,
+        out_specs=[pl.BlockSpec(shape, lambda i: (0, 0)) for shape in shapes],
+        out_shape=[jax.ShapeDtypeStruct(shape, jnp.float32) for shape in shapes],
         compiler_params=params(),
         cost_estimate=cost(6 * EARLY * units * width, 6 * units * width + 4 * EARLY * width),
         name="forward_early",
@@ -133,9 +165,9 @@
 
 def late_kernel(steps, matrix_ref, weight_ref, *refs):
     toks, cots, scales = refs[0:2], refs[2:4], refs[4:8]
-    early = refs[8:11]
-    gate_out, up_out, hidden_out, route_out = refs[11:15]
-    accs = refs[15:18]
+    early = refs[8:10]
+    deltas_out, hidden_out, route_out = refs[10:13]
+    accs = refs[13:15]
     step = pl.program_id(0)
 
     @pl.when(step == 0)
@@ -146,15 +178,17 @@
     tok, cot = (
         jnp.concatenate([r[0][EARLY - 2 * BLOCK :], r[1][...]], axis=0) for r in (toks, cots)
     )
-    for kind, right in enumerate((tok, tok, cot)):
-        accs[kind][...] += product(weight_ref[kind], right, LAST)
+    accs[0][...] += product(two(weight_ref), tok, LAST)
+    accs[1][...] += product(weight_ref[2], cot, LAST)
 
     @pl.when(step == steps - 1)
     def _():
         matrix = matrix_ref[...]
-        gate_pre, up_pre, back = (
+        both, back = (
             jnp.concatenate([first[...], acc[...]], axis=1) for first, acc in zip(early, accs)
         )
+        units = back.shape[0]
+        gate_pre, up_pre = both[:units], both[units:]
         lane = lax.broadcasted_iota(jnp.int32, (8, EXTRA), 1)
         first_lane = jnp.where(lane == 0, 1.0, 0.0).astype(jnp.bfloat16)
         scale = jnp.concatenate([ref[...] for ref in scales], axis=0)
@@ -162,15 +196,17 @@
         grad = scale * back
         high = grad.astype(jnp.bfloat16)
         low = (grad - high.astype(jnp.float32)).astype(jnp.bfloat16)
-        grad = product(high, matrix) + product(low, matrix)
         logistic = 1.0 / (1.0 + jnp.exp(-gate_pre))
         gated = gate_pre * logistic
-        hidden = product((gated * up_pre).astype(jnp.bfloat16), matrix)
+        hidden = (gated * up_pre).astype(jnp.bfloat16)
+        turned = product(jnp.concatenate([high, low, hidden], axis=0), matrix)
+        grad = turned[:units] + turned[units : 2 * units]
+        hidden = turned[2 * units :]
         hidden_out[...] = hidden.astype(jnp.bfloat16)
-        gate_out[...] = (grad * up_pre * logistic * (1.0 + gate_pre * (1.0 - logistic))).astype(
-            jnp.bfloat16
-        )
-        up_out[...] = (grad * gated).astype(jnp.bfloat16)
+        deltas_out[:units] = (
+            grad * up_pre * logistic * (1.0 + gate_pre * (1.0 - logistic))
+        ).astype(jnp.bfloat16)
+        deltas_out[units:] = (grad * gated).astype(jnp.bfloat16)
         route = jnp.sum(hidden * back, axis=0, keepdims=True).astype(jnp.bfloat16)
         route_out[...] = product(matrix, jnp.broadcast_to(route, (EXTRA, ROWS)), LAST).astype(
             jnp.bfloat16
@@ -183,8 +219,7 @@
     steps = width // tile
     rows = pl.BlockSpec((BLOCK, tile), lambda i: (0, i))
     extra = pl.BlockSpec((BLOCK, EXTRA), lambda i: (0, width // EXTRA))
-    whole = pl.BlockSpec((units, ROWS), lambda i: (0, 0))
-    small = jax.ShapeDtypeStruct((units, ROWS), jnp.bfloat16)
+    shapes = [(2 * units, ROWS), (units, ROWS), (ROWS, EXTRA)]
     late = ROWS - EARLY
     return pl.pallas_call(
         functools.partial(late_kernel, steps),
@@ -195,17 +230,17 @@
         ]
         + [rows] * 4
         + [extra] * 4
-        + [pl.BlockSpec((units, EARLY), lambda i: (0, 0))] * 3,
-        out_specs=[whole] * 3 + [pl.BlockSpec((ROWS, EXTRA), lambda i: (0, 0))],
-        out_shape=[small] * 3 + [jax.ShapeDtypeStruct((ROWS, EXTRA), jnp.bfloat16)],
-        scratch_shapes=[pltpu.VMEM((units, late), jnp.float32)] * 3,
+        + [pl.BlockSpec(array.shape, lambda i: (0, 0)) for array in early],
+        out_specs=[pl.BlockSpec(shape, lambda i: (0, 0)) for shape in shapes],
+        out_shape=[jax.ShapeDtypeStruct(shape, jnp.bfloat16) for shape in shapes],
+        scratch_shapes=[pltpu.VMEM((n * units, late), jnp.float32) for n in (2, 1)],
         compiler_params=params(),
         cost_estimate=cost(6 * late * units * width, 6 * units * width + 12 * EARLY * units),
         name="forward_late",
     )(matrix, weights, *toks[2:], *cots[2:], *cots, *early)
 
 
-def terms_kernel(gate_ref, up_ref, hidden_ref, *refs):
+def terms_kernel(deltas_ref, hidden_ref, *refs):
     toks, cots, scales, out_ref = refs[0:4], refs[4:8], refs[8:12], refs[12]
     tok = jnp.concatenate([ref[...] for ref in toks], axis=0)
     scaled = jnp.concatenate(
@@ -216,74 +251,76 @@
         axis=0,
     )
     share = out_ref.shape[2]
-    for kind, (left, right) in enumerate(((gate_ref, tok), (up_ref, tok), (hidden_ref, scaled))):
+    units = hidden_ref.shape[0]
+    kind = 0
+    for left, right in ((deltas_ref, tok), (hidden_ref, scaled)):
         term = product(left[...], right)
-        for owner in range(out_ref.shape[0]):
-            out_ref[owner, kind] = term[owner * share : (owner + 1) * share].astype(jnp.bfloat16)
-
-
-def terms(gate_delta, up_delta, hidden, toks, cots, owners):
-    units = gate_delta.shape[0]
+        for first in range(0, left.shape[0], units):
+            for owner in range(units // share):
+                rows = term[first + owner * share : first + (owner + 1) * share]
+                out_ref[owner, kind] = rows.astype(jnp.bfloat16)
+            kind += 1
+
+
+def terms(deltas, hidden, toks, cots, owners):
+    units = hidden.shape[0]
     width = toks[0].shape[1]
-    tile = 512
+    tile = 1024
     rows = pl.BlockSpec((BLOCK, tile), lambda i: (0, i))
     extra = pl.BlockSpec((BLOCK, EXTRA), lambda i: (0, width // EXTRA))
-    whole = pl.BlockSpec((units, ROWS), lambda i: (0, 0))
     share = units // owners
     return pl.pallas_call(
         terms_kernel,
         grid=(width // tile,),
-        in_specs=[whole] * 3 + [rows] * 8 + [extra] * 4,
+        in_specs=[pl.BlockSpec(array.shape, lambda i: (0, 0)) for array in (deltas, hidden)]
+        + [rows] * 8
+        + [extra] * 4,
         out_specs=pl.BlockSpec((owners, 3, share, tile), lambda i: (0, 0, 0, i)),
         out_shape=jax.ShapeDtypeStruct((owners, 3, share, width), jnp.bfloat16),
         compiler_params=params(),
         cost_estimate=cost(6 * ROWS * units * width, 6 * units * width + 4 * ROWS * width),
         name="terms",
-    )(gate_delta, up_delta, hidden, *toks, *cots, *cots)
-
-
-def inputs_kernel(tile, turn_ref, gate_ref, up_ref, weight_ref, route_ref, *refs):
-    outs, (gate_rows, up_rows) = refs[:SIDE], refs[SIDE:]
+    )(deltas, hidden, *toks, *cots, *cots)
+
+
+def inputs_kernel(tile, turn_ref, deltas_ref, weight_ref, route_ref, *refs):
+    outs, delta_rows = refs[:SIDE], refs[SIDE]
     step = pl.program_id(0)
 
     @pl.when(step == 0)
     def _():
-        gate_rows[...] = product(turn_ref[...], gate_ref[...], LAST).astype(jnp.bfloat16)
-        up_rows[...] = product(turn_ref[...], up_ref[...], LAST).astype(jnp.bfloat16)
+        delta_rows[...] = product(turn_ref[...], deltas_ref[...], LAST).astype(jnp.bfloat16)
         for p in range(SIDE):
             width = outs[p].shape[1]
             if width % tile:
                 outs[p][:, width - EXTRA :] = route_ref[p * BLOCK : (p + 1) * BLOCK]
 
-    value = product(gate_rows[...], weight_ref[0]) + product(up_rows[...], weight_ref[1])
-    value = value.astype(jnp.bfloat16)
+    value = product(delta_rows[...], two(weight_ref)).astype(jnp.bfloat16)
     columns = pl.ds(pl.multiple_of(step * tile, tile), tile)
     for p in range(SIDE):
         outs[p][:, columns] = value[p * BLOCK : (p + 1) * BLOCK]
 
 
-def inputs(turn, gate_delta, up_delta, weights, route, first, count, extra):
+def inputs(turn, deltas, weights, route, first, count, extra):
     units = weights.shape[1]
     tile = 512
-    whole = pl.BlockSpec((units, ROWS), lambda i: (0, 0))
     block = (BLOCK, count + extra)
     return pl.pallas_call(
         functools.partial(inputs_kernel, tile),
         grid=(count // tile,),
         in_specs=[
             pl.BlockSpec((ROWS, ROWS), lambda i: (0, 0)),
-            whole,
-            whole,
+            pl.BlockSpec((2 * units, ROWS), lambda i: (0, 0)),
             pl.BlockSpec((2, units, tile), lambda i: (0, 0, first // tile + i)),
             pl.BlockSpec((ROWS, EXTRA), lambda i: (0, 0)),
         ],
         out_specs=[pl.BlockSpec(block, lambda i: (0, 0))] * SIDE,
         out_shape=[jax.ShapeDtypeStruct(block, jnp.bfloat16)] * SIDE,
-        scratch_shapes=[pltpu.VMEM((ROWS, units), jnp.bfloat16)] * 2,
+        scratch_shapes=[pltpu.VMEM((ROWS, 2 * units), jnp.bfloat16)],
         compiler_params=params(),
         cost_estimate=cost(4 * ROWS * units * count, 4 * units * count + 2 * ROWS * count),
         name="inputs",
-    )(turn, gate_delta, up_delta, weights, route)
+    )(turn, deltas, weights, route)
 
 
 def shards(tokens, cotangent, expert_ids, route_weights, expert_weights):
@@ -348,18 +385,18 @@
         far = lax.optimization_barrier((blocks[3], near[1], near[2]))
         return [near[0], far[1], far[2], move(far[0], axis, HOPS[3])]
 
-    toks = near_then_far(swap_blocks(small_turn, spread(tok_blocks, "z", 1)), "x")
-    cots = near_then_far(swap_blocks(small_turn, spread(cot_blocks, "x", 1)), "z")
+    toks = near_then_far(swap_blocks(small_turn, near_then_far(tok_blocks, "z")), "x")
+    cots = near_then_far(swap_blocks(small_turn, near_then_far(cot_blocks, "x")), "z")
 
     weights = expert_weights[0].transpose(1, 0, 2)
     early = forward_early(weights, toks[:3], cots[:3])
-    gate_delta, up_delta, hidden, route = forward_late(turn, weights, toks, cots, early)
-    partial_sums = terms(gate_delta, up_delta, hidden, toks, cots, owners)
+    deltas, hidden, route = forward_late(turn, weights, toks, cots, early)
+    partial_sums = terms(deltas, hidden, toks, cots, owners)
     summed = lax.psum_scatter(partial_sums, "dp", scatter_dimension=0, tiled=True)
     weight_grad = summed.astype(jnp.float32).transpose(0, 2, 1, 3)
 
-    right = inputs(turn, gate_delta, up_delta, weights, route, half, half, 0)
-    left = inputs(same, gate_delta, up_delta, weights, route, 0, half, EXTRA)
+    right = inputs(turn, deltas, weights, route, half, half, 0)
+    left = inputs(same, deltas, weights, route, 0, half, EXTRA)
     left = spread(swap_blocks(small_turn, spread(left, "x", -1)), "z", -1)
     right = spread(swap_blocks(small_turn, spread(right, "z", -1)), "x", -1)
 

time: 303 us -> 283 us (0.934)
  starting transfers between devices: 50.1 us -> 33.8 us
  waiting for transfers between devices: 120 us -> 111 us
  Pallas kernels: 86.5 us -> 90.2 us
    reduce_scatter x1, waiting for transfers between devices: 30.2 us -> 13.8 us  [shards(): lax.psum_scatter(partial_sums, 'dp', scatter_dimension=0, tiled=True)]
    ppermute x24, starting transfers between devices: 50 us -> 33.7 us  [move(): lax.ppermute(value, 'expert', hop(step, 0) if axis == 'z' else hop(0, step))]
    ppermute x24, waiting for transfers between devices: 89.8 us -> 97 us  [move(): lax.ppermute(value, 'expert', hop(step, 0) if axis == 'z' else hop(0, step))]
    pallas_call x5 -> x9, Pallas kernels: 36.7 us -> 41 us  [the longest x1 19 us: terms(): pl.pallas_call(terms_kernel, grid=(width // tile,), in_specs=[pl.BlockSpe...]
    unnamed x38 -> x46, local copies, waits for them, and re-layouts: 4.9 us -> 7.87 us
  transfers between devices with their start and end apart: 25 -> 25, of which waited for: 14 -> 15; matrix products, arithmetic and copies ran while one was open for 6% -> 6% of each run, Pallas kernels for 17% -> 20%
where the time goes in v2:
time: 283 us; the launch traced here: 282 us
  waiting for transfers between devices  111 us (39%)
  Pallas kernels  90.2 us (32%)
  starting transfers between devices  33.8 us (12%)
  between operations  14.4 us (5%)
  other arithmetic  13.8 us (5%)
  local copies, waits for them, and re-layouts  10.7 us (4%)
  matrix products  8.63 us (3%)
    ppermute x24, waiting for transfers between devices, move(): lax.ppermute(value, 'expert', hop(step, 0) if axis == 'z' else hop(0, step))  97 us
    ppermute x24, starting transfers between devices, move(): lax.ppermute(value, 'expert', hop(step, 0) if axis == 'z' else hop(0, step))  33.7 us
    pallas_call x2, Pallas kernels, inputs(): pl.pallas_call(functools.partial(inputs_kernel, tile), grid=(count // til...  19.5 us
    pallas_call x1, Pallas kernels, terms(): pl.pallas_call(terms_kernel, grid=(width // tile,), in_specs=[pl.BlockSpe...  19 us
    pallas_call x1, Pallas kernels, forward_late(): pl.pallas_call(functools.partial(late_kernel, steps), grid=(steps,), in_s...  15.7 us
    pallas_call x1, Pallas kernels, forward_early(): pl.pallas_call(early_kernel, grid=(width // tile,), in_specs=[pl.BlockSpe...  14 us
    reduce_scatter x1, waiting for transfers between devices, shards(): lax.psum_scatter(partial_sums, 'dp', scatter_dimension=0, tiled=True)  13.8 us
    pallas_call x4, Pallas kernels, swap_blocks(): pl.pallas_call(swap_near_kernel, grid=grid, in_specs=[pl.BlockSpec((SIDE...  12 us
  transfers between devices with their start and end apart: 25, of which 15 were waited for; matrix products, arithmetic and copies ran while one was open for 6% of the time, Pallas kernels for 20%

profile of v2, /device:TPU:1, one launch (start us, length us, event | category | flops | bytes accessed | tf_op | source)
XLA Modules:
  0.0 282.3 jit_solution(2195182836799938397)
XLA Ops:
  7.3 0.8 fusion.118
  9.1 1.2 select_reduce_fusion.1
  11.1 2.1 collective-permute-start.6
  13.9 1.4 collective-permute-start.7
  15.9 4.0 %collective-permute-start.1 = (bf16[144,4096]{1,0:T(8,128)(2,1)S(1)}, bf16[144,4096]{1,0:T(8,128)(2,1)S(1)}, u32[]{:S(2)}, u32[]{:S(2)}) collective-permute-start(bf16[144,4096]{1,0:T(8,128)(2,1)S(1)} %convolution_convert_fusion.5), channel_id=1, source_target_pairs={{0,12},{1,13},{2,14},{3,15},{4,0},{5,1},{6,2},{7,3},{8,4},{9,5},{1... | collective-permute-start | bytes 3538952 | tf_op jit(solution)/shard_map/ppermute | solution.py:33
  21.3 19.2 %collective-permute-done.6.refs_1_ = bf16[144,4224]{1,0:T(8,128)(2,1)S(1)} collective-permute-done((bf16[144,4224]{1,0:T(8,128)(2,1)S(1)}, bf16[144,4224]{1,0:T(8,128)(2,1)S(1)}, u32[]{:S(2)}, u32[]{:S(2)}) %collective-permute-start.6) | collective-permute-done | bytes 1216544 | tf_op jit(solution)/shard_map/ppermute | solution.py:33
  40.5 0.8 collective-permute-done.7.refs_2_
  41.3 2.4 collective-permute-start.8
  44.4 1.6 convolution_convert_fusion.7
  46.1 1.6 collective-permute-done.refs_1_
  47.6 2.1 collective-permute-start.2
  50.4 1.1 pad_maximum_fusion.4.refs_0_
  51.5 3.6 %swap_near.5 = (bf16[144,4224]{1,0:T(8,128)(2,1)}, bf16[144,4224]{1,0:T(8,128)(2,1)}, bf16[144,4224]{1,0:T(8,128)(2,1)}, bf16[144,4224]{1,0:T(8,128)(2,1)}) custom-call(bf16[144,4224]{1,0:T(8,128)(2,1)} %pad_maximum_fusion.4.refs_0_, bf16[144,4224]{1,0:T(8,128)(2,1)} %copy-done.5, bf16[144,4224]{1,0:T(8,128)(2,1)} %copy-done.6), custom_call_target="tpu_custom_call" | custom-call | bytes 7299072 | tf_op jit(solution)/shard_map/swap_near/pallas_call | solution.py:94
  55.1 14.1 %collective-permute-done.8.far_ref = bf16[144,4224]{1,0:T(8,128)(2,1)S(1)} collective-permute-done((bf16[144,4224]{1,0:T(8,128)(2,1)S(1)}, bf16[144,4224]{1,0:T(8,128)(2,1)S(1)}, u32[]{:S(2)}, u32[]{:S(2)}) %collective-permute-start.8) | collective-permute-done | bytes 1216544 | tf_op jit(solution)/shard_map/ppermute | solution.py:33
  69.2 1.0 copy-done.14
  70.2 2.9 %swap_far.5 = (bf16[144,4224]{1,0:T(8,128)(2,1)}, bf16[144,4224]{1,0:T(8,128)(2,1)}, bf16[144,4224]{1,0:T(8,128)(2,1)}, bf16[144,4224]{1,0:T(8,128)(2,1)}) custom-call(bf16[64,64]{1,0:T(8,128)(2,1)} %fusion.174.matrix_ref, bf16[144,4224]{1,0:T(8,128)(2,1)} %copy-done.14, ...), custom_call_target="tpu_custom_call", output_to_operand_aliasing={{0}: (5, {}), {1}: (6, {}), {2}: (7, {}), {3}: (8, {})} | custom-call | flops 34603008 | bytes 2433024 | tf_op jit(solution)/shard_map/swap_far/pallas_call | solution.py:106
  73.1 3.8 %collective-permute-start.10 = (bf16[144,4224]{1,0:T(8,128)(2,1)}, bf16[144,4224]{1,0:T(8,128)(2,1)S(1)}, u32[]{:S(2)}, u32[]{:S(2)}) collective-permute-start(bf16[144,4224]{1,0:T(8,128)(2,1)} %get-tuple-element.81), channel_id=1, source_target_pairs={{0,12},{1,13},{2,14},{3,15},{4,0},{5,1},{6,2},{7,3},{8,4},{9,5},{1... | collective-permute-start | bytes 3649544 | tf_op jit(solution)/shard_map/ppermute | solution.py:33
  76.9 1.5 convolution_convert_fusion.4.refs_0_
  78.4 3.1 %swap_near.4 = (bf16[144,4096]{1,0:T(8,128)(2,1)}, bf16[144,4096]{1,0:T(8,128)(2,1)}, bf16[144,4096]{1,0:T(8,128)(2,1)}, bf16[144,4096]{1,0:T(8,128)(2,1)}) custom-call(bf16[144,4096]{1,0:T(8,128)(2,1)} %convolution_convert_fusion.4.refs_0_, bf16[144,4096]{1,0:T(8,128)(2,1)} %copy-done.8, bf16[144,4096]{1,0:T(8,128)(2,1)} %copy-done.7), custom_call_target="tpu_custom_call" | custom-call | bytes 7077888 | tf_op jit(solution)/shard_map/swap_near/pallas_call | solution.py:94
  81.5 1.0 copy-done.16
  82.5 2.6 swap_far.4
  85.1 1.2 collective-permute-start.3
  86.4 1.5 collective-permute-start.4
  87.9 13.3 %collective-permute-done.10.refs_5_.refs_2_.refs_6_.refs_10_ = bf16[144,4224]{1,0:T(8,128)(2,1)S(1)} collective-permute-done((bf16[144,4224]{1,0:T(8,128)(2,1)}, bf16[144,4224]{1,0:T(8,128)(2,1)S(1)}, u32[]{:S(2)}, u32[]{:S(2)}) %collective-permute-start.10) | collective-permute-done | bytes 1216544 | tf_op jit(solution)/shard_map/ppermute | solution.py:33
  101.2 2.3 collective-permute-done.9.refs_4_.refs_5_.refs_9_
  103.5 7.5 %collective-permute-done.3.refs_1_ = bf16[144,4096]{1,0:T(8,128)(2,1)S(1)} collective-permute-done((bf16[144,4096]{1,0:T(8,128)(2,1)}, bf16[144,4096]{1,0:T(8,128)(2,1)S(1)}, u32[]{:S(2)}, u32[]{:S(2)}) %collective-permute-start.3) | collective-permute-done | bytes 1179680 | tf_op jit(solution)/shard_map/ppermute | solution.py:33
  111.0 1.0 copy-done.22
  112.0 1.3 collective-permute-start.5
  113.4 1.1 fusion.15.matrix_ref.turn_ref
  114.4 14.0 %forward_early.1 = (f32[1408,384]{1,0:T(8,128)}, f32[704,384]{1,0:T(8,128)}) custom-call(bf16[3,704,4096]{2,1,0:T(8,128)(2,1)} %bitcast.31, bf16[144,4096]{1,0:T(8,128)(2,1)} %get-tuple-element.86.refs_0_, bf16[144,4096]{1,0:T(8,128)(2,1)} %copy-done.22, bf16[144,4096]{1,0:T(8,128)(2,1)} %copy-done.17, ...), custom_call_target="tpu_custom_call" | custom-call | flops 6643777536 | bytes 23592960 | tf_op jit(solution)/shard_map/forward_early/pallas_call | solution.py:154
  128.5 8.7 %collective-permute-done.5.refs_1_.refs_3_ = bf16[144,4096]{1,0:T(8,128)(2,1)S(1)} collective-permute-done((bf16[144,4096]{1,0:T(8,128)(2,1)}, bf16[144,4096]{1,0:T(8,128)(2,1)S(1)}, u32[]{:S(2)}, u32[]{:S(2)}) %collective-permute-start.5) | collective-permute-done | bytes 1179680 | tf_op jit(solution)/shard_map/ppermute | solution.py:33
  137.2 1.0 copy-done.18
  138.6 15.7 %forward_late.1 = (bf16[1408,576]{1,0:T(8,128)(2,1)}, bf16[704,576]{1,0:T(8,128)(2,1)}, bf16[576,128]{1,0:T(8,128)(2,1)}) custom-call(bf16[576,576]{1,0:T(8,128)(2,1)} %fusion.15.matrix_ref.turn_ref, bf16[3,704,4096]{2,1,0:T(8,128)(2,1)} %bitcast.32, bf16[144,4096]{1,0:T(8,128)(2,1)} %copy-done.17, bf16[144,4096]{1,0:T(8,128)(2,1)} %copy-done.18, ...), custom_call_target="tpu_custom_call" | custom-call | flops 3321888768 | bytes 20545536 | tf_op jit(solution)/shard_map/forward_late/pallas_call | solution.py:224
  154.3 19.0 %terms.1 = bf16[8,3,88,4096]{3,2,1,0:T(8,128)(2,1)} custom-call(bf16[1408,576]{1,0:T(8,128)(2,1)} %get-tuple-element.90.deltas_ref, bf16[704,576]{1,0:T(8,128)(2,1)} %get-tuple-element.116.hidden_ref, bf16[144,4096]{1,0:T(8,128)(2,1)} %get-tuple-element.86.refs_0_, bf16[144,4096]{1,0:T(8,128)(2,1)} %copy-done.22, bf16[144,4096]{1,0:T(8,128)(2,1)} %copy-done.17, ...), custom_call_target="tpu_custom_call" | custom-call | flops 9965666304 | bytes 26738688 | tf_op jit(solution)/shard_map/terms/pallas_call | solution.py:272
  173.3 0.9 fusion.14.turn_ref
  174.3 9.7 %inputs.3 = (bf16[144,2048]{1,0:T(8,128)(2,1)}, bf16[144,2048]{1,0:T(8,128)(2,1)}, bf16[144,2048]{1,0:T(8,128)(2,1)}, bf16[144,2048]{1,0:T(8,128)(2,1)}) custom-call(bf16[576,576]{1,0:T(8,128)(2,1)} %fusion.15.matrix_ref.turn_ref, bf16[1408,576]{1,0:T(8,128)(2,1)} %get-tuple-element.90.deltas_ref, bf16[3,704,4096]{2,1,0:T(8,128)(2,1)} %bitcast.33, ...), custom_call_target="tpu_custom_call" | custom-call | flops 3321888768 | bytes 8126464 | tf_op jit(solution)/shard_map/inputs/pallas_call | solution.py:308
  183.9 2.1 collective-permute-start.19
  186.0 1.3 collective-permute-start.18
  187.3 9.8 %inputs.2 = (bf16[144,2176]{1,0:T(8,128)(2,1)}, bf16[144,2176]{1,0:T(8,128)(2,1)}, bf16[144,2176]{1,0:T(8,128)(2,1)}, bf16[144,2176]{1,0:T(8,128)(2,1)}) custom-call(bf16[576,576]{1,0:T(8,128)(2,1)} %fusion.14.turn_ref, bf16[1408,576]{1,0:T(8,128)(2,1)} %get-tuple-element.90.deltas_ref, bf16[3,704,4096]{2,1,0:T(8,128)(2,1)} %bitcast.34, ...), custom_call_target="tpu_custom_call" | custom-call | flops 3321888768 | bytes 8126464 | tf_op jit(solution)/shard_map/inputs/pallas_call | solution.py:308
  197.1 1.7 collective-permute-start.13
  198.8 1.2 collective-permute-start.12
  200.8 2.6 swap_near.7
  203.5 4.9 %collective-permute-done.18.far_ref = bf16[144,2048]{1,0:T(8,128)(2,1)S(1)} collective-permute-done((bf16[144,2048]{1,0:T(8,128)(2,1)}, bf16[144,2048]{1,0:T(8,128)(2,1)S(1)}, u32[]{:S(2)}, u32[]{:S(2)}) %collective-permute-start.18) | collective-permute-done | bytes 589856 | tf_op jit(solution)/shard_map/ppermute | solution.py:33
  209.2 2.2 swap_far.7
  211.4 1.0 collective-permute-start.21
  212.8 1.7 collective-permute-start.23
  214.6 0.8 copy-done.10
  215.4 2.6 swap_near.6
  218.0 3.7 %collective-permute-done.12.far_ref = bf16[144,2176]{1,0:T(8,128)(2,1)S(1)} collective-permute-done((bf16[144,2176]{1,0:T(8,128)(2,1)}, bf16[144,2176]{1,0:T(8,128)(2,1)S(1)}, u32[]{:S(2)}, u32[]{:S(2)}) %collective-permute-start.12) | collective-permute-done | bytes 626720 | tf_op jit(solution)/shard_map/ppermute | solution.py:33
  221.8 0.8 copy-done.19
  222.6 2.3 swap_far.6
  225.0 2.6 collective-permute-start.15
  227.6 11.4 %collective-permute-done.21 = bf16[144,2048]{1,0:T(8,128)(2,1)S(1)} collective-permute-done((bf16[144,2048]{1,0:T(8,128)(2,1)}, bf16[144,2048]{1,0:T(8,128)(2,1)S(1)}, u32[]{:S(2)}, u32[]{:S(2)}) %collective-permute-start.21) | collective-permute-done | bytes 589856 | tf_op jit(solution)/shard_map/ppermute | solution.py:33
  238.9 1.8 collective-permute-start.17
  240.7 1.1 slice.52
  241.8 0.9 slice_reduce_fusion.3
  242.8 3.9 %collective-permute-done.23 = bf16[144,2048]{1,0:T(8,128)(2,1)S(1)} collective-permute-done((bf16[144,2048]{1,0:T(8,128)(2,1)}, bf16[144,2048]{1,0:T(8,128)(2,1)S(1)}, u32[]{:S(2)}, u32[]{:S(2)}) %collective-permute-start.23) | collective-permute-done | bytes 589856 | tf_op jit(solution)/shard_map/ppermute | solution.py:33
  246.8 1.0 convolution_convert_fusion.8
  248.0 5.3 %collective-permute-done.17 = bf16[144,2176]{1,0:T(8,128)(2,1)S(1)} collective-permute-done((bf16[144,2176]{1,0:T(8,128)(2,1)}, bf16[144,2176]{1,0:T(8,128)(2,1)S(1)}, u32[]{:S(2)}, u32[]{:S(2)}) %collective-permute-start.17) | collective-permute-done | bytes 626720 | tf_op jit(solution)/shard_map/ppermute | solution.py:33
  253.8 1.2 select_reduce_fusion
  255.0 1.0 convolution_convert_fusion.9
  256.0 1.3 pad_maximum_fusion
  257.3 13.8 %reduce-scatter.2.cloned.1.call-done = bf16[1,3,88,4096]{3,2,1,0:T(8,128)(2,1)} async-done(((bf16[8,3,88,4096]{3,2,1,0:T(8,128)(2,1)}), bf16[1,3,88,4096]{3,2,1,0:T(8,128)(2,1)}) %reduce-scatter.2.cloned.1.call-update) | async-done | bytes 2162704 | tf_op jit(solution)/shard_map/reduce_scatter | solution.py:395
  271.1 4.3 %convert_bitcast_fusion = f32[1,88,3,4096]{3,1,2,0:T(8,128)} fusion(bf16[1,3,88,4096]{3,2,1,0:T(8,128)(2,1)} %reduce-scatter.2.cloned.1.call-done), kind=kLoop, calls=%fused_computation.8 | loop fusion | flops 1081344 | bytes 6488064 | tf_op jit(solution)/shard_map/transpose | solution.py:396
  (93 shorter events, 9.0 us)
Async XLA Ops:
  7.2 3.1 %copy-start = (bf16[192,4096]{1,0:T(8,128)(2,1)S(1)}, bf16[192,4096]{1,0:T(8,128)(2,1)}, u32[]{:S(2)}) copy-start(bf16[192,4096]{1,0:T(8,128)(2,1)} %param.6) | copy-start | bytes 4718596
  7.2 264.0 %reduce-scatter.2.cloned.1.call-start = ((), (), s32[]{:S(2)}) async-start(), calls=%async_computation.1 | async-start | bytes 19464192 | tf_op jit(solution)/shard_map/reduce_scatter | solution.py:395
  11.1 29.4 %collective-permute-start.6 = (bf16[144,4224]{1,0:T(8,128)(2,1)S(1)}, bf16[144,4224]{1,0:T(8,128)(2,1)S(1)}, u32[]{:S(2)}, u32[]{:S(2)}) collective-permute-start(bf16[144,4224]{1,0:T(8,128)(2,1)S(1)} %pad_maximum_fusion.2), channel_id=1, source_target_pairs={{0,1},{1,2},{2,3},{3,0},{4,5},{5,6},{6,7},{7,4},{8,9},{9,10},{10,1... | collective-permute-start | bytes 3649544 | tf_op jit(solution)/shard_map/ppermute | solution.py:33
  13.7 1.6 copy-start.2
  13.9 27.4 %collective-permute-start.7 = (bf16[144,4224]{1,0:T(8,128)(2,1)S(1)}, bf16[144,4224]{1,0:T(8,128)(2,1)S(1)}, u32[]{:S(2)}, u32[]{:S(2)}) collective-permute-start(bf16[144,4224]{1,0:T(8,128)(2,1)S(1)} %pad_maximum_fusion.3), channel_id=1, source_target_pairs={{0,3},{1,0},{2,1},{3,2},{4,7},{5,4},{6,5},{7,6},{8,11},{9,8},{10,9... | collective-permute-start | bytes 3649544 | tf_op jit(solution)/shard_map/ppermute | solution.py:33
  15.9 30.2 %collective-permute-start.1 = (bf16[144,4096]{1,0:T(8,128)(2,1)S(1)}, bf16[144,4096]{1,0:T(8,128)(2,1)S(1)}, u32[]{:S(2)}, u32[]{:S(2)}) collective-permute-start(bf16[144,4096]{1,0:T(8,128)(2,1)S(1)} %convolution_convert_fusion.5), channel_id=1, source_target_pairs={{0,12},{1,13},{2,14},{3,15},{4,0},{5,1},{6,2},{7,3},{8,4},{9,5},{1... | collective-permute-start | bytes 3538952 | tf_op jit(solution)/shard_map/ppermute | solution.py:33
  20.4 27.2 %collective-permute-start = (bf16[144,4096]{1,0:T(8,128)(2,1)S(1)}, bf16[144,4096]{1,0:T(8,128)(2,1)S(1)}, u32[]{:S(2)}, u32[]{:S(2)}) collective-permute-start(bf16[144,4096]{1,0:T(8,128)(2,1)S(1)} %convolution_convert_fusion.6), channel_id=1, source_target_pairs={{0,4},{1,5},{2,6},{3,7},{4,8},{5,9},{6,10},{7,11},{8,12},{9,13},{1... | collective-permute-start | bytes 3538952 | tf_op jit(solution)/shard_map/ppermute | solution.py:33
  40.5 9.8 %copy-start.5 = (bf16[144,4224]{1,0:T(8,128)(2,1)}, bf16[144,4224]{1,0:T(8,128)(2,1)S(1)}, u32[]{:S(2)}) copy-start(bf16[144,4224]{1,0:T(8,128)(2,1)S(1)} %collective-permute-done.6.refs_1_) | copy-start | bytes 3649540
  41.3 9.0 %copy-start.6 = (bf16[144,4224]{1,0:T(8,128)(2,1)}, bf16[144,4224]{1,0:T(8,128)(2,1)S(1)}, u32[]{:S(2)}) copy-start(bf16[144,4224]{1,0:T(8,128)(2,1)S(1)} %collective-permute-done.7.refs_2_) | copy-start | bytes 3649540
  41.3 27.9 %collective-permute-start.8 = (bf16[144,4224]{1,0:T(8,128)(2,1)S(1)}, bf16[144,4224]{1,0:T(8,128)(2,1)S(1)}, u32[]{:S(2)}, u32[]{:S(2)}) collective-permute-start(bf16[144,4224]{1,0:T(8,128)(2,1)S(1)} %pad_maximum_fusion.1), channel_id=1, source_target_pairs={{0,2},{1,3},{2,0},{3,1},{4,6},{5,7},{6,4},{7,5},{8,10},{9,11},{10,... | collective-permute-start | bytes 3649544 | tf_op jit(solution)/shard_map/ppermute | solution.py:33
  46.1 5.4 %copy-start.7 = (bf16[144,4096]{1,0:T(8,128)(2,1)}, bf16[144,4096]{1,0:T(8,128)(2,1)S(1)}, u32[]{:S(2)}) copy-start(bf16[144,4096]{1,0:T(8,128)(2,1)S(1)} %collective-permute-done.1.refs_2_) | copy-start | bytes 3538948
  47.6 2.6 copy-start.8
  47.6 33.9 %collective-permute-start.2 = (bf16[144,4096]{1,0:T(8,128)(2,1)}, bf16[144,4096]{1,0:T(8,128)(2,1)S(1)}, u32[]{:S(2)}, u32[]{:S(2)}) collective-permute-start(bf16[144,4096]{1,0:T(8,128)(2,1)} %convolution_convert_fusion.7), channel_id=1, source_target_pairs={{0,8},{1,9},{2,10},{3,11},{4,12},{5,13},{6,14},{7,15},{8,0},{9,1},... | collective-permute-start | bytes 3538952 | tf_op jit(solution)/shard_map/ppermute | solution.py:33
  69.2 1.0 copy-start.14
  73.1 28.0 %collective-permute-start.10 = (bf16[144,4224]{1,0:T(8,128)(2,1)}, bf16[144,4224]{1,0:T(8,128)(2,1)S(1)}, u32[]{:S(2)}, u32[]{:S(2)}) collective-permute-start(bf16[144,4224]{1,0:T(8,128)(2,1)} %get-tuple-element.81), channel_id=1, source_target_pairs={{0,12},{1,13},{2,14},{3,15},{4,0},{5,1},{6,2},{7,3},{8,4},{9,5},{1... | collective-permute-start | bytes 3649544 | tf_op jit(solution)/shard_map/ppermute | solution.py:33
  76.9 26.6 %collective-permute-start.9 = (bf16[144,4224]{1,0:T(8,128)(2,1)}, bf16[144,4224]{1,0:T(8,128)(2,1)S(1)}, u32[]{:S(2)}, u32[]{:S(2)}) collective-permute-start(bf16[144,4224]{1,0:T(8,128)(2,1)} %get-tuple-element.80), channel_id=1, source_target_pairs={{0,4},{1,5},{2,6},{3,7},{4,8},{5,9},{6,10},{7,11},{8,12},{9,13},{1... | collective-permute-start | bytes 3649544 | tf_op jit(solution)/shard_map/ppermute | solution.py:33
  81.5 1.0 copy-start.16
  82.5 21.0 %copy-start.15 = (bf16[144,4224]{1,0:T(8,128)(2,1)S(1)}, bf16[144,4224]{1,0:T(8,128)(2,1)}, u32[]{:S(2)}) copy-start(bf16[144,4224]{1,0:T(8,128)(2,1)} %get-tuple-element.83) | copy-start | bytes 3649540
  85.1 25.8 %collective-permute-start.3 = (bf16[144,4096]{1,0:T(8,128)(2,1)}, bf16[144,4096]{1,0:T(8,128)(2,1)S(1)}, u32[]{:S(2)}, u32[]{:S(2)}) collective-permute-start(bf16[144,4096]{1,0:T(8,128)(2,1)} %get-tuple-element.68), channel_id=1, source_target_pairs={{0,1},{1,2},{2,3},{3,0},{4,5},{5,6},{6,7},{7,4},{8,9},{9,10},{10,1... | collective-permute-start | bytes 3538952 | tf_op jit(solution)/shard_map/ppermute | solution.py:33
  86.4 24.6 %collective-permute-start.4 = (bf16[144,4096]{1,0:T(8,128)(2,1)}, bf16[144,4096]{1,0:T(8,128)(2,1)S(1)}, u32[]{:S(2)}, u32[]{:S(2)}) collective-permute-start(bf16[144,4096]{1,0:T(8,128)(2,1)} %get-tuple-element.69), channel_id=1, source_target_pairs={{0,3},{1,0},{2,1},{3,2},{4,7},{5,4},{6,5},{7,6},{8,11},{9,8},{10,9... | collective-permute-start | bytes 3538952 | tf_op jit(solution)/shard_map/ppermute | solution.py:33
  101.1 13.3 %copy-start.3 = (bf16[144,4224]{1,0:T(8,128)(2,1)}, bf16[144,4224]{1,0:T(8,128)(2,1)S(1)}, u32[]{:S(2)}) copy-start(bf16[144,4224]{1,0:T(8,128)(2,1)S(1)} %collective-permute-done.10.refs_5_.refs_2_.refs_6_.refs_10_) | copy-start | bytes 3649540
  103.5 11.0 %copy-start.13 = (bf16[144,4224]{1,0:T(8,128)(2,1)}, bf16[144,4224]{1,0:T(8,128)(2,1)S(1)}, u32[]{:S(2)}) copy-start(bf16[144,4224]{1,0:T(8,128)(2,1)S(1)} %collective-permute-done.9.refs_4_.refs_5_.refs_9_) | copy-start | bytes 3649540
  103.5 33.7 %collective-permute-start.11 = (bf16[144,4224]{1,0:T(8,128)(2,1)S(1)}, bf16[144,4224]{1,0:T(8,128)(2,1)S(1)}, u32[]{:S(2)}, u32[]{:S(2)}) collective-permute-start(bf16[144,4224]{1,0:T(8,128)(2,1)S(1)} %copy-done.15), channel_id=1, source_target_pairs={{0,8},{1,9},{2,10},{3,11},{4,12},{5,13},{6,14},{7,15},{8,0},{9,1},... | collective-permute-start | bytes 3649544 | tf_op jit(solution)/shard_map/ppermute | solution.py:33
  111.0 1.1 copy-start.22
  112.0 2.4 copy-start.17
  112.0 25.2 %collective-permute-start.5 = (bf16[144,4096]{1,0:T(8,128)(2,1)}, bf16[144,4096]{1,0:T(8,128)(2,1)S(1)}, u32[]{:S(2)}, u32[]{:S(2)}) collective-permute-start(bf16[144,4096]{1,0:T(8,128)(2,1)} %get-tuple-element.71), channel_id=1, source_target_pairs={{0,2},{1,3},{2,0},{3,1},{4,6},{5,7},{6,4},{7,5},{8,10},{9,11},{10,... | collective-permute-start | bytes 3538952 | tf_op jit(solution)/shard_map/ppermute | solution.py:33
  137.2 1.1 copy-start.18
  137.2 1.4 copy-start.4
  183.9 14.9 %collective-permute-start.19 = (bf16[144,2048]{1,0:T(8,128)(2,1)}, bf16[144,2048]{1,0:T(8,128)(2,1)S(1)}, u32[]{:S(2)}, u32[]{:S(2)}) collective-permute-start(bf16[144,2048]{1,0:T(8,128)(2,1)} %get-tuple-element.106), channel_id=1, source_target_pairs={{0,12},{1,13},{2,14},{3,15},{4,0},{5,1},{6,2},{7,3},{8,4},{9,5},{1... | collective-permute-start | bytes 1769480 | tf_op jit(solution)/shard_map/ppermute | solution.py:33
  186.0 14.0 %collective-permute-start.20 = (bf16[144,2048]{1,0:T(8,128)(2,1)}, bf16[144,2048]{1,0:T(8,128)(2,1)S(1)}, u32[]{:S(2)}, u32[]{:S(2)}) collective-permute-start(bf16[144,2048]{1,0:T(8,128)(2,1)} %get-tuple-element.107), channel_id=1, source_target_pairs={{0,4},{1,5},{2,6},{3,7},{4,8},{5,9},{6,10},{7,11},{8,12},{9,13},{1... | collective-permute-start | bytes 1769480 | tf_op jit(solution)/shard_map/ppermute | solution.py:33
  186.0 22.3 %collective-permute-start.18 = (bf16[144,2048]{1,0:T(8,128)(2,1)}, bf16[144,2048]{1,0:T(8,128)(2,1)S(1)}, u32[]{:S(2)}, u32[]{:S(2)}) collective-permute-start(bf16[144,2048]{1,0:T(8,128)(2,1)} %get-tuple-element.104), channel_id=1, source_target_pairs={{0,8},{1,9},{2,10},{3,11},{4,12},{5,13},{6,14},{7,15},{8,0},{9,1},... | collective-permute-start | bytes 1769480 | tf_op jit(solution)/shard_map/ppermute | solution.py:33
  197.1 15.7 %collective-permute-start.13 = (bf16[144,2176]{1,0:T(8,128)(2,1)}, bf16[144,2176]{1,0:T(8,128)(2,1)S(1)}, u32[]{:S(2)}, u32[]{:S(2)}) collective-permute-start(bf16[144,2176]{1,0:T(8,128)(2,1)} %get-tuple-element.94), channel_id=1, source_target_pairs={{0,3},{1,0},{2,1},{3,2},{4,7},{5,4},{6,5},{7,6},{8,11},{9,8},{10,9... | collective-permute-start | bytes 1880072 | tf_op jit(solution)/shard_map/ppermute | solution.py:33
  198.8 15.7 %collective-permute-start.14 = (bf16[144,2176]{1,0:T(8,128)(2,1)}, bf16[144,2176]{1,0:T(8,128)(2,1)S(1)}, u32[]{:S(2)}, u32[]{:S(2)}) collective-permute-start(bf16[144,2176]{1,0:T(8,128)(2,1)} %get-tuple-element.95), channel_id=1, source_target_pairs={{0,1},{1,2},{2,3},{3,0},{4,5},{5,6},{6,7},{7,4},{8,9},{9,10},{10,1... | collective-permute-start | bytes 1880072 | tf_op jit(solution)/shard_map/ppermute | solution.py:33
  198.8 1.2 copy-start.11
  198.8 22.9 %collective-permute-start.12 = (bf16[144,2176]{1,0:T(8,128)(2,1)}, bf16[144,2176]{1,0:T(8,128)(2,1)S(1)}, u32[]{:S(2)}, u32[]{:S(2)}) collective-permute-start(bf16[144,2176]{1,0:T(8,128)(2,1)} %get-tuple-element.92), channel_id=1, source_target_pairs={{0,2},{1,3},{2,0},{3,1},{4,6},{5,7},{6,4},{7,5},{8,10},{9,11},{10,... | collective-permute-start | bytes 1880072 | tf_op jit(solution)/shard_map/ppermute | solution.py:33
  200.0 0.8 copy-start.12
  208.4 0.8 copy-start.20
  211.4 27.6 %collective-permute-start.21 = (bf16[144,2048]{1,0:T(8,128)(2,1)}, bf16[144,2048]{1,0:T(8,128)(2,1)S(1)}, u32[]{:S(2)}, u32[]{:S(2)}) collective-permute-start(bf16[144,2048]{1,0:T(8,128)(2,1)} %get-tuple-element.113), channel_id=1, source_target_pairs={{0,3},{1,0},{2,1},{3,2},{4,7},{5,4},{6,5},{7,6},{8,11},{9,8},{10,9... | collective-permute-start | bytes 1769480 | tf_op jit(solution)/shard_map/ppermute | solution.py:33
  212.4 30.4 %collective-permute-start.22 = (bf16[144,2048]{1,0:T(8,128)(2,1)}, bf16[144,2048]{1,0:T(8,128)(2,1)S(1)}, u32[]{:S(2)}, u32[]{:S(2)}) collective-permute-start(bf16[144,2048]{1,0:T(8,128)(2,1)} %get-tuple-element.114), channel_id=1, source_target_pairs={{0,1},{1,2},{2,3},{3,0},{4,5},{5,6},{6,7},{7,4},{8,9},{9,10},{10,1... | collective-permute-start | bytes 1769480 | tf_op jit(solution)/shard_map/ppermute | solution.py:33
  212.8 1.7 copy-start.9
  212.8 33.9 %collective-permute-start.23 = (bf16[144,2048]{1,0:T(8,128)(2,1)}, bf16[144,2048]{1,0:T(8,128)(2,1)S(1)}, u32[]{:S(2)}, u32[]{:S(2)}) collective-permute-start(bf16[144,2048]{1,0:T(8,128)(2,1)} %get-tuple-element.115), channel_id=1, source_target_pairs={{0,2},{1,3},{2,0},{3,1},{4,6},{5,7},{6,4},{7,5},{8,10},{9,11},{10,... | collective-permute-start | bytes 1769480 | tf_op jit(solution)/shard_map/ppermute | solution.py:33
  214.6 0.8 copy-start.10
  221.8 0.8 copy-start.19
  222.6 24.2 %copy-start.21 = (bf16[144,2048]{1,0:T(8,128)(2,1)S(1)}, bf16[144,2048]{1,0:T(8,128)(2,1)}, u32[]{:S(2)}) copy-start(bf16[144,2048]{1,0:T(8,128)(2,1)} %get-tuple-element.112) | copy-start | bytes 1769476
  225.0 22.9 %collective-permute-start.15 = (bf16[144,2176]{1,0:T(8,128)(2,1)}, bf16[144,2176]{1,0:T(8,128)(2,1)S(1)}, u32[]{:S(2)}, u32[]{:S(2)}) collective-permute-start(bf16[144,2176]{1,0:T(8,128)(2,1)} %get-tuple-element.101), channel_id=1, source_target_pairs={{0,12},{1,13},{2,14},{3,15},{4,0},{5,1},{6,2},{7,3},{8,4},{9,5},{1... | collective-permute-start | bytes 1880072 | tf_op jit(solution)/shard_map/ppermute | solution.py:33
  227.5 20.3 %collective-permute-start.16 = (bf16[144,2176]{1,0:T(8,128)(2,1)}, bf16[144,2176]{1,0:T(8,128)(2,1)S(1)}, u32[]{:S(2)}, u32[]{:S(2)}) collective-permute-start(bf16[144,2176]{1,0:T(8,128)(2,1)} %get-tuple-element.102), channel_id=1, source_target_pairs={{0,4},{1,5},{2,6},{3,7},{4,8},{5,9},{6,10},{7,11},{8,12},{9,13},{1... | collective-permute-start | bytes 1880072 | tf_op jit(solution)/shard_map/ppermute | solution.py:33
  238.9 14.4 %collective-permute-start.17 = (bf16[144,2176]{1,0:T(8,128)(2,1)}, bf16[144,2176]{1,0:T(8,128)(2,1)S(1)}, u32[]{:S(2)}, u32[]{:S(2)}) collective-permute-start(bf16[144,2176]{1,0:T(8,128)(2,1)} %get-tuple-element.103), channel_id=1, source_target_pairs={{0,8},{1,9},{2,10},{3,11},{4,12},{5,13},{6,14},{7,15},{8,0},{9,1},... | collective-permute-start | bytes 1880072 | tf_op jit(solution)/shard_map/ppermute | solution.py:33
  271.1 4.3 %copy-start.1 = (bf16[192,4096]{1,0:T(8,128)(2,1)S(1)}, bf16[192,4096]{1,0:T(8,128)(2,1)}, u32[]{:S(2)}) copy-start(bf16[192,4096]{1,0:T(8,128)(2,1)} %param.6) | copy-start | bytes 4718596
Sparse Core Ops, SparseCore 0:
  173.4 97.6 reduce-scatter.1

commit v3 on v2

--- a/solution.py
+++ b/solution.py
@@ -16,7 +16,7 @@
 MAIN = 32
 TAIL = CAP - MAIN
 EARLY = 384
-BIG = 56 << 20
+LIMITS = {"swap": 16, "early": 16, "late": 16, "terms": 16, "inputs": 16, "widen": 56}
 
 
 def hop(dz, dx):
@@ -60,8 +60,10 @@
     return (source[:, None] == row[None, :]).astype(jnp.bfloat16)
 
 
-def params():
-    return pltpu.CompilerParams(dimension_semantics=("arbitrary",), vmem_limit_bytes=BIG)
+def params(kernel):
+    return pltpu.CompilerParams(
+        dimension_semantics=("arbitrary",), vmem_limit_bytes=LIMITS[kernel] << 20
+    )
 
 
 def cost(flops, moved):
@@ -97,7 +99,7 @@
         in_specs=[pl.BlockSpec((SIDE * MAIN, tile), lambda i: (0, i))] * last,
         out_specs=[pl.BlockSpec((last * MAIN, tile), lambda i: (0, i))] * SIDE,
         out_shape=shapes,
-        compiler_params=params(),
+        compiler_params=params("swap"),
         cost_estimate=cost(0, 3 * ROWS * width),
         name="swap_near",
     )(*blocks[:last])
@@ -115,7 +117,7 @@
         out_specs=[pl.BlockSpec((left, tile), lambda i: (BLOCK // left - 1, i))] * SIDE,
         out_shape=shapes,
         input_output_aliases={2 + last + q: q for q in range(SIDE)},
-        compiler_params=params(),
+        compiler_params=params("swap"),
         cost_estimate=cost(2 * 64 * 64 * width, ROWS * width),
         name="swap_far",
     )(matrix, blocks[last], *blocks[:last], *placed)
@@ -148,7 +150,7 @@
 
 def forward_early(weights, toks, cots):
     units, width = weights.shape[1:]
-    tile = 1024
+    tile = 512
     rows = pl.BlockSpec((BLOCK, tile), lambda i: (0, i))
     shapes = [(2 * units, EARLY), (units, EARLY)]
     return pl.pallas_call(
@@ -157,7 +159,7 @@
         in_specs=[pl.BlockSpec((3, units, tile), lambda i: (0, 0, i))] + [rows] * 6,
         out_specs=[pl.BlockSpec(shape, lambda i: (0, 0)) for shape in shapes],
         out_shape=[jax.ShapeDtypeStruct(shape, jnp.float32) for shape in shapes],
-        compiler_params=params(),
+        compiler_params=params("early"),
         cost_estimate=cost(6 * EARLY * units * width, 6 * units * width + 4 * EARLY * width),
         name="forward_early",
     )(weights, *toks, *cots)
@@ -215,7 +217,7 @@
 
 def forward_late(matrix, weights, toks, cots, early):
     units, width = weights.shape[1:]
-    tile = 1024
+    tile = 512
     steps = width // tile
     rows = pl.BlockSpec((BLOCK, tile), lambda i: (0, i))
     extra = pl.BlockSpec((BLOCK, EXTRA), lambda i: (0, width // EXTRA))
@@ -234,7 +236,7 @@
         out_specs=[pl.BlockSpec(shape, lambda i: (0, 0)) for shape in shapes],
         out_shape=[jax.ShapeDtypeStruct(shape, jnp.bfloat16) for shape in shapes],
         scratch_shapes=[pltpu.VMEM((n * units, late), jnp.float32) for n in (2, 1)],
-        compiler_params=params(),
+        compiler_params=params("late"),
         cost_estimate=cost(6 * late * units * width, 6 * units * width + 12 * EARLY * units),
         name="forward_late",
     )(matrix, weights, *toks[2:], *cots[2:], *cots, *early)
@@ -265,7 +267,7 @@
 def terms(deltas, hidden, toks, cots, owners):
     units = hidden.shape[0]
     width = toks[0].shape[1]
-    tile = 1024
+    tile = 512
     rows = pl.BlockSpec((BLOCK, tile), lambda i: (0, i))
     extra = pl.BlockSpec((BLOCK, EXTRA), lambda i: (0, width // EXTRA))
     share = units // owners
@@ -276,11 +278,31 @@
         + [rows] * 8
         + [extra] * 4,
         out_specs=pl.BlockSpec((owners, 3, share, tile), lambda i: (0, 0, 0, i)),
-        out_shape=jax.ShapeDtypeStruct((owners, 3, share, width), jnp.bfloat16),
-        compiler_params=params(),
+        out_shape=pltpu.HBM((owners, 3, share, width), jnp.bfloat16),
+        compiler_params=params("terms"),
         cost_estimate=cost(6 * ROWS * units * width, 6 * units * width + 4 * ROWS * width),
         name="terms",
     )(deltas, hidden, *toks, *cots, *cots)
+
+
+def widen_kernel(in_ref, out_ref):
+    out_ref[0, 0] = in_ref[0, 0].astype(jnp.float32)
+
+
+def widen(summed):
+    _, kinds, share, width = summed.shape
+    tile = width // 2
+    spec = pl.BlockSpec((1, 1, share, tile), lambda i: (0, i // 2, 0, i % 2))
+    return pl.pallas_call(
+        widen_kernel,
+        grid=(2 * kinds,),
+        in_specs=[spec],
+        out_specs=spec,
+        out_shape=jax.ShapeDtypeStruct(summed.shape, jnp.float32),
+        compiler_params=params("widen"),
+        cost_estimate=cost(0, 6 * kinds * share * width),
+        name="widen",
+    )(summed)
 
 
 def inputs_kernel(tile, turn_ref, deltas_ref, weight_ref, route_ref, *refs):
@@ -317,7 +339,7 @@
         out_specs=[pl.BlockSpec(block, lambda i: (0, 0))] * SIDE,
         out_shape=[jax.ShapeDtypeStruct(block, jnp.bfloat16)] * SIDE,
         scratch_shapes=[pltpu.VMEM((ROWS, 2 * units), jnp.bfloat16)],
-        compiler_params=params(),
+        compiler_params=params("inputs"),
         cost_estimate=cost(4 * ROWS * units * count, 4 * units * count + 2 * ROWS * count),
         name="inputs",
     )(turn, deltas, weights, route)
@@ -393,7 +415,7 @@
     deltas, hidden, route = forward_late(turn, weights, toks, cots, early)
     partial_sums = terms(deltas, hidden, toks, cots, owners)
     summed = lax.psum_scatter(partial_sums, "dp", scatter_dimension=0, tiled=True)
-    weight_grad = summed.astype(jnp.float32).transpose(0, 2, 1, 3)
+    weight_grad = widen(summed).transpose(0, 2, 1, 3)
 
     right = inputs(turn, deltas, weights, route, half, half, 0)
     left = inputs(same, deltas, weights, route, 0, half, EXTRA)

time: 283 us -> 271 us (0.958)
  waiting for transfers between devices: 111 us -> 139 us
  Pallas kernels: 90.2 us -> 64.7 us
  other arithmetic: 13.8 us -> 6.06 us
  starting transfers between devices: 33.8 us -> 30.6 us
    ppermute x24, waiting for transfers between devices: 97 us -> 126 us  [move(): lax.ppermute(value, 'expert', hop(step, 0) if axis == 'z' else hop(0, step))]
    pallas_call x4, Pallas kernels: 12 us -> 1.46 us  [swap_blocks(): pl.pallas_call(swap_near_kernel, grid=grid, in_specs=[pl.BlockSpec((SIDE...]
    pallas_call x4, Pallas kernels: 10 us -> 1.44 us  [swap_blocks(): pl.pallas_call(swap_far_kernel, grid=grid, in_specs=[pl.BlockSpec(matrix....]
    pallas_call x2, Pallas kernels: 19.5 us -> 12.7 us  [inputs(): pl.pallas_call(functools.partial(inputs_kernel, tile), grid=(count // til...]
    pallas_call x0 -> x1, Pallas kernels: none -> 5.27 us  [widen(): pl.pallas_call(widen_kernel, grid=(2 * kinds,), in_specs=[spec], out_spec...]
    transpose x1 -> x0, other arithmetic: 4.3 us -> none  [shards(): weight_grad = summed.astype(jnp.float32).transpose(0, 2, 1, 3)]
    pallas_call x1, Pallas kernels: 15.7 us -> 12 us  [forward_late(): pl.pallas_call(functools.partial(late_kernel, steps), grid=(steps,), in_s...]
    ppermute x24, starting transfers between devices: 33.7 us -> 30.6 us  [move(): lax.ppermute(value, 'expert', hop(step, 0) if axis == 'z' else hop(0, step))]
  transfers between devices with their start and end apart: 25 -> 25, of which waited for: 15 -> 17; matrix products, arithmetic and copies ran while one was open for 6% -> 4% of each run, Pallas kernels for 20% -> 11%
where the time goes in v3:
time: 271 us
  waiting for transfers between devices  139 us (51%)
  Pallas kernels  64.7 us (24%)
  starting transfers between devices  30.6 us (11%)
  between operations  14.6 us (5%)
  local copies, waits for them, and re-layouts  9.59 us (4%)
  matrix products  6.56 us (2%)
  other arithmetic  6.06 us (2%)
    ppermute x24, waiting for transfers between devices, move(): lax.ppermute(value, 'expert', hop(step, 0) if axis == 'z' else hop(0, step))  126 us
    ppermute x24, starting transfers between devices, move(): lax.ppermute(value, 'expert', hop(step, 0) if axis == 'z' else hop(0, step))  30.6 us
    pallas_call x1, Pallas kernels, terms(): pl.pallas_call(terms_kernel, grid=(width // tile,), in_specs=[pl.BlockSpe...  18.2 us
    pallas_call x1, Pallas kernels, forward_early(): pl.pallas_call(early_kernel, grid=(width // tile,), in_specs=[pl.BlockSpe...  13.7 us
    pallas_call x2, Pallas kernels, inputs(): pl.pallas_call(functools.partial(inputs_kernel, tile), grid=(count // til...  12.7 us
    reduce_scatter x1, waiting for transfers between devices, shards(): lax.psum_scatter(partial_sums, 'dp', scatter_dimension=0, tiled=True)  12.5 us
    pallas_call x1, Pallas kernels, forward_late(): pl.pallas_call(functools.partial(late_kernel, steps), grid=(steps,), in_s...  12 us
    unnamed x22, local copies, waits for them, and re-layouts  8.58 us
  transfers between devices with their start and end apart: 25, of which 17 were waited for; matrix products, arithmetic and copies ran while one was open for 4% of the time, Pallas kernels for 11%

profile of v3, /device:TPU:1, one launch (start us, length us, event | category | flops | bytes accessed | tf_op | source)
XLA Modules:
  0.0 270.9 jit_solution(17462516096889149963)
XLA Ops:
  7.3 0.8 fusion.118
  8.3 0.7 select_reduce_fusion.5
  9.1 1.2 select_reduce_fusion.1
  10.3 0.6 convolution_convert_fusion.2
  11.1 2.1 collective-permute-start.6
  13.2 0.6 convolution_convert_fusion.1
  13.9 1.4 collective-permute-start.7
  15.3 0.6 convolution_convert_fusion.5
  15.8 4.0 %collective-permute-start.1 = (bf16[144,4096]{1,0:T(8,128)(2,1)S(1)}, bf16[144,4096]{1,0:T(8,128)(2,1)S(1)}, u32[]{:S(2)}, u32[]{:S(2)}) collective-permute-start(bf16[144,4096]{1,0:T(8,128)(2,1)S(1)} %convolution_convert_fusion.5), channel_id=1, source_target_pairs={{0,12},{1,13},{2,14},{3,15},{4,0},{5,1},{6,2},{7,3},{8,4},{9,5},{1... | collective-permute-start | bytes 3538952 | tf_op jit(solution)/shard_map/ppermute | solution.py:33
  19.9 0.6 convolution_convert_fusion.6
  20.5 0.6 convolution_convert_fusion.3
  21.3 19.2 %collective-permute-done.6.refs_1_ = bf16[144,4224]{1,0:T(8,128)(2,1)S(1)} collective-permute-done((bf16[144,4224]{1,0:T(8,128)(2,1)S(1)}, bf16[144,4224]{1,0:T(8,128)(2,1)S(1)}, u32[]{:S(2)}, u32[]{:S(2)}) %collective-permute-start.6) | collective-permute-done | bytes 1216544 | tf_op jit(solution)/shard_map/ppermute | solution.py:33
  40.5 0.8 collective-permute-done.7.refs_2_
  41.3 2.5 collective-permute-start.8
  43.8 0.6 convolution_convert_fusion.7
  44.4 3.2 %collective-permute-done.refs_1_ = bf16[144,4096]{1,0:T(8,128)(2,1)S(1)} collective-permute-done((bf16[144,4096]{1,0:T(8,128)(2,1)S(1)}, bf16[144,4096]{1,0:T(8,128)(2,1)S(1)}, u32[]{:S(2)}, u32[]{:S(2)}) %collective-permute-start) | collective-permute-done | bytes 1179680 | tf_op jit(solution)/shard_map/ppermute | solution.py:33
  47.6 0.5 collective-permute-start.2
  48.1 0.5 convolution_convert_fusion
  48.8 0.4 swap_near.5
  49.2 19.9 %collective-permute-done.8.far_ref = bf16[144,4224]{1,0:T(8,128)(2,1)S(1)} collective-permute-done((bf16[144,4224]{1,0:T(8,128)(2,1)S(1)}, bf16[144,4224]{1,0:T(8,128)(2,1)S(1)}, u32[]{:S(2)}, u32[]{:S(2)}) %collective-permute-start.8) | collective-permute-done | bytes 1216544 | tf_op jit(solution)/shard_map/ppermute | solution.py:33
  69.2 0.3 swap_far.5
  69.5 3.8 %collective-permute-start.10 = (bf16[144,4224]{1,0:T(8,128)(2,1)S(1)}, bf16[144,4224]{1,0:T(8,128)(2,1)S(1)}, u32[]{:S(2)}, u32[]{:S(2)}) collective-permute-start(bf16[144,4224]{1,0:T(8,128)(2,1)S(1)} %get-tuple-element.81), channel_id=1, source_target_pairs={{0,12},{1,13},{2,14},{3,15},{4,0},{5,1},{6,2},{7,3},{8,4},{9,5},{1... | collective-permute-start | bytes 3649544 | tf_op jit(solution)/shard_map/ppermute | solution.py:33
  73.4 0.5 convolution_convert_fusion.4.refs_0_
  73.9 0.7 swap_near.4
  74.6 0.7 swap_far.4
  75.3 1.3 collective-permute-start.3
  76.6 1.5 collective-permute-start.4
  78.1 21.6 %collective-permute-done.10.refs_5_.refs_2_.refs_6_.refs_10_ = bf16[144,4224]{1,0:T(8,128)(2,1)S(1)} collective-permute-done((bf16[144,4224]{1,0:T(8,128)(2,1)S(1)}, bf16[144,4224]{1,0:T(8,128)(2,1)S(1)}, u32[]{:S(2)}, u32[]{:S(2)}) %collective-permute-start.10) | collective-permute-done | bytes 1216544 | tf_op jit(solution)/shard_map/ppermute | solution.py:33
  99.8 1.0 collective-permute-done.9.refs_4_.refs_5_.refs_9_
  100.7 1.2 collective-permute-start.11
  101.9 1.5 collective-permute-start.5
  103.7 13.7 %forward_early.1 = (f32[1408,384]{1,0:T(8,128)S(1)}, f32[704,384]{1,0:T(8,128)S(1)}) custom-call(bf16[3,704,4096]{2,1,0:T(8,128)(2,1)S(1)} %bitcast.32, bf16[144,4096]{1,0:T(8,128)(2,1)S(1)} %get-tuple-element.86.refs_0_, bf16[144,4096]{1,0:T(8,128)(2,1)S(1)} %collective-permute-done.3.refs_1_, bf16[144,4096]{1,0:T(8,128)(2,1)S(1)} %collective-permute-done.4.refs_2_.refs_0_, ...), custom_call_target="tpu_custom_call" | custom-call | flops 6643777536 | bytes 23592960 | tf_op jit(solution)/shard_map/forward_early/pallas_call | solution.py:156
  117.4 1.4 collective-permute-done.5.refs_1_.refs_3_
  118.8 8.2 %collective-permute-done.11.refs_3_.refs_7_.refs_11_ = bf16[144,4224]{1,0:T(8,128)(2,1)S(1)} collective-permute-done((bf16[144,4224]{1,0:T(8,128)(2,1)S(1)}, bf16[144,4224]{1,0:T(8,128)(2,1)S(1)}, u32[]{:S(2)}, u32[]{:S(2)}) %collective-permute-start.11) | collective-permute-done | bytes 1216544 | tf_op jit(solution)/shard_map/ppermute | solution.py:33
  127.0 12.0 %forward_late.1 = (bf16[1408,576]{1,0:T(8,128)(2,1)S(1)}, bf16[704,576]{1,0:T(8,128)(2,1)S(1)}, bf16[576,128]{1,0:T(8,128)(2,1)S(1)}) custom-call(bf16[576,576]{1,0:T(8,128)(2,1)S(1)} %fusion.15.matrix_ref.turn_ref, bf16[3,704,4096]{2,1,0:T(8,128)(2,1)S(1)} %bitcast.33, bf16[144,4096]{1,0:T(8,128)(2,1)S(1)} %collective-permute-done.4.refs_2_.refs_0_, ...), custom_call_target="tpu_custom_call" | custom-call | flops 3321888768 | bytes 20545536 | tf_op jit(solution)/shard_map/forward_late/pallas_call | solution.py:226
  139.0 18.2 %terms.1 = bf16[8,3,88,4096]{3,2,1,0:T(8,128)(2,1)} custom-call(bf16[1408,576]{1,0:T(8,128)(2,1)S(1)} %get-tuple-element.90.deltas_ref, bf16[704,576]{1,0:T(8,128)(2,1)S(1)} %get-tuple-element.116.hidden_ref, bf16[144,4096]{1,0:T(8,128)(2,1)S(1)} %get-tuple-element.86.refs_0_, bf16[144,4096]{1,0:T(8,128)(2,1)S(1)} %collective-permute-done.3.refs_1_, ...), custom_call_target="tpu_custom_call" | custom-call | flops 9965666304 | bytes 26738688 | tf_op jit(solution)/shard_map/terms/pallas_call | solution.py:274
  157.2 1.2 copy-done.3
  158.5 1.4 copy-done.4
  159.9 5.9 %copy-done.2 = bf16[1,704,3,4096]{3,1,2,0:T(8,128)(2,1)S(1)} copy-done((bf16[1,704,3,4096]{3,1,2,0:T(8,128)(2,1)S(1)}, bf16[1,704,3,4096]{3,1,2,0:T(8,128)(2,1)}, u32[]{:S(2)}) %copy-start.2) | copy-done | bytes 17301528
  165.8 6.4 %inputs.3 = (bf16[144,2048]{1,0:T(8,128)(2,1)S(1)}, bf16[144,2048]{1,0:T(8,128)(2,1)S(1)}, bf16[144,2048]{1,0:T(8,128)(2,1)S(1)}, bf16[144,2048]{1,0:T(8,128)(2,1)S(1)}) custom-call(bf16[576,576]{1,0:T(8,128)(2,1)S(1)} %fusion.15.matrix_ref.turn_ref, bf16[1408,576]{1,0:T(8,128)(2,1)S(1)} %copy-done.4, bf16[3,704,4096]{2,1,0:T(8,128)(2,1)S(1)} %bitcast.34, ...), custom_call_target="tpu_custom_call" | custom-call | flops 3321888768 | bytes 8126464 | tf_op jit(solution)/shard_map/inputs/pallas_call | solution.py:330
  172.2 3.8 %collective-permute-start.19 = (bf16[144,2048]{1,0:T(8,128)(2,1)S(1)}, bf16[144,2048]{1,0:T(8,128)(2,1)S(1)}, u32[]{:S(2)}, u32[]{:S(2)}) collective-permute-start(bf16[144,2048]{1,0:T(8,128)(2,1)S(1)} %get-tuple-element.106), channel_id=1, source_target_pairs={{0,12},{1,13},{2,14},{3,15},{4,0},{5,1},{6,2},{7,3},{8,4},{9,5},{1... | collective-permute-start | bytes 1769480 | tf_op jit(solution)/shard_map/ppermute | solution.py:33
  176.0 1.3 collective-permute-start.18
  177.4 6.4 %inputs.2 = (bf16[144,2176]{1,0:T(8,128)(2,1)S(1)}, bf16[144,2176]{1,0:T(8,128)(2,1)S(1)}, bf16[144,2176]{1,0:T(8,128)(2,1)S(1)}, bf16[144,2176]{1,0:T(8,128)(2,1)S(1)}) custom-call(bf16[576,576]{1,0:T(8,128)(2,1)S(1)} %fusion.14.turn_ref, bf16[1408,576]{1,0:T(8,128)(2,1)S(1)} %copy-done.4, bf16[3,704,4096]{2,1,0:T(8,128)(2,1)S(1)} %bitcast.35, ...), custom_call_target="tpu_custom_call" | custom-call | flops 3321888768 | bytes 8126464 | tf_op jit(solution)/shard_map/inputs/pallas_call | solution.py:330
  183.8 1.5 collective-permute-start.14
  185.2 2.2 collective-permute-done.19.refs_1_
  187.5 1.4 collective-permute-done.20.refs_2_
  189.0 11.0 %collective-permute-done.18.far_ref = bf16[144,2048]{1,0:T(8,128)(2,1)S(1)} collective-permute-done((bf16[144,2048]{1,0:T(8,128)(2,1)S(1)}, bf16[144,2048]{1,0:T(8,128)(2,1)S(1)}, u32[]{:S(2)}, u32[]{:S(2)}) %collective-permute-start.18) | collective-permute-done | bytes 589856 | tf_op jit(solution)/shard_map/ppermute | solution.py:33
  200.0 0.2 swap_far.7
  200.3 1.5 collective-permute-start.22
  201.8 0.8 collective-permute-start.23
  202.5 0.2 swap_near.6
  202.8 5.0 %collective-permute-done.12.far_ref = bf16[144,2176]{1,0:T(8,128)(2,1)S(1)} collective-permute-done((bf16[144,2176]{1,0:T(8,128)(2,1)S(1)}, bf16[144,2176]{1,0:T(8,128)(2,1)S(1)}, u32[]{:S(2)}, u32[]{:S(2)}) %collective-permute-start.12) | collective-permute-done | bytes 626720 | tf_op jit(solution)/shard_map/ppermute | solution.py:33
  207.8 0.2 swap_far.6
  208.0 1.8 collective-permute-start.15
  209.8 16.6 %collective-permute-done.21 = bf16[144,2048]{1,0:T(8,128)(2,1)S(1)} collective-permute-done((bf16[144,2048]{1,0:T(8,128)(2,1)S(1)}, bf16[144,2048]{1,0:T(8,128)(2,1)S(1)}, u32[]{:S(2)}, u32[]{:S(2)}) %collective-permute-start.21) | collective-permute-done | bytes 589856 | tf_op jit(solution)/shard_map/ppermute | solution.py:33
  226.6 3.9 %collective-permute-done.22 = bf16[144,2048]{1,0:T(8,128)(2,1)S(1)} collective-permute-done((bf16[144,2048]{1,0:T(8,128)(2,1)S(1)}, bf16[144,2048]{1,0:T(8,128)(2,1)S(1)}, u32[]{:S(2)}, u32[]{:S(2)}) %collective-permute-start.22) | collective-permute-done | bytes 589856 | tf_op jit(solution)/shard_map/ppermute | solution.py:33
  230.6 2.5 collective-permute-done.23
  233.1 1.0 convolution_convert_fusion.8
  234.2 8.1 %collective-permute-done.17 = bf16[144,2176]{1,0:T(8,128)(2,1)S(1)} collective-permute-done((bf16[144,2176]{1,0:T(8,128)(2,1)S(1)}, bf16[144,2176]{1,0:T(8,128)(2,1)S(1)}, u32[]{:S(2)}, u32[]{:S(2)}) %collective-permute-start.17) | collective-permute-done | bytes 626720 | tf_op jit(solution)/shard_map/ppermute | solution.py:33
  242.9 1.2 select_reduce_fusion
  244.0 1.0 convolution_convert_fusion.9
  245.1 1.2 pad_maximum_fusion
  246.3 12.5 %reduce-scatter.2.cloned.1.call-done.in_ref = bf16[1,3,88,4096]{3,2,1,0:T(8,128)(2,1)} async-done(((bf16[8,3,88,4096]{3,2,1,0:T(8,128)(2,1)}), bf16[1,3,88,4096]{3,2,1,0:T(8,128)(2,1)}) %reduce-scatter.2.cloned.1.call-update) | async-done | bytes 2162704 | tf_op jit(solution)/shard_map/reduce_scatter | solution.py:417
  258.8 5.3 %widen.1 = f32[1,3,88,4096]{3,2,1,0:T(8,128)} custom-call(bf16[1,3,88,4096]{3,2,1,0:T(8,128)(2,1)} %reduce-scatter.2.cloned.1.call-done.in_ref), custom_call_target="tpu_custom_call" | custom-call | bytes 6488064 | tf_op jit(solution)/shard_map/widen/pallas_call | solution.py:296
  (70 shorter events, 2.5 us)
Async XLA Ops:
  7.2 3.1 %copy-start = (bf16[192,4096]{1,0:T(8,128)(2,1)S(1)}, bf16[192,4096]{1,0:T(8,128)(2,1)}, u32[]{:S(2)}) copy-start(bf16[192,4096]{1,0:T(8,128)(2,1)} %param.6) | copy-start | bytes 4718596
  7.2 251.6 %reduce-scatter.2.cloned.1.call-start = ((), (), s32[]{:S(2)}) async-start(), calls=%async_computation.1 | async-start | bytes 19464192 | tf_op jit(solution)/shard_map/reduce_scatter | solution.py:417
  11.1 29.4 %collective-permute-start.6 = (bf16[144,4224]{1,0:T(8,128)(2,1)S(1)}, bf16[144,4224]{1,0:T(8,128)(2,1)S(1)}, u32[]{:S(2)}, u32[]{:S(2)}) collective-permute-start(bf16[144,4224]{1,0:T(8,128)(2,1)S(1)} %pad_maximum_fusion.2), channel_id=1, source_target_pairs={{0,1},{1,2},{2,3},{3,0},{4,5},{5,6},{6,7},{7,4},{8,9},{9,10},{10,1... | collective-permute-start | bytes 3649544 | tf_op jit(solution)/shard_map/ppermute | solution.py:33
  13.7 1.6 copy-start.5
  13.9 27.4 %collective-permute-start.7 = (bf16[144,4224]{1,0:T(8,128)(2,1)S(1)}, bf16[144,4224]{1,0:T(8,128)(2,1)S(1)}, u32[]{:S(2)}, u32[]{:S(2)}) collective-permute-start(bf16[144,4224]{1,0:T(8,128)(2,1)S(1)} %pad_maximum_fusion.3), channel_id=1, source_target_pairs={{0,3},{1,0},{2,1},{3,2},{4,7},{5,4},{6,5},{7,6},{8,11},{9,8},{10,9... | collective-permute-start | bytes 3649544 | tf_op jit(solution)/shard_map/ppermute | solution.py:33
  15.8 28.6 %collective-permute-start.1 = (bf16[144,4096]{1,0:T(8,128)(2,1)S(1)}, bf16[144,4096]{1,0:T(8,128)(2,1)S(1)}, u32[]{:S(2)}, u32[]{:S(2)}) collective-permute-start(bf16[144,4096]{1,0:T(8,128)(2,1)S(1)} %convolution_convert_fusion.5), channel_id=1, source_target_pairs={{0,12},{1,13},{2,14},{3,15},{4,0},{5,1},{6,2},{7,3},{8,4},{9,5},{1... | collective-permute-start | bytes 3538952 | tf_op jit(solution)/shard_map/ppermute | solution.py:33
  20.4 27.2 %collective-permute-start = (bf16[144,4096]{1,0:T(8,128)(2,1)S(1)}, bf16[144,4096]{1,0:T(8,128)(2,1)S(1)}, u32[]{:S(2)}, u32[]{:S(2)}) collective-permute-start(bf16[144,4096]{1,0:T(8,128)(2,1)S(1)} %convolution_convert_fusion.6), channel_id=1, source_target_pairs={{0,4},{1,5},{2,6},{3,7},{4,8},{5,9},{6,10},{7,11},{8,12},{9,13},{1... | collective-permute-start | bytes 3538952 | tf_op jit(solution)/shard_map/ppermute | solution.py:33
  41.3 27.9 %collective-permute-start.8 = (bf16[144,4224]{1,0:T(8,128)(2,1)S(1)}, bf16[144,4224]{1,0:T(8,128)(2,1)S(1)}, u32[]{:S(2)}, u32[]{:S(2)}) collective-permute-start(bf16[144,4224]{1,0:T(8,128)(2,1)S(1)} %pad_maximum_fusion.1), channel_id=1, source_target_pairs={{0,2},{1,3},{2,0},{3,1},{4,6},{5,7},{6,4},{7,5},{8,10},{9,11},{10,... | collective-permute-start | bytes 3649544 | tf_op jit(solution)/shard_map/ppermute | solution.py:33
  43.8 59.8 %slice-start = ((s8[17301504]{0:T(1024)(128)(4,1)}), s8[4194304]{0:T(1024)(128)(4,1)S(1)}, s32[]{:S(2)}) async-start(s8[17301504]{0:T(1024)(128)(4,1)} %bitcast.30), calls=%async_computation.2 | async-start | bytes 8388608
  47.6 27.0 %collective-permute-start.2 = (bf16[144,4096]{1,0:T(8,128)(2,1)S(1)}, bf16[144,4096]{1,0:T(8,128)(2,1)S(1)}, u32[]{:S(2)}, u32[]{:S(2)}) collective-permute-start(bf16[144,4096]{1,0:T(8,128)(2,1)S(1)} %convolution_convert_fusion.7), channel_id=1, source_target_pairs={{0,8},{1,9},{2,10},{3,11},{4,12},{5,13},{6,14},{7,15},{8,0},{9,1},... | collective-permute-start | bytes 3538952 | tf_op jit(solution)/shard_map/ppermute | solution.py:33
  48.7 54.9 %slice-start.1 = ((s8[17301504]{0:T(1024)(128)(4,1)}), s8[4194304]{0:T(1024)(128)(4,1)S(1)}, s32[]{:S(2)}) async-start(s8[17301504]{0:T(1024)(128)(4,1)} %bitcast.30), calls=%async_computation.3 | async-start | bytes 8388608
  69.2 34.5 %slice-start.2 = ((s8[17301504]{0:T(1024)(128)(4,1)}), s8[4194304]{0:T(1024)(128)(4,1)S(1)}, s32[]{:S(2)}) async-start(s8[17301504]{0:T(1024)(128)(4,1)} %bitcast.30), calls=%async_computation.4 | async-start | bytes 8388608
  69.5 30.2 %collective-permute-start.10 = (bf16[144,4224]{1,0:T(8,128)(2,1)S(1)}, bf16[144,4224]{1,0:T(8,128)(2,1)S(1)}, u32[]{:S(2)}, u32[]{:S(2)}) collective-permute-start(bf16[144,4224]{1,0:T(8,128)(2,1)S(1)} %get-tuple-element.81), channel_id=1, source_target_pairs={{0,12},{1,13},{2,14},{3,15},{4,0},{5,1},{6,2},{7,3},{8,4},{9,5},{1... | collective-permute-start | bytes 3649544 | tf_op jit(solution)/shard_map/ppermute | solution.py:33
  73.4 30.3 %slice-start.3 = ((s8[17301504]{0:T(1024)(128)(4,1)}), s8[4194304]{0:T(1024)(128)(4,1)S(1)}, s32[]{:S(2)}) async-start(s8[17301504]{0:T(1024)(128)(4,1)} %bitcast.30), calls=%async_computation.5 | async-start | bytes 8388608
  73.4 27.4 %collective-permute-start.9 = (bf16[144,4224]{1,0:T(8,128)(2,1)S(1)}, bf16[144,4224]{1,0:T(8,128)(2,1)S(1)}, u32[]{:S(2)}, u32[]{:S(2)}) collective-permute-start(bf16[144,4224]{1,0:T(8,128)(2,1)S(1)} %get-tuple-element.80), channel_id=1, source_target_pairs={{0,4},{1,5},{2,6},{3,7},{4,8},{5,9},{6,10},{7,11},{8,12},{9,13},{1... | collective-permute-start | bytes 3649544 | tf_op jit(solution)/shard_map/ppermute | solution.py:33
  74.6 29.1 %slice-start.4 = ((s8[17301504]{0:T(1024)(128)(4,1)}), s8[524288]{0:T(1024)(128)(4,1)S(1)}, s32[]{:S(2)}) async-start(s8[17301504]{0:T(1024)(128)(4,1)} %bitcast.30), calls=%async_computation.6 | async-start | bytes 1048576
  75.3 26.6 %collective-permute-start.3 = (bf16[144,4096]{1,0:T(8,128)(2,1)S(1)}, bf16[144,4096]{1,0:T(8,128)(2,1)S(1)}, u32[]{:S(2)}, u32[]{:S(2)}) collective-permute-start(bf16[144,4096]{1,0:T(8,128)(2,1)S(1)} %get-tuple-element.68), channel_id=1, source_target_pairs={{0,1},{1,2},{2,3},{3,0},{4,5},{5,6},{6,7},{7,4},{8,9},{9,10},{10,1... | collective-permute-start | bytes 3538952 | tf_op jit(solution)/shard_map/ppermute | solution.py:33
  76.6 25.3 %collective-permute-start.4 = (bf16[144,4096]{1,0:T(8,128)(2,1)S(1)}, bf16[144,4096]{1,0:T(8,128)(2,1)S(1)}, u32[]{:S(2)}, u32[]{:S(2)}) collective-permute-start(bf16[144,4096]{1,0:T(8,128)(2,1)S(1)} %get-tuple-element.69), channel_id=1, source_target_pairs={{0,3},{1,0},{2,1},{3,2},{4,7},{5,4},{6,5},{7,6},{8,11},{9,8},{10,9... | collective-permute-start | bytes 3538952 | tf_op jit(solution)/shard_map/ppermute | solution.py:33
  100.7 26.3 %collective-permute-start.11 = (bf16[144,4224]{1,0:T(8,128)(2,1)S(1)}, bf16[144,4224]{1,0:T(8,128)(2,1)S(1)}, u32[]{:S(2)}, u32[]{:S(2)}) collective-permute-start(bf16[144,4224]{1,0:T(8,128)(2,1)S(1)} %get-tuple-element.83), channel_id=1, source_target_pairs={{0,8},{1,9},{2,10},{3,11},{4,12},{5,13},{6,14},{7,15},{8,0},{9,1},... | collective-permute-start | bytes 3649544 | tf_op jit(solution)/shard_map/ppermute | solution.py:33
  101.9 16.9 %collective-permute-start.5 = (bf16[144,4096]{1,0:T(8,128)(2,1)S(1)}, bf16[144,4096]{1,0:T(8,128)(2,1)S(1)}, u32[]{:S(2)}, u32[]{:S(2)}) collective-permute-start(bf16[144,4096]{1,0:T(8,128)(2,1)S(1)} %get-tuple-element.71), channel_id=1, source_target_pairs={{0,2},{1,3},{2,0},{3,1},{4,6},{5,7},{6,4},{7,5},{8,10},{9,11},{10,... | collective-permute-start | bytes 3538952 | tf_op jit(solution)/shard_map/ppermute | solution.py:33
  157.2 1.2 copy-start.3
  158.4 1.5 copy-start.4
  159.9 5.9 %copy-start.2 = (bf16[1,704,3,4096]{3,1,2,0:T(8,128)(2,1)S(1)}, bf16[1,704,3,4096]{3,1,2,0:T(8,128)(2,1)}, u32[]{:S(2)}) copy-start(bf16[1,704,3,4096]{3,1,2,0:T(8,128)(2,1)} %param.9) | copy-start | bytes 51904516
  172.2 15.3 %collective-permute-start.19 = (bf16[144,2048]{1,0:T(8,128)(2,1)S(1)}, bf16[144,2048]{1,0:T(8,128)(2,1)S(1)}, u32[]{:S(2)}, u32[]{:S(2)}) collective-permute-start(bf16[144,2048]{1,0:T(8,128)(2,1)S(1)} %get-tuple-element.106), channel_id=1, source_target_pairs={{0,12},{1,13},{2,14},{3,15},{4,0},{5,1},{6,2},{7,3},{8,4},{9,5},{1... | collective-permute-start | bytes 1769480 | tf_op jit(solution)/shard_map/ppermute | solution.py:33
  176.0 12.9 %collective-permute-start.20 = (bf16[144,2048]{1,0:T(8,128)(2,1)S(1)}, bf16[144,2048]{1,0:T(8,128)(2,1)S(1)}, u32[]{:S(2)}, u32[]{:S(2)}) collective-permute-start(bf16[144,2048]{1,0:T(8,128)(2,1)S(1)} %get-tuple-element.107), channel_id=1, source_target_pairs={{0,4},{1,5},{2,6},{3,7},{4,8},{5,9},{6,10},{7,11},{8,12},{9,13},{1... | collective-permute-start | bytes 1769480 | tf_op jit(solution)/shard_map/ppermute | solution.py:33
  176.0 24.0 %collective-permute-start.18 = (bf16[144,2048]{1,0:T(8,128)(2,1)S(1)}, bf16[144,2048]{1,0:T(8,128)(2,1)S(1)}, u32[]{:S(2)}, u32[]{:S(2)}) collective-permute-start(bf16[144,2048]{1,0:T(8,128)(2,1)S(1)} %get-tuple-element.104), channel_id=1, source_target_pairs={{0,8},{1,9},{2,10},{3,11},{4,12},{5,13},{6,14},{7,15},{8,0},{9,1},... | collective-permute-start | bytes 1769480 | tf_op jit(solution)/shard_map/ppermute | solution.py:33
  183.7 18.1 %collective-permute-start.13 = (bf16[144,2176]{1,0:T(8,128)(2,1)S(1)}, bf16[144,2176]{1,0:T(8,128)(2,1)S(1)}, u32[]{:S(2)}, u32[]{:S(2)}) collective-permute-start(bf16[144,2176]{1,0:T(8,128)(2,1)S(1)} %get-tuple-element.94), channel_id=1, source_target_pairs={{0,3},{1,0},{2,1},{3,2},{4,7},{5,4},{6,5},{7,6},{8,11},{9,8},{10,9... | collective-permute-start | bytes 1880072 | tf_op jit(solution)/shard_map/ppermute | solution.py:33
  183.8 18.7 %collective-permute-start.14 = (bf16[144,2176]{1,0:T(8,128)(2,1)S(1)}, bf16[144,2176]{1,0:T(8,128)(2,1)S(1)}, u32[]{:S(2)}, u32[]{:S(2)}) collective-permute-start(bf16[144,2176]{1,0:T(8,128)(2,1)S(1)} %get-tuple-element.95), channel_id=1, source_target_pairs={{0,1},{1,2},{2,3},{3,0},{4,5},{5,6},{6,7},{7,4},{8,9},{9,10},{10,1... | collective-permute-start | bytes 1880072 | tf_op jit(solution)/shard_map/ppermute | solution.py:33
  187.5 20.3 %collective-permute-start.12 = (bf16[144,2176]{1,0:T(8,128)(2,1)S(1)}, bf16[144,2176]{1,0:T(8,128)(2,1)S(1)}, u32[]{:S(2)}, u32[]{:S(2)}) collective-permute-start(bf16[144,2176]{1,0:T(8,128)(2,1)S(1)} %get-tuple-element.92), channel_id=1, source_target_pairs={{0,2},{1,3},{2,0},{3,1},{4,6},{5,7},{6,4},{7,5},{8,10},{9,11},{10,... | collective-permute-start | bytes 1880072 | tf_op jit(solution)/shard_map/ppermute | solution.py:33
  200.2 26.2 %collective-permute-start.21 = (bf16[144,2048]{1,0:T(8,128)(2,1)S(1)}, bf16[144,2048]{1,0:T(8,128)(2,1)S(1)}, u32[]{:S(2)}, u32[]{:S(2)}) collective-permute-start(bf16[144,2048]{1,0:T(8,128)(2,1)S(1)} %get-tuple-element.113), channel_id=1, source_target_pairs={{0,3},{1,0},{2,1},{3,2},{4,7},{5,4},{6,5},{7,6},{8,11},{9,8},{10,9... | collective-permute-start | bytes 1769480 | tf_op jit(solution)/shard_map/ppermute | solution.py:33
  200.3 30.3 %collective-permute-start.22 = (bf16[144,2048]{1,0:T(8,128)(2,1)S(1)}, bf16[144,2048]{1,0:T(8,128)(2,1)S(1)}, u32[]{:S(2)}, u32[]{:S(2)}) collective-permute-start(bf16[144,2048]{1,0:T(8,128)(2,1)S(1)} %get-tuple-element.114), channel_id=1, source_target_pairs={{0,1},{1,2},{2,3},{3,0},{4,5},{5,6},{6,7},{7,4},{8,9},{9,10},{10,1... | collective-permute-start | bytes 1769480 | tf_op jit(solution)/shard_map/ppermute | solution.py:33
  201.8 31.3 %collective-permute-start.23 = (bf16[144,2048]{1,0:T(8,128)(2,1)S(1)}, bf16[144,2048]{1,0:T(8,128)(2,1)S(1)}, u32[]{:S(2)}, u32[]{:S(2)}) collective-permute-start(bf16[144,2048]{1,0:T(8,128)(2,1)S(1)} %get-tuple-element.115), channel_id=1, source_target_pairs={{0,2},{1,3},{2,0},{3,1},{4,6},{5,7},{6,4},{7,5},{8,10},{9,11},{10,... | collective-permute-start | bytes 1769480 | tf_op jit(solution)/shard_map/ppermute | solution.py:33
  208.0 26.1 %collective-permute-start.15 = (bf16[144,2176]{1,0:T(8,128)(2,1)S(1)}, bf16[144,2176]{1,0:T(8,128)(2,1)S(1)}, u32[]{:S(2)}, u32[]{:S(2)}) collective-permute-start(bf16[144,2176]{1,0:T(8,128)(2,1)S(1)} %get-tuple-element.101), channel_id=1, source_target_pairs={{0,12},{1,13},{2,14},{3,15},{4,0},{5,1},{6,2},{7,3},{8,4},{9,5},{1... | collective-permute-start | bytes 1880072 | tf_op jit(solution)/shard_map/ppermute | solution.py:33
  209.8 24.4 %collective-permute-start.16 = (bf16[144,2176]{1,0:T(8,128)(2,1)S(1)}, bf16[144,2176]{1,0:T(8,128)(2,1)S(1)}, u32[]{:S(2)}, u32[]{:S(2)}) collective-permute-start(bf16[144,2176]{1,0:T(8,128)(2,1)S(1)} %get-tuple-element.102), channel_id=1, source_target_pairs={{0,4},{1,5},{2,6},{3,7},{4,8},{5,9},{6,10},{7,11},{8,12},{9,13},{1... | collective-permute-start | bytes 1880072 | tf_op jit(solution)/shard_map/ppermute | solution.py:33
  226.5 15.9 %collective-permute-start.17 = (bf16[144,2176]{1,0:T(8,128)(2,1)S(1)}, bf16[144,2176]{1,0:T(8,128)(2,1)S(1)}, u32[]{:S(2)}, u32[]{:S(2)}) collective-permute-start(bf16[144,2176]{1,0:T(8,128)(2,1)S(1)} %get-tuple-element.103), channel_id=1, source_target_pairs={{0,8},{1,9},{2,10},{3,11},{4,12},{5,13},{6,14},{7,15},{8,0},{9,1},... | collective-permute-start | bytes 1880072 | tf_op jit(solution)/shard_map/ppermute | solution.py:33
  258.8 5.3 %copy-start.1 = (bf16[192,4096]{1,0:T(8,128)(2,1)S(1)}, bf16[192,4096]{1,0:T(8,128)(2,1)}, u32[]{:S(2)}) copy-start(bf16[192,4096]{1,0:T(8,128)(2,1)} %param.6) | copy-start | bytes 4718596
Sparse Core Ops, SparseCore 0:
  158.6 100.1 reduce-scatter.1

commit v4 on v3

--- a/solution.py
+++ b/solution.py
@@ -16,7 +16,7 @@
 MAIN = 32
 TAIL = CAP - MAIN
 EARLY = 384
-LIMITS = {"swap": 16, "early": 16, "late": 16, "terms": 16, "inputs": 16, "widen": 56}
+LIMITS = {"swap": 16, "early": 16, "late": 16, "terms": 16, "inputs": 16}
 
 
 def hop(dz, dx):
@@ -285,26 +285,6 @@
     )(deltas, hidden, *toks, *cots, *cots)
 
 
-def widen_kernel(in_ref, out_ref):
-    out_ref[0, 0] = in_ref[0, 0].astype(jnp.float32)
-
-
-def widen(summed):
-    _, kinds, share, width = summed.shape
-    tile = width // 2
-    spec = pl.BlockSpec((1, 1, share, tile), lambda i: (0, i // 2, 0, i % 2))
-    return pl.pallas_call(
-        widen_kernel,
-        grid=(2 * kinds,),
-        in_specs=[spec],
-        out_specs=spec,
-        out_shape=jax.ShapeDtypeStruct(summed.shape, jnp.float32),
-        compiler_params=params("widen"),
-        cost_estimate=cost(0, 6 * kinds * share * width),
-        name="widen",
-    )(summed)
-
-
 def inputs_kernel(tile, turn_ref, deltas_ref, weight_ref, route_ref, *refs):
     outs, delta_rows = refs[:SIDE], refs[SIDE]
     step = pl.program_id(0)
@@ -415,7 +395,7 @@
     deltas, hidden, route = forward_late(turn, weights, toks, cots, early)
     partial_sums = terms(deltas, hidden, toks, cots, owners)
     summed = lax.psum_scatter(partial_sums, "dp", scatter_dimension=0, tiled=True)
-    weight_grad = widen(summed).transpose(0, 2, 1, 3)
+    weight_grad = summed.astype(jnp.float32).transpose(0, 2, 1, 3)
 
     right = inputs(turn, deltas, weights, route, half, half, 0)
     left = inputs(same, deltas, weights, route, 0, half, EXTRA)

time: 271 us -> 270 us (level)
  Pallas kernels: 64.7 us -> 59.4 us
  other arithmetic: 6.06 us -> 10.4 us
    pallas_call x1 -> x0, Pallas kernels: 5.27 us -> none  [widen(): pl.pallas_call(widen_kernel, grid=(2 * kinds,), in_specs=[spec], out_spec...]
    transpose x0 -> x1, other arithmetic: none -> 4.3 us  [shards(): weight_grad = summed.astype(jnp.float32).transpose(0, 2, 1, 3)]
where the time goes in v4:
time: 270 us
  waiting for transfers between devices  139 us (51%)
  Pallas kernels  59.4 us (22%)
  starting transfers between devices  30.6 us (11%)
  between operations  14.6 us (5%)
  other arithmetic  10.4 us (4%)
  local copies, waits for them, and re-layouts  9.59 us (4%)
  matrix products  6.56 us (2%)
    ppermute x24, waiting for transfers between devices, move(): lax.ppermute(value, 'expert', hop(step, 0) if axis == 'z' else hop(0, step))  126 us
    ppermute x24, starting transfers between devices, move(): lax.ppermute(value, 'expert', hop(step, 0) if axis == 'z' else hop(0, step))  30.6 us
    pallas_call x1, Pallas kernels, terms(): pl.pallas_call(terms_kernel, grid=(width // tile,), in_specs=[pl.BlockSpe...  18.2 us
    pallas_call x1, Pallas kernels, forward_early(): pl.pallas_call(early_kernel, grid=(width // tile,), in_specs=[pl.BlockSpe...  13.7 us
    pallas_call x2, Pallas kernels, inputs(): pl.pallas_call(functools.partial(inputs_kernel, tile), grid=(count // til...  12.7 us
    reduce_scatter x1, waiting for transfers between devices, shards(): lax.psum_scatter(partial_sums, 'dp', scatter_dimension=0, tiled=True)  12.5 us
    pallas_call x1, Pallas kernels, forward_late(): pl.pallas_call(functools.partial(late_kernel, steps), grid=(steps,), in_s...  12 us
    unnamed x22, local copies, waits for them, and re-layouts  8.58 us
  transfers between devices with their start and end apart: 25, of which 17 were waited for; matrix products, arithmetic and copies ran while one was open for 4% of the time, Pallas kernels for 11%

profile of v4, /device:TPU:1, one launch (start us, length us, event | category | flops | bytes accessed | tf_op | source)
XLA Modules:
  0.0 270.0 jit_solution(13427204090815409854)
XLA Ops:
  7.3 0.8 fusion.118
  8.3 0.7 select_reduce_fusion.5
  9.1 1.2 select_reduce_fusion.1
  10.3 0.6 convolution_convert_fusion.2
  11.1 2.1 collective-permute-start.6
  13.2 0.6 convolution_convert_fusion.1
  13.9 1.4 collective-permute-start.7
  15.3 0.6 convolution_convert_fusion.5
  15.8 4.0 %collective-permute-start.1 = (bf16[144,4096]{1,0:T(8,128)(2,1)S(1)}, bf16[144,4096]{1,0:T(8,128)(2,1)S(1)}, u32[]{:S(2)}, u32[]{:S(2)}) collective-permute-start(bf16[144,4096]{1,0:T(8,128)(2,1)S(1)} %convolution_convert_fusion.5), channel_id=1, source_target_pairs={{0,12},{1,13},{2,14},{3,15},{4,0},{5,1},{6,2},{7,3},{8,4},{9,5},{1... | collective-permute-start | bytes 3538952 | tf_op jit(solution)/shard_map/ppermute | solution.py:33
  19.9 0.6 convolution_convert_fusion.6
  20.5 0.6 convolution_convert_fusion.3
  21.3 19.2 %collective-permute-done.6.refs_1_ = bf16[144,4224]{1,0:T(8,128)(2,1)S(1)} collective-permute-done((bf16[144,4224]{1,0:T(8,128)(2,1)S(1)}, bf16[144,4224]{1,0:T(8,128)(2,1)S(1)}, u32[]{:S(2)}, u32[]{:S(2)}) %collective-permute-start.6) | collective-permute-done | bytes 1216544 | tf_op jit(solution)/shard_map/ppermute | solution.py:33
  40.5 0.8 collective-permute-done.7.refs_2_
  41.3 2.5 collective-permute-start.8
  43.8 0.6 convolution_convert_fusion.7
  44.4 3.2 %collective-permute-done.refs_1_ = bf16[144,4096]{1,0:T(8,128)(2,1)S(1)} collective-permute-done((bf16[144,4096]{1,0:T(8,128)(2,1)S(1)}, bf16[144,4096]{1,0:T(8,128)(2,1)S(1)}, u32[]{:S(2)}, u32[]{:S(2)}) %collective-permute-start) | collective-permute-done | bytes 1179680 | tf_op jit(solution)/shard_map/ppermute | solution.py:33
  47.6 0.5 collective-permute-start.2
  48.1 0.5 convolution_convert_fusion
  48.8 0.4 swap_near.5
  49.2 19.9 %collective-permute-done.8.far_ref = bf16[144,4224]{1,0:T(8,128)(2,1)S(1)} collective-permute-done((bf16[144,4224]{1,0:T(8,128)(2,1)S(1)}, bf16[144,4224]{1,0:T(8,128)(2,1)S(1)}, u32[]{:S(2)}, u32[]{:S(2)}) %collective-permute-start.8) | collective-permute-done | bytes 1216544 | tf_op jit(solution)/shard_map/ppermute | solution.py:33
  69.2 0.3 swap_far.5
  69.5 3.8 %collective-permute-start.10 = (bf16[144,4224]{1,0:T(8,128)(2,1)S(1)}, bf16[144,4224]{1,0:T(8,128)(2,1)S(1)}, u32[]{:S(2)}, u32[]{:S(2)}) collective-permute-start(bf16[144,4224]{1,0:T(8,128)(2,1)S(1)} %get-tuple-element.81), channel_id=1, source_target_pairs={{0,12},{1,13},{2,14},{3,15},{4,0},{5,1},{6,2},{7,3},{8,4},{9,5},{1... | collective-permute-start | bytes 3649544 | tf_op jit(solution)/shard_map/ppermute | solution.py:33
  73.4 0.5 convolution_convert_fusion.4.refs_0_
  73.9 0.7 swap_near.4
  74.6 0.7 swap_far.4
  75.3 1.3 collective-permute-start.3
  76.6 1.5 collective-permute-start.4
  78.1 21.6 %collective-permute-done.10.refs_5_.refs_2_.refs_6_.refs_10_ = bf16[144,4224]{1,0:T(8,128)(2,1)S(1)} collective-permute-done((bf16[144,4224]{1,0:T(8,128)(2,1)S(1)}, bf16[144,4224]{1,0:T(8,128)(2,1)S(1)}, u32[]{:S(2)}, u32[]{:S(2)}) %collective-permute-start.10) | collective-permute-done | bytes 1216544 | tf_op jit(solution)/shard_map/ppermute | solution.py:33
  99.8 1.0 collective-permute-done.9.refs_4_.refs_5_.refs_9_
  100.7 1.2 collective-permute-start.11
  101.9 1.5 collective-permute-start.5
  103.7 13.7 %forward_early.1 = (f32[1408,384]{1,0:T(8,128)S(1)}, f32[704,384]{1,0:T(8,128)S(1)}) custom-call(bf16[3,704,4096]{2,1,0:T(8,128)(2,1)S(1)} %bitcast.33, bf16[144,4096]{1,0:T(8,128)(2,1)S(1)} %get-tuple-element.86.refs_0_, bf16[144,4096]{1,0:T(8,128)(2,1)S(1)} %collective-permute-done.3.refs_1_, bf16[144,4096]{1,0:T(8,128)(2,1)S(1)} %collective-permute-done.4.refs_2_.refs_0_, ...), custom_call_target="tpu_custom_call" | custom-call | flops 6643777536 | bytes 23592960 | tf_op jit(solution)/shard_map/forward_early/pallas_call | solution.py:156
  117.4 1.4 collective-permute-done.5.refs_1_.refs_3_
  118.8 8.2 %collective-permute-done.11.refs_3_.refs_7_.refs_11_ = bf16[144,4224]{1,0:T(8,128)(2,1)S(1)} collective-permute-done((bf16[144,4224]{1,0:T(8,128)(2,1)S(1)}, bf16[144,4224]{1,0:T(8,128)(2,1)S(1)}, u32[]{:S(2)}, u32[]{:S(2)}) %collective-permute-start.11) | collective-permute-done | bytes 1216544 | tf_op jit(solution)/shard_map/ppermute | solution.py:33
  127.0 12.0 %forward_late.1 = (bf16[1408,576]{1,0:T(8,128)(2,1)S(1)}, bf16[704,576]{1,0:T(8,128)(2,1)S(1)}, bf16[576,128]{1,0:T(8,128)(2,1)S(1)}) custom-call(bf16[576,576]{1,0:T(8,128)(2,1)S(1)} %fusion.15.matrix_ref.turn_ref, bf16[3,704,4096]{2,1,0:T(8,128)(2,1)S(1)} %bitcast.34, bf16[144,4096]{1,0:T(8,128)(2,1)S(1)} %collective-permute-done.4.refs_2_.refs_0_, ...), custom_call_target="tpu_custom_call" | custom-call | flops 3321888768 | bytes 20545536 | tf_op jit(solution)/shard_map/forward_late/pallas_call | solution.py:226
  139.0 18.2 %terms.1 = bf16[8,3,88,4096]{3,2,1,0:T(8,128)(2,1)} custom-call(bf16[1408,576]{1,0:T(8,128)(2,1)S(1)} %get-tuple-element.90.deltas_ref, bf16[704,576]{1,0:T(8,128)(2,1)S(1)} %get-tuple-element.116.hidden_ref, bf16[144,4096]{1,0:T(8,128)(2,1)S(1)} %get-tuple-element.86.refs_0_, bf16[144,4096]{1,0:T(8,128)(2,1)S(1)} %collective-permute-done.3.refs_1_, ...), custom_call_target="tpu_custom_call" | custom-call | flops 9965666304 | bytes 26738688 | tf_op jit(solution)/shard_map/terms/pallas_call | solution.py:274
  157.2 1.2 copy-done.3
  158.5 1.4 copy-done.4
  159.9 5.9 %copy-done.2 = bf16[1,704,3,4096]{3,1,2,0:T(8,128)(2,1)S(1)} copy-done((bf16[1,704,3,4096]{3,1,2,0:T(8,128)(2,1)S(1)}, bf16[1,704,3,4096]{3,1,2,0:T(8,128)(2,1)}, u32[]{:S(2)}) %copy-start.2) | copy-done | bytes 17301528
  165.8 6.4 %inputs.3 = (bf16[144,2048]{1,0:T(8,128)(2,1)S(1)}, bf16[144,2048]{1,0:T(8,128)(2,1)S(1)}, bf16[144,2048]{1,0:T(8,128)(2,1)S(1)}, bf16[144,2048]{1,0:T(8,128)(2,1)S(1)}) custom-call(bf16[576,576]{1,0:T(8,128)(2,1)S(1)} %fusion.15.matrix_ref.turn_ref, bf16[1408,576]{1,0:T(8,128)(2,1)S(1)} %copy-done.4, bf16[3,704,4096]{2,1,0:T(8,128)(2,1)S(1)} %bitcast.35, ...), custom_call_target="tpu_custom_call" | custom-call | flops 3321888768 | bytes 8126464 | tf_op jit(solution)/shard_map/inputs/pallas_call | solution.py:310
  172.2 3.8 %collective-permute-start.19 = (bf16[144,2048]{1,0:T(8,128)(2,1)S(1)}, bf16[144,2048]{1,0:T(8,128)(2,1)S(1)}, u32[]{:S(2)}, u32[]{:S(2)}) collective-permute-start(bf16[144,2048]{1,0:T(8,128)(2,1)S(1)} %get-tuple-element.106), channel_id=1, source_target_pairs={{0,12},{1,13},{2,14},{3,15},{4,0},{5,1},{6,2},{7,3},{8,4},{9,5},{1... | collective-permute-start | bytes 1769480 | tf_op jit(solution)/shard_map/ppermute | solution.py:33
  176.0 1.3 collective-permute-start.18
  177.4 6.4 %inputs.2 = (bf16[144,2176]{1,0:T(8,128)(2,1)S(1)}, bf16[144,2176]{1,0:T(8,128)(2,1)S(1)}, bf16[144,2176]{1,0:T(8,128)(2,1)S(1)}, bf16[144,2176]{1,0:T(8,128)(2,1)S(1)}) custom-call(bf16[576,576]{1,0:T(8,128)(2,1)S(1)} %fusion.14.turn_ref, bf16[1408,576]{1,0:T(8,128)(2,1)S(1)} %copy-done.4, bf16[3,704,4096]{2,1,0:T(8,128)(2,1)S(1)} %bitcast.36, ...), custom_call_target="tpu_custom_call" | custom-call | flops 3321888768 | bytes 8126464 | tf_op jit(solution)/shard_map/inputs/pallas_call | solution.py:310
  183.8 1.5 collective-permute-start.14
  185.2 2.2 collective-permute-done.19.refs_1_
  187.5 1.4 collective-permute-done.20.refs_2_
  189.0 11.0 %collective-permute-done.18.far_ref = bf16[144,2048]{1,0:T(8,128)(2,1)S(1)} collective-permute-done((bf16[144,2048]{1,0:T(8,128)(2,1)S(1)}, bf16[144,2048]{1,0:T(8,128)(2,1)S(1)}, u32[]{:S(2)}, u32[]{:S(2)}) %collective-permute-start.18) | collective-permute-done | bytes 589856 | tf_op jit(solution)/shard_map/ppermute | solution.py:33
  200.0 0.2 swap_far.7
  200.3 1.5 collective-permute-start.22
  201.8 0.8 collective-permute-start.23
  202.5 0.2 swap_near.6
  202.8 5.0 %collective-permute-done.12.far_ref = bf16[144,2176]{1,0:T(8,128)(2,1)S(1)} collective-permute-done((bf16[144,2176]{1,0:T(8,128)(2,1)S(1)}, bf16[144,2176]{1,0:T(8,128)(2,1)S(1)}, u32[]{:S(2)}, u32[]{:S(2)}) %collective-permute-start.12) | collective-permute-done | bytes 626720 | tf_op jit(solution)/shard_map/ppermute | solution.py:33
  207.8 0.2 swap_far.6
  208.0 1.8 collective-permute-start.15
  209.8 16.6 %collective-permute-done.21 = bf16[144,2048]{1,0:T(8,128)(2,1)S(1)} collective-permute-done((bf16[144,2048]{1,0:T(8,128)(2,1)S(1)}, bf16[144,2048]{1,0:T(8,128)(2,1)S(1)}, u32[]{:S(2)}, u32[]{:S(2)}) %collective-permute-start.21) | collective-permute-done | bytes 589856 | tf_op jit(solution)/shard_map/ppermute | solution.py:33
  226.6 3.9 %collective-permute-done.22 = bf16[144,2048]{1,0:T(8,128)(2,1)S(1)} collective-permute-done((bf16[144,2048]{1,0:T(8,128)(2,1)S(1)}, bf16[144,2048]{1,0:T(8,128)(2,1)S(1)}, u32[]{:S(2)}, u32[]{:S(2)}) %collective-permute-start.22) | collective-permute-done | bytes 589856 | tf_op jit(solution)/shard_map/ppermute | solution.py:33
  230.6 2.5 collective-permute-done.23
  233.1 1.0 convolution_convert_fusion.8
  234.2 8.1 %collective-permute-done.17 = bf16[144,2176]{1,0:T(8,128)(2,1)S(1)} collective-permute-done((bf16[144,2176]{1,0:T(8,128)(2,1)S(1)}, bf16[144,2176]{1,0:T(8,128)(2,1)S(1)}, u32[]{:S(2)}, u32[]{:S(2)}) %collective-permute-start.17) | collective-permute-done | bytes 626720 | tf_op jit(solution)/shard_map/ppermute | solution.py:33
  242.9 1.2 select_reduce_fusion
  244.0 1.0 convolution_convert_fusion.9
  245.1 1.2 pad_maximum_fusion
  246.3 12.5 %reduce-scatter.2.cloned.1.call-done = bf16[1,3,88,4096]{3,2,1,0:T(8,128)(2,1)} async-done(((bf16[8,3,88,4096]{3,2,1,0:T(8,128)(2,1)}), bf16[1,3,88,4096]{3,2,1,0:T(8,128)(2,1)}) %reduce-scatter.2.cloned.1.call-update) | async-done | bytes 2162704 | tf_op jit(solution)/shard_map/reduce_scatter | solution.py:397
  258.8 4.3 %convert_bitcast_fusion = f32[1,88,3,4096]{3,1,2,0:T(8,128)} fusion(bf16[1,3,88,4096]{3,2,1,0:T(8,128)(2,1)} %reduce-scatter.2.cloned.1.call-done), kind=kLoop, calls=%fused_computation.8 | loop fusion | flops 1081344 | bytes 6488064 | tf_op jit(solution)/shard_map/transpose | solution.py:398
  (70 shorter events, 2.5 us)
Async XLA Ops:
  7.2 3.1 %copy-start = (bf16[192,4096]{1,0:T(8,128)(2,1)S(1)}, bf16[192,4096]{1,0:T(8,128)(2,1)}, u32[]{:S(2)}) copy-start(bf16[192,4096]{1,0:T(8,128)(2,1)} %param.6) | copy-start | bytes 4718596
  7.2 251.6 %reduce-scatter.2.cloned.1.call-start = ((), (), s32[]{:S(2)}) async-start(), calls=%async_computation.1 | async-start | bytes 19464192 | tf_op jit(solution)/shard_map/reduce_scatter | solution.py:397
  11.1 29.4 %collective-permute-start.6 = (bf16[144,4224]{1,0:T(8,128)(2,1)S(1)}, bf16[144,4224]{1,0:T(8,128)(2,1)S(1)}, u32[]{:S(2)}, u32[]{:S(2)}) collective-permute-start(bf16[144,4224]{1,0:T(8,128)(2,1)S(1)} %pad_maximum_fusion.2), channel_id=1, source_target_pairs={{0,1},{1,2},{2,3},{3,0},{4,5},{5,6},{6,7},{7,4},{8,9},{9,10},{10,1... | collective-permute-start | bytes 3649544 | tf_op jit(solution)/shard_map/ppermute | solution.py:33
  13.7 1.6 copy-start.5
  13.9 27.4 %collective-permute-start.7 = (bf16[144,4224]{1,0:T(8,128)(2,1)S(1)}, bf16[144,4224]{1,0:T(8,128)(2,1)S(1)}, u32[]{:S(2)}, u32[]{:S(2)}) collective-permute-start(bf16[144,4224]{1,0:T(8,128)(2,1)S(1)} %pad_maximum_fusion.3), channel_id=1, source_target_pairs={{0,3},{1,0},{2,1},{3,2},{4,7},{5,4},{6,5},{7,6},{8,11},{9,8},{10,9... | collective-permute-start | bytes 3649544 | tf_op jit(solution)/shard_map/ppermute | solution.py:33
  15.8 28.6 %collective-permute-start.1 = (bf16[144,4096]{1,0:T(8,128)(2,1)S(1)}, bf16[144,4096]{1,0:T(8,128)(2,1)S(1)}, u32[]{:S(2)}, u32[]{:S(2)}) collective-permute-start(bf16[144,4096]{1,0:T(8,128)(2,1)S(1)} %convolution_convert_fusion.5), channel_id=1, source_target_pairs={{0,12},{1,13},{2,14},{3,15},{4,0},{5,1},{6,2},{7,3},{8,4},{9,5},{1... | collective-permute-start | bytes 3538952 | tf_op jit(solution)/shard_map/ppermute | solution.py:33
  20.4 27.2 %collective-permute-start = (bf16[144,4096]{1,0:T(8,128)(2,1)S(1)}, bf16[144,4096]{1,0:T(8,128)(2,1)S(1)}, u32[]{:S(2)}, u32[]{:S(2)}) collective-permute-start(bf16[144,4096]{1,0:T(8,128)(2,1)S(1)} %convolution_convert_fusion.6), channel_id=1, source_target_pairs={{0,4},{1,5},{2,6},{3,7},{4,8},{5,9},{6,10},{7,11},{8,12},{9,13},{1... | collective-permute-start | bytes 3538952 | tf_op jit(solution)/shard_map/ppermute | solution.py:33
  41.3 27.9 %collective-permute-start.8 = (bf16[144,4224]{1,0:T(8,128)(2,1)S(1)}, bf16[144,4224]{1,0:T(8,128)(2,1)S(1)}, u32[]{:S(2)}, u32[]{:S(2)}) collective-permute-start(bf16[144,4224]{1,0:T(8,128)(2,1)S(1)} %pad_maximum_fusion.1), channel_id=1, source_target_pairs={{0,2},{1,3},{2,0},{3,1},{4,6},{5,7},{6,4},{7,5},{8,10},{9,11},{10,... | collective-permute-start | bytes 3649544 | tf_op jit(solution)/shard_map/ppermute | solution.py:33
  43.8 59.8 %slice-start = ((s8[17301504]{0:T(1024)(128)(4,1)}), s8[4194304]{0:T(1024)(128)(4,1)S(1)}, s32[]{:S(2)}) async-start(s8[17301504]{0:T(1024)(128)(4,1)} %bitcast.31), calls=%async_computation.2 | async-start | bytes 8388608
  47.6 27.0 %collective-permute-start.2 = (bf16[144,4096]{1,0:T(8,128)(2,1)S(1)}, bf16[144,4096]{1,0:T(8,128)(2,1)S(1)}, u32[]{:S(2)}, u32[]{:S(2)}) collective-permute-start(bf16[144,4096]{1,0:T(8,128)(2,1)S(1)} %convolution_convert_fusion.7), channel_id=1, source_target_pairs={{0,8},{1,9},{2,10},{3,11},{4,12},{5,13},{6,14},{7,15},{8,0},{9,1},... | collective-permute-start | bytes 3538952 | tf_op jit(solution)/shard_map/ppermute | solution.py:33
  48.7 54.9 %slice-start.1 = ((s8[17301504]{0:T(1024)(128)(4,1)}), s8[4194304]{0:T(1024)(128)(4,1)S(1)}, s32[]{:S(2)}) async-start(s8[17301504]{0:T(1024)(128)(4,1)} %bitcast.31), calls=%async_computation.3 | async-start | bytes 8388608
  69.2 34.5 %slice-start.2 = ((s8[17301504]{0:T(1024)(128)(4,1)}), s8[4194304]{0:T(1024)(128)(4,1)S(1)}, s32[]{:S(2)}) async-start(s8[17301504]{0:T(1024)(128)(4,1)} %bitcast.31), calls=%async_computation.4 | async-start | bytes 8388608
  69.5 30.2 %collective-permute-start.10 = (bf16[144,4224]{1,0:T(8,128)(2,1)S(1)}, bf16[144,4224]{1,0:T(8,128)(2,1)S(1)}, u32[]{:S(2)}, u32[]{:S(2)}) collective-permute-start(bf16[144,4224]{1,0:T(8,128)(2,1)S(1)} %get-tuple-element.81), channel_id=1, source_target_pairs={{0,12},{1,13},{2,14},{3,15},{4,0},{5,1},{6,2},{7,3},{8,4},{9,5},{1... | collective-permute-start | bytes 3649544 | tf_op jit(solution)/shard_map/ppermute | solution.py:33
  73.4 30.3 %slice-start.3 = ((s8[17301504]{0:T(1024)(128)(4,1)}), s8[4194304]{0:T(1024)(128)(4,1)S(1)}, s32[]{:S(2)}) async-start(s8[17301504]{0:T(1024)(128)(4,1)} %bitcast.31), calls=%async_computation.5 | async-start | bytes 8388608
  73.4 27.4 %collective-permute-start.9 = (bf16[144,4224]{1,0:T(8,128)(2,1)S(1)}, bf16[144,4224]{1,0:T(8,128)(2,1)S(1)}, u32[]{:S(2)}, u32[]{:S(2)}) collective-permute-start(bf16[144,4224]{1,0:T(8,128)(2,1)S(1)} %get-tuple-element.80), channel_id=1, source_target_pairs={{0,4},{1,5},{2,6},{3,7},{4,8},{5,9},{6,10},{7,11},{8,12},{9,13},{1... | collective-permute-start | bytes 3649544 | tf_op jit(solution)/shard_map/ppermute | solution.py:33
  74.6 29.1 %slice-start.4 = ((s8[17301504]{0:T(1024)(128)(4,1)}), s8[524288]{0:T(1024)(128)(4,1)S(1)}, s32[]{:S(2)}) async-start(s8[17301504]{0:T(1024)(128)(4,1)} %bitcast.31), calls=%async_computation.6 | async-start | bytes 1048576
  75.3 26.6 %collective-permute-start.3 = (bf16[144,4096]{1,0:T(8,128)(2,1)S(1)}, bf16[144,4096]{1,0:T(8,128)(2,1)S(1)}, u32[]{:S(2)}, u32[]{:S(2)}) collective-permute-start(bf16[144,4096]{1,0:T(8,128)(2,1)S(1)} %get-tuple-element.68), channel_id=1, source_target_pairs={{0,1},{1,2},{2,3},{3,0},{4,5},{5,6},{6,7},{7,4},{8,9},{9,10},{10,1... | collective-permute-start | bytes 3538952 | tf_op jit(solution)/shard_map/ppermute | solution.py:33
  76.6 25.3 %collective-permute-start.4 = (bf16[144,4096]{1,0:T(8,128)(2,1)S(1)}, bf16[144,4096]{1,0:T(8,128)(2,1)S(1)}, u32[]{:S(2)}, u32[]{:S(2)}) collective-permute-start(bf16[144,4096]{1,0:T(8,128)(2,1)S(1)} %get-tuple-element.69), channel_id=1, source_target_pairs={{0,3},{1,0},{2,1},{3,2},{4,7},{5,4},{6,5},{7,6},{8,11},{9,8},{10,9... | collective-permute-start | bytes 3538952 | tf_op jit(solution)/shard_map/ppermute | solution.py:33
  100.7 26.3 %collective-permute-start.11 = (bf16[144,4224]{1,0:T(8,128)(2,1)S(1)}, bf16[144,4224]{1,0:T(8,128)(2,1)S(1)}, u32[]{:S(2)}, u32[]{:S(2)}) collective-permute-start(bf16[144,4224]{1,0:T(8,128)(2,1)S(1)} %get-tuple-element.83), channel_id=1, source_target_pairs={{0,8},{1,9},{2,10},{3,11},{4,12},{5,13},{6,14},{7,15},{8,0},{9,1},... | collective-permute-start | bytes 3649544 | tf_op jit(solution)/shard_map/ppermute | solution.py:33
  101.9 16.9 %collective-permute-start.5 = (bf16[144,4096]{1,0:T(8,128)(2,1)S(1)}, bf16[144,4096]{1,0:T(8,128)(2,1)S(1)}, u32[]{:S(2)}, u32[]{:S(2)}) collective-permute-start(bf16[144,4096]{1,0:T(8,128)(2,1)S(1)} %get-tuple-element.71), channel_id=1, source_target_pairs={{0,2},{1,3},{2,0},{3,1},{4,6},{5,7},{6,4},{7,5},{8,10},{9,11},{10,... | collective-permute-start | bytes 3538952 | tf_op jit(solution)/shard_map/ppermute | solution.py:33
  157.2 1.2 copy-start.3
  158.4 1.5 copy-start.4
  159.9 5.9 %copy-start.2 = (bf16[1,704,3,4096]{3,1,2,0:T(8,128)(2,1)S(1)}, bf16[1,704,3,4096]{3,1,2,0:T(8,128)(2,1)}, u32[]{:S(2)}) copy-start(bf16[1,704,3,4096]{3,1,2,0:T(8,128)(2,1)} %param.9) | copy-start | bytes 51904516
  172.2 15.3 %collective-permute-start.19 = (bf16[144,2048]{1,0:T(8,128)(2,1)S(1)}, bf16[144,2048]{1,0:T(8,128)(2,1)S(1)}, u32[]{:S(2)}, u32[]{:S(2)}) collective-permute-start(bf16[144,2048]{1,0:T(8,128)(2,1)S(1)} %get-tuple-element.106), channel_id=1, source_target_pairs={{0,12},{1,13},{2,14},{3,15},{4,0},{5,1},{6,2},{7,3},{8,4},{9,5},{1... | collective-permute-start | bytes 1769480 | tf_op jit(solution)/shard_map/ppermute | solution.py:33
  176.0 12.9 %collective-permute-start.20 = (bf16[144,2048]{1,0:T(8,128)(2,1)S(1)}, bf16[144,2048]{1,0:T(8,128)(2,1)S(1)}, u32[]{:S(2)}, u32[]{:S(2)}) collective-permute-start(bf16[144,2048]{1,0:T(8,128)(2,1)S(1)} %get-tuple-element.107), channel_id=1, source_target_pairs={{0,4},{1,5},{2,6},{3,7},{4,8},{5,9},{6,10},{7,11},{8,12},{9,13},{1... | collective-permute-start | bytes 1769480 | tf_op jit(solution)/shard_map/ppermute | solution.py:33
  176.0 24.0 %collective-permute-start.18 = (bf16[144,2048]{1,0:T(8,128)(2,1)S(1)}, bf16[144,2048]{1,0:T(8,128)(2,1)S(1)}, u32[]{:S(2)}, u32[]{:S(2)}) collective-permute-start(bf16[144,2048]{1,0:T(8,128)(2,1)S(1)} %get-tuple-element.104), channel_id=1, source_target_pairs={{0,8},{1,9},{2,10},{3,11},{4,12},{5,13},{6,14},{7,15},{8,0},{9,1},... | collective-permute-start | bytes 1769480 | tf_op jit(solution)/shard_map/ppermute | solution.py:33
  183.7 18.1 %collective-permute-start.13 = (bf16[144,2176]{1,0:T(8,128)(2,1)S(1)}, bf16[144,2176]{1,0:T(8,128)(2,1)S(1)}, u32[]{:S(2)}, u32[]{:S(2)}) collective-permute-start(bf16[144,2176]{1,0:T(8,128)(2,1)S(1)} %get-tuple-element.94), channel_id=1, source_target_pairs={{0,3},{1,0},{2,1},{3,2},{4,7},{5,4},{6,5},{7,6},{8,11},{9,8},{10,9... | collective-permute-start | bytes 1880072 | tf_op jit(solution)/shard_map/ppermute | solution.py:33
  183.8 18.7 %collective-permute-start.14 = (bf16[144,2176]{1,0:T(8,128)(2,1)S(1)}, bf16[144,2176]{1,0:T(8,128)(2,1)S(1)}, u32[]{:S(2)}, u32[]{:S(2)}) collective-permute-start(bf16[144,2176]{1,0:T(8,128)(2,1)S(1)} %get-tuple-element.95), channel_id=1, source_target_pairs={{0,1},{1,2},{2,3},{3,0},{4,5},{5,6},{6,7},{7,4},{8,9},{9,10},{10,1... | collective-permute-start | bytes 1880072 | tf_op jit(solution)/shard_map/ppermute | solution.py:33
  187.5 20.3 %collective-permute-start.12 = (bf16[144,2176]{1,0:T(8,128)(2,1)S(1)}, bf16[144,2176]{1,0:T(8,128)(2,1)S(1)}, u32[]{:S(2)}, u32[]{:S(2)}) collective-permute-start(bf16[144,2176]{1,0:T(8,128)(2,1)S(1)} %get-tuple-element.92), channel_id=1, source_target_pairs={{0,2},{1,3},{2,0},{3,1},{4,6},{5,7},{6,4},{7,5},{8,10},{9,11},{10,... | collective-permute-start | bytes 1880072 | tf_op jit(solution)/shard_map/ppermute | solution.py:33
  200.2 26.2 %collective-permute-start.21 = (bf16[144,2048]{1,0:T(8,128)(2,1)S(1)}, bf16[144,2048]{1,0:T(8,128)(2,1)S(1)}, u32[]{:S(2)}, u32[]{:S(2)}) collective-permute-start(bf16[144,2048]{1,0:T(8,128)(2,1)S(1)} %get-tuple-element.113), channel_id=1, source_target_pairs={{0,3},{1,0},{2,1},{3,2},{4,7},{5,4},{6,5},{7,6},{8,11},{9,8},{10,9... | collective-permute-start | bytes 1769480 | tf_op jit(solution)/shard_map/ppermute | solution.py:33
  200.3 30.3 %collective-permute-start.22 = (bf16[144,2048]{1,0:T(8,128)(2,1)S(1)}, bf16[144,2048]{1,0:T(8,128)(2,1)S(1)}, u32[]{:S(2)}, u32[]{:S(2)}) collective-permute-start(bf16[144,2048]{1,0:T(8,128)(2,1)S(1)} %get-tuple-element.114), channel_id=1, source_target_pairs={{0,1},{1,2},{2,3},{3,0},{4,5},{5,6},{6,7},{7,4},{8,9},{9,10},{10,1... | collective-permute-start | bytes 1769480 | tf_op jit(solution)/shard_map/ppermute | solution.py:33
  201.8 31.3 %collective-permute-start.23 = (bf16[144,2048]{1,0:T(8,128)(2,1)S(1)}, bf16[144,2048]{1,0:T(8,128)(2,1)S(1)}, u32[]{:S(2)}, u32[]{:S(2)}) collective-permute-start(bf16[144,2048]{1,0:T(8,128)(2,1)S(1)} %get-tuple-element.115), channel_id=1, source_target_pairs={{0,2},{1,3},{2,0},{3,1},{4,6},{5,7},{6,4},{7,5},{8,10},{9,11},{10,... | collective-permute-start | bytes 1769480 | tf_op jit(solution)/shard_map/ppermute | solution.py:33
  208.0 26.1 %collective-permute-start.15 = (bf16[144,2176]{1,0:T(8,128)(2,1)S(1)}, bf16[144,2176]{1,0:T(8,128)(2,1)S(1)}, u32[]{:S(2)}, u32[]{:S(2)}) collective-permute-start(bf16[144,2176]{1,0:T(8,128)(2,1)S(1)} %get-tuple-element.101), channel_id=1, source_target_pairs={{0,12},{1,13},{2,14},{3,15},{4,0},{5,1},{6,2},{7,3},{8,4},{9,5},{1... | collective-permute-start | bytes 1880072 | tf_op jit(solution)/shard_map/ppermute | solution.py:33
  209.8 24.4 %collective-permute-start.16 = (bf16[144,2176]{1,0:T(8,128)(2,1)S(1)}, bf16[144,2176]{1,0:T(8,128)(2,1)S(1)}, u32[]{:S(2)}, u32[]{:S(2)}) collective-permute-start(bf16[144,2176]{1,0:T(8,128)(2,1)S(1)} %get-tuple-element.102), channel_id=1, source_target_pairs={{0,4},{1,5},{2,6},{3,7},{4,8},{5,9},{6,10},{7,11},{8,12},{9,13},{1... | collective-permute-start | bytes 1880072 | tf_op jit(solution)/shard_map/ppermute | solution.py:33
  226.5 15.9 %collective-permute-start.17 = (bf16[144,2176]{1,0:T(8,128)(2,1)S(1)}, bf16[144,2176]{1,0:T(8,128)(2,1)S(1)}, u32[]{:S(2)}, u32[]{:S(2)}) collective-permute-start(bf16[144,2176]{1,0:T(8,128)(2,1)S(1)} %get-tuple-element.103), channel_id=1, source_target_pairs={{0,8},{1,9},{2,10},{3,11},{4,12},{5,13},{6,14},{7,15},{8,0},{9,1},... | collective-permute-start | bytes 1880072 | tf_op jit(solution)/shard_map/ppermute | solution.py:33
  258.8 4.3 %copy-start.1 = (bf16[192,4096]{1,0:T(8,128)(2,1)S(1)}, bf16[192,4096]{1,0:T(8,128)(2,1)}, u32[]{:S(2)}) copy-start(bf16[192,4096]{1,0:T(8,128)(2,1)} %param.6) | copy-start | bytes 4718596
Sparse Core Ops, SparseCore 0:
  158.6 100.1 reduce-scatter.1
